TPU v7x, 32 devices: a whole 2x2x4 slice. The times are simulated.
32 devices in a mesh: grp: 2 (over y), chan: 4 (over z), stn: 2 (over x), pol: 2 (over core).
Axes of the slice: x: 2, y: 2, z: 4, core: 2. Of those that a mesh axis runs over, the one named last changes fastest.
Arguments:
- voltages: bfloat16 [4, 256, 16384], P(('grp', 'pol'), 'stn', 'chan'), parts along dimension 0, may hold values from -6 to 6
- fir_coeffs: float32 [16, 4096], replicated, may hold values from -1.5 to 1.5
- flags: int32 [4, 256], P(('grp', 'pol'), 'stn'), parts along dimension 0, may hold values 0 or 1
- station_slot: int32 [256], replicated, may hold values from 0 to 255, each once
- chan_map: int32 [2048], replicated, may hold values from 0 to 2047, each once
Outputs:
- visibilities: float32 [4, 256, 2, 256, 2, 256], P('grp', ('chan', 'stn'), 'pol'), parts along dimension 0
There are 2 independent parts, one for each index of `grp`. A program takes and returns all parts, laid end to end along the dimension named above; an argument that names none is the same for every part. Nothing has to cross between parts.
Inputs may be any that keep to these rules, and one draw needn't show every extreme that they name: A permutation: station a's voltages are in row station_slot[a]. `chan_map`: a permutation of the 2048 channels.
All inputs are finite; a program needn't handle non-finite values. No bound on the sum of `flags` on one device may be relied on, other than what follows from the above.
Results may differ from a plain program's by a relative error of at most 0.0033.
Values may be sent and summed in bfloat16 or wider, within the bound.
No kernel may reach another device: no remote copies, remote signals or barrier semaphores. Data moves between devices by JAX's collectives and lax.ppermute only.
A program may use at most 128 MiB of HBM per device.

v0:
```python
import math

import jax
import jax.numpy as jnp
from jax import lax
from jax.sharding import PartitionSpec as P

TAPS = 16
FA = 64
FB = 64
FL = 4096
CH = 2048
COARSE = 8


highest_precision = lax.Precision.HIGHEST


def from_behind(block, axis, distance):
    devices = range(lax.axis_size(axis))
    route = [(i - distance, i) for i in devices if i - distance in devices]
    return lax.ppermute(block, axis, route)


def angle_table(rows, cols, period):
    row_index = lax.broadcasted_iota(jnp.int32, (rows, cols), 0)
    col_index = lax.broadcasted_iota(jnp.int32, (rows, cols), 1)
    phase = (row_index * col_index % period).astype(jnp.float32) * (2.0 * math.pi / period)
    return (jnp.cos(phase), jnp.sin(phase))


def transform(filtered):
    stations_here, frames_here, frame_len = filtered.shape
    grid = filtered.reshape(stations_here, frames_here, FB, FA)
    cos_one, sin_one = angle_table(FB, FB, FB)
    part_re = jnp.einsum("sfqp,qc->sfpc", grid, cos_one, precision=highest_precision)
    part_im = -jnp.einsum("sfqp,qc->sfpc", grid, sin_one, precision=highest_precision)
    cos_two, sin_two = angle_table(FA, FB, FL)
    turn_re = part_re * cos_two + part_im * sin_two
    turn_im = part_im * cos_two - part_re * sin_two
    cos_three, sin_three = angle_table(FA, FA // 2, FA)
    form = "sfpc,pk->kcfs"
    out_re = jnp.einsum(form, turn_re, cos_three, precision=highest_precision) + jnp.einsum(
        form, turn_im, sin_three, precision=highest_precision
    )
    out_im = jnp.einsum(form, turn_im, cos_three, precision=highest_precision) - jnp.einsum(
        form, turn_re, sin_three, precision=highest_precision
    )
    return (
        out_re.reshape(CH, frames_here * stations_here),
        out_im.reshape(CH, frames_here * stations_here),
    )


def filterbank(window, frames_here, fir_coeffs):
    rows_here = window.shape[0]
    filtered = jnp.zeros((rows_here, frames_here, FL), jnp.float32)
    for tap_index in range(TAPS):
        filtered = filtered + fir_coeffs[tap_index][None, None, :] * window[
            :, tap_index : tap_index + frames_here, :
        ].astype(jnp.float32)
    return transform(filtered)


def body(voltages, fir_coeffs, flags, station_slot, chan_map):
    stations_here = voltages.shape[1]
    chan_count = lax.axis_size("chan")
    stn_count = lax.axis_size("stn")
    frames_here = voltages.shape[2] // FL
    frames = voltages.reshape(stations_here, frames_here, FL)
    rounds = (TAPS - 1 + frames_here - 1) // frames_here
    history = []
    for distance in range(1, rounds + 1):
        moved = from_behind(frames, "chan", distance)
        history = [moved] + history
    window = jnp.concatenate(history + [frames], axis=1)
    flag_rows = flags[0]
    out_re, out_im = filterbank(window, frames_here, fir_coeffs)
    weight = jnp.tile(flag_rows.astype(jnp.float32), frames_here) * FL ** (-0.5)
    spectra = jnp.stack(
        [(out_re * weight).astype(jnp.bfloat16), (out_im * weight).astype(jnp.bfloat16)], axis=1
    )
    spectra = jnp.take(spectra, chan_map, axis=0)
    pieces = lax.all_to_all(spectra, ("chan", "stn"), split_axis=0, concat_axis=2, tiled=True)
    pieces = pieces.reshape(-1, 2, chan_count, stn_count, frames_here, stations_here)
    turned = pieces.transpose(0, 1, 3, 5, 2, 4)
    channels_here = turned.shape[0]
    all_stations = turned.shape[2] * turned.shape[3]
    total_frames = turned.shape[4] * turned.shape[5]
    turned = turned.reshape(channels_here // COARSE, COARSE, 2, all_stations, total_frames)
    turned = jnp.take(turned, station_slot, axis=3)
    own_re = turned[:, :, 0]
    own_im = turned[:, :, 1]
    piece = lax.all_gather(turned[None], "pol", axis=0, tiled=True)
    other_re = piece[:, :, :, 0]
    other_im = piece[:, :, :, 1]
    form = "jkrf,qjksf->jrqs"
    real_part = jnp.einsum(form, own_re, other_re, preferred_element_type=jnp.float32) + jnp.einsum(
        form, own_im, other_im, preferred_element_type=jnp.float32
    )
    imag_part = jnp.einsum(form, own_im, other_re, preferred_element_type=jnp.float32) - jnp.einsum(
        form, own_re, other_im, preferred_element_type=jnp.float32
    )
    block = jnp.stack([real_part, imag_part], axis=0)
    gram = block
    gram = gram * (1.0 / (total_frames * COARSE))
    return gram[:, :, None]


def solution(mesh):
    in_specs = (P(("grp", "pol"), "stn", "chan"), P(), P(("grp", "pol"), "stn"), P(), P())
    out_specs = P("grp", ("chan", "stn"), "pol", None, None, None)
    return jax.shard_map(body, mesh=mesh, in_specs=in_specs, out_specs=out_specs, check_vma=False)
```

profile of v0, /device:TPU:9, one launch (start us, length us, event | category | flops | bytes accessed | tf_op | source)
XLA Modules:
  0.0 347.6 jit_solution(15083775156415018377)
XLA Ops:
  6.5 0.0 copy-start.2
  6.5 0.0 copy-start.4
  6.5 0.0 copy-start.1
  6.5 1.7 copy.47
  8.2 3.2 collective-permute-start.3
  11.4 2.4 collective-permute-start.2
  13.8 1.6 collective-permute-start.1
  15.4 1.6 collective-permute-start
  17.1 0.0 copy-done.2
  17.1 0.1 fusion.56
  17.2 0.1 fusion.55
  17.4 0.1 copy.49
  17.5 0.1 copy.51
  17.5 0.0 copy-done.4
  17.6 0.0 copy-done.1
  17.6 0.2 fusion.93
  17.8 16.4 %collective-permute-done.3 = bf16[128,1,4096]{0,2,1:T(8,128)(2,1)S(1)} collective-permute-done((bf16[128,1,4096]{0,2,1:T(8,128)(2,1)S(1)}, bf16[128,1,4096]{0,2,1:T(8,128)(2,1)S(1)}, u32[]{:S(2)}, u32[]{:S(2)}) %collective-permute-start.3) | collective-permute-done | bytes 1048608 | tf_op jit(solution)/shard_map/ppermute | solution.py:22
  34.1 66.5 %collective-permute-done.2 = bf16[128,1,4096]{0,2,1:T(8,128)(2,1)S(1)} collective-permute-done((bf16[128,1,4096]{0,2,1:T(8,128)(2,1)S(1)}, bf16[128,1,4096]{0,2,1:T(8,128)(2,1)S(1)}, u32[]{:S(2)}, u32[]{:S(2)}) %collective-permute-start.2) | collective-permute-done | bytes 1048608 | tf_op jit(solution)/shard_map/ppermute | solution.py:22
  100.6 0.0 collective-permute-done.1
  100.6 0.0 collective-permute-done
  100.6 6.2 %fusion.4 = f32[128,1,4096]{0,2,1:T(8,128)S(1)} fusion(bf16[128,1,4096]{0,2,1:T(8,128)(2,1)S(1)} %collective-permute-done.3, bf16[128,1,4096]{0,2,1:T(8,128)(2,1)S(1)} %collective-permute-done.2, bf16[128,1,4096]{0,2,1:T(8,128)(2,1)} %collective-permute-done.1, bf16[128,1,4096]{0,2,1:T(8,128)(2,1)} %collective-permute-done, f32[4096]{0:T(1024)S(1)} %bitcast.108, ...), kind=kLoop, calls=%fused_computation.10 | loop fusion | flops 7340032 | bytes 7421952 | tf_op jit(solution)/shard_map/add | solution.py:59
  106.9 3.3 fusion.13
  110.2 4.5 %multiply_add_fusion.1 = (f32[128,64,64]{0,2,1:T(8,128)S(1)}, f32[128,64,64]{0,2,1:T(8,128)S(1)}) fusion(f32[128,64,64]{0,2,1:T(8,128)S(1)} %fusion.13, f32[64,64]{1,0:T(8,128)S(1)} %copy.51, f32[64,64]{1,0:T(8,128)S(1)} %copy.49, f32[128,64,64]{0,2,1:T(8,128)S(1)} %bitcast.100), kind=kOutput, calls=%fused_computation.12 | convolution fusion | flops 406380544 | bytes 8421376 | tf_op jit(solution)/shard_map/sfqp,qc->sfpc/dot_general | solution.py:36
  114.7 2.4 fusion.5
  117.0 2.6 fusion.7
  119.7 2.4 fusion.20
  122.1 2.4 fusion.26
  124.6 0.6 copy.57
  125.2 0.6 copy.54
  125.8 0.2 fusion.30
  126.0 0.1 pad_maximum_fusion
  126.1 8.7 %copy.58 = bf16[2048,2,128]{2,1,0:T(2,128)(2,1)S(1)} copy(bf16[2048,2,128]{2,0,1:T(8,128)(2,1)S(1)} %pad_maximum_fusion) | data formatting | bytes 2097152 | tf_op jit(solution)/shard_map/stack | solution.py:80
  134.8 7.1 %gather_fusion = bf16[2048,2,128]{2,1,0:T(2,128)(2,1)S(1)} fusion(bf16[2048,2,128]{2,1,0:T(2,128)(2,1)S(1)} %copy.58, s32[2048]{0:T(1024)S(1)} %fusion.68), kind=kCustom, calls=%fused_computation | custom fusion | bytes 2105344 | tf_op jit(solution)/shard_map/jit(_take)/gather | solution.py:83
  141.9 0.0 copy-start.3
  141.9 19.9 %broadcast_select_fusion = bf16[2048,2,128]{2,1,0:T(2,128)(2,1)} fusion(bf16[2048,2,128]{2,1,0:T(2,128)(2,1)S(1)} %gather_fusion, pred[2048]{0:T(1024)(128)(4,1)S(1)} %compare_and_fusion), kind=kLoop, calls=%fused_computation.13 | loop fusion | flops 524288 | bytes 2099200 | tf_op jit(solution)/shard_map/jit(_take)/select_n | solution.py:83
  161.7 6.5 %all-to-all-start = ((bf16[2048,2,128]{2,1,0:T(2,128)(2,1)}), bf16[2048,2,128]{2,1,0:T(2,128)(2,1)S(1)}, u32[]{:S(2)}, u32[]{:S(2)}) async-start(bf16[2048,2,128]{2,1,0:T(2,128)(2,1)} %broadcast_select_fusion), calls=%async_computation | async-start | bytes 2097152 | tf_op jit(solution)/shard_map/all_to_all | solution.py:84
  168.2 0.0 all-gather.2.cloned.1.call-start
  168.2 0.0 copy-done.3
  168.3 22.1 %all-to-all-done = bf16[2048,2,128]{2,1,0:T(2,128)(2,1)S(1)} async-done(((bf16[2048,2,128]{2,1,0:T(2,128)(2,1)}), bf16[2048,2,128]{2,1,0:T(2,128)(2,1)S(1)}, u32[]{:S(2)}, u32[]{:S(2)}) %all-to-all-start) | async-done | bytes 1048608 | tf_op jit(solution)/shard_map/all_to_all | solution.py:84
  190.3 0.2 copy.59
  190.5 1.1 copy.60
  191.6 0.7 reshape.291
  192.4 7.2 %copy.61 = bf16[32,8,2,256,4]{0,1,4,3,2:T(8,128)(2,1)} copy(bf16[32,8,2,256,4]{3,1,0,4,2:T(8,128)(2,1)S(1)} %reshape.291) | data formatting | bytes 2097152 | tf_op jit(solution)/shard_map/reshape | solution.py:90
  199.5 5.2 %gather_fusion.1 = bf16[256,32,8,2,4]{1,2,4,3,0:T(8,128)(2,1)} fusion(bf16[32,8,2,256,4]{0,1,4,3,2:T(8,128)(2,1)} %copy.61, s32[1024]{0:T(1024)S(1)} %pad_clamp_fusion), kind=kCustom, calls=%fused_computation.1 | custom fusion | bytes 2098176 | tf_op jit(solution)/shard_map/jit(_take)/gather | solution.py:91
  204.8 6.1 %copy.62 = bf16[256,32,8,2,4]{0,2,4,1,3:T(8,128)(2,1)S(1)} copy(bf16[256,32,8,2,4]{1,2,4,3,0:T(8,128)(2,1)} %gather_fusion.1) | data formatting | bytes 2097152 | tf_op jit(solution)/shard_map/jit(_take)/gather | solution.py:91
  210.9 1.1 bitcast_select_fusion
  212.0 0.0 all-gather.2.cloned.1.call-update
  212.0 0.1 bitcast_select_fusion.1
  212.1 14.1 %all-gather.2.cloned.1.call-done = bf16[2,32,8,2,256,4]{4,2,5,0,1,3:T(8,128)(2,1)} async-done(((bf16[1,32,8,2,256,4]{4,2,5,0,1,3:T(8,128)(2,1)}), bf16[2,32,8,2,256,4]{4,2,5,0,1,3:T(8,128)(2,1)}) %all-gather.2.cloned.1.call-update) | async-done | bytes 2097168 | tf_op jit(solution)/shard_map/all_gather | solution.py:94
  226.2 0.0 copy-start
  226.2 9.9 %fusion.31 = f32[32,256,2,256,1]{3,1,4,2,0:T(8,128)} fusion(bf16[2,32,8,2,256,4]{4,2,5,0,1,3:T(8,128)(2,1)} %all-gather.2.cloned.1.call-done, bf16[32,8,2,256,4]{3,1,4,0,2:T(8,128)(2,1)S(1)} %bitcast_select_fusion.1), kind=kOutput, calls=%fused_computation.39 | convolution fusion | flops 268435456 | bytes 18350080 | tf_op jit(solution)/shard_map/jkrf,qjksf->jrqs/dot_general | solution.py:101
  236.1 0.0 copy-done
  236.1 8.1 %fusion.32 = f32[32,256,2,256,1]{3,1,4,2,0:T(8,128)} fusion(bf16[2,32,8,2,256,4]{4,2,5,0,1,3:T(8,128)(2,1)S(1)} %copy-done, bf16[32,8,2,256,4]{3,1,4,0,2:T(8,128)(2,1)S(1)} %bitcast_select_fusion.1), kind=kOutput, calls=%fused_computation.40 | convolution fusion | flops 268435456 | bytes 18350080 | tf_op jit(solution)/shard_map/jkrf,qjksf->jrqs/dot_general | solution.py:98
  244.2 8.5 %fusion = f32[1,32,1,256,2,256]{5,3,4,1,2,0:T(8,128)S(1)} fusion(f32[32,256,2,256,1]{3,1,4,2,0:T(8,128)} %fusion.31, bf16[2,32,8,2,256,4]{4,2,5,0,1,3:T(8,128)(2,1)} %all-gather.2.cloned.1.call-done, bf16[32,8,2,256,4]{3,1,4,0,2:T(8,128)(2,1)S(1)} %bitcast_select_fusion.1), kind=kOutput, calls=%fused_computation.4 | convolution fusion | flops 272629760 | bytes 35127296 | tf_op jit(solution)/shard_map/jkrf,qjksf->jrqs/dot_general | solution.py:101
  252.7 14.7 %fusion.1 = f32[1,32,1,256,2,256]{5,3,4,1,2,0:T(8,128)} fusion(f32[32,256,2,256,1]{3,1,4,2,0:T(8,128)} %fusion.32, bf16[2,32,8,2,256,4]{4,2,5,0,1,3:T(8,128)(2,1)} %all-gather.2.cloned.1.call-done, bf16[32,8,2,256,4]{3,1,4,0,2:T(8,128)(2,1)S(1)} %bitcast_select_fusion.1), kind=kOutput, calls=%fused_computation.6 | convolution fusion | flops 272629760 | bytes 35127296 | tf_op jit(solution)/shard_map/jkrf,qjksf->jrqs/dot_general | solution.py:98
  267.4 18.3 %maximum_multiply_fusion = f32[2,32,1,256,2,256]{5,3,4,1,2,0:T(8,128)} fusion(f32[1,32,1,256,2,256]{5,3,4,1,2,0:T(8,128)S(1)} %fusion, f32[1,32,1,256,2,256]{5,3,4,1,2,0:T(8,128)} %fusion.1), kind=kLoop, calls=%fused_computation.2 | loop fusion | flops 16777216 | bytes 67108864 | tf_op jit(solution)/shard_map/mul | solution.py:106
  285.7 54.9 %copy.63 = f32[2,32,1,256,2,256]{5,4,3,2,1,0:T(2,128)} copy(f32[2,32,1,256,2,256]{5,3,4,1,2,0:T(8,128)} %maximum_multiply_fusion) | data formatting | bytes 67108864 | tf_op jit(solution)/shard_map/mul | solution.py:106
  (6 shorter events, 0.0 us)
Async XLA Ops:
  6.5 10.5 %copy-start.2 = (s32[2048]{0:T(1024)S(1)}, s32[2048]{0:T(1024)}, u32[]{:S(2)}) copy-start(s32[2048]{0:T(1024)} %param.9) | copy-start | bytes 24580
  6.5 11.0 %copy-start.4 = (s32[1,128]{1,0:T(1,128)S(1)}, s32[1,128]{1,0:T(1,128)}, u32[]{:S(2)}) copy-start(s32[1,128]{1,0:T(1,128)} %param.7) | copy-start | bytes 1540
  6.5 11.0 %copy-start.1 = (f32[16,4096]{1,0:T(8,128)S(1)}, f32[16,4096]{1,0:T(8,128)}, u32[]{:S(2)}) copy-start(f32[16,4096]{1,0:T(8,128)} %param.6) | copy-start | bytes 786436
  8.2 25.9 %collective-permute-start.3 = (bf16[128,1,4096]{0,2,1:T(8,128)(2,1)S(1)}, bf16[128,1,4096]{0,2,1:T(8,128)(2,1)S(1)}, u32[]{:S(2)}, u32[]{:S(2)}) collective-permute-start(bf16[128,1,4096]{0,2,1:T(8,128)(2,1)S(1)} %bitcast.101), channel_id=1, source_target_pairs={{0,4},{4,8},{8,12},{1,5},{5,9},{9,13},{2,6},{6,10},{10,14},{3,7},{... | collective-permute-start | bytes 3145736 | tf_op jit(solution)/shard_map/ppermute | solution.py:22
  11.4 89.2 %collective-permute-start.2 = (bf16[128,1,4096]{0,2,1:T(8,128)(2,1)S(1)}, bf16[128,1,4096]{0,2,1:T(8,128)(2,1)S(1)}, u32[]{:S(2)}, u32[]{:S(2)}) collective-permute-start(bf16[128,1,4096]{0,2,1:T(8,128)(2,1)S(1)} %bitcast.102), channel_id=1, source_target_pairs={{0,8},{4,12},{1,9},{5,13},{2,10},{6,14},{3,11},{7,15},{16,24},{20,... | collective-permute-start | bytes 3145736 | tf_op jit(solution)/shard_map/ppermute | solution.py:22
  13.8 86.8 %collective-permute-start.1 = (bf16[128,1,4096]{0,2,1:T(8,128)(2,1)S(1)}, bf16[128,1,4096]{0,2,1:T(8,128)(2,1)}, u32[]{:S(2)}, u32[]{:S(2)}) collective-permute-start(bf16[128,1,4096]{0,2,1:T(8,128)(2,1)S(1)} %bitcast.103), channel_id=1, source_target_pairs={{0,12},{1,13},{2,14},{3,15},{16,28},{17,29},{18,30},{19,31}} | collective-permute-start | bytes 3145736 | tf_op jit(solution)/shard_map/ppermute | solution.py:22
  15.4 85.2 %collective-permute-start = (bf16[128,1,4096]{0,2,1:T(8,128)(2,1)S(1)}, bf16[128,1,4096]{0,2,1:T(8,128)(2,1)}, u32[]{:S(2)}, u32[]{:S(2)}) collective-permute-start(bf16[128,1,4096]{0,2,1:T(8,128)(2,1)S(1)} %bitcast.104), channel_id=1, source_target_pairs={} | collective-permute-start | bytes 3145736 | tf_op jit(solution)/shard_map/ppermute | solution.py:22
  141.9 26.4 %copy-start.3 = (s32[256]{0:T(256)S(1)}, s32[256]{0:T(256)}, u32[]{:S(2)}) copy-start(s32[256]{0:T(256)} %param.8) | copy-start | bytes 3076
  161.7 28.6 %all-to-all-start = ((bf16[2048,2,128]{2,1,0:T(2,128)(2,1)}), bf16[2048,2,128]{2,1,0:T(2,128)(2,1)S(1)}, u32[]{:S(2)}, u32[]{:S(2)}) async-start(bf16[2048,2,128]{2,1,0:T(2,128)(2,1)} %broadcast_select_fusion), calls=%async_computation | async-start | bytes 2097152 | tf_op jit(solution)/shard_map/all_to_all | solution.py:84
  168.2 58.0 %all-gather.2.cloned.1.call-start = ((), (), s32[]{:S(2)}) async-start(), calls=%async_computation.1 | async-start | bytes 3145728 | tf_op jit(solution)/shard_map/all_gather | solution.py:94
  226.2 9.9 %copy-start = (bf16[2,32,8,2,256,4]{4,2,5,0,1,3:T(8,128)(2,1)S(1)}, bf16[2,32,8,2,256,4]{4,2,5,0,1,3:T(8,128)(2,1)}, u32[]{:S(2)}) copy-start(bf16[2,32,8,2,256,4]{4,2,5,0,1,3:T(8,128)(2,1)} %all-gather.2.cloned.1.call-done) | copy-start | bytes 6291460
Sparse Core Ops, SparseCore 0:
  212.1 13.9 all-gather.1
where the time goes:
time: 353 us; the launch traced here: 348 us
  waiting for transfers between devices  119 us (34%)
  local copies, waits for them, and re-layouts  94.2 us (27%)
  matrix products  58.8 us (17%)
  other arithmetic  46.3 us (13%)
  starting transfers between devices  15.3 us (4%)
  between operations  13.8 us (4%)
    ppermute x4, waiting for transfers between devices, from_behind(): return lax.ppermute(block, axis, route)  82.9 us
    mul x1, local copies, waits for them, and re-layouts, body(): gram = gram * (1.0 / (total_frames * COARSE))  54.9 us
    all_to_all x1, waiting for transfers between devices, body(): lax.all_to_all(spectra, ('chan', 'stn'), split_axis=0, concat_axis=2, til...  22.1 us
    select_n x1, other arithmetic, body(): spectra = jnp.take(spectra, chan_map, axis=0)  19.9 us
    mul x1, other arithmetic, body(): gram = gram * (1.0 / (total_frames * COARSE))  18.3 us
    dot_general x1, matrix products, body(): jnp.einsum(form, own_im, other_im, preferred_element_type=jnp.float32)  14.7 us
    all_gather x1, waiting for transfers between devices, body(): piece = lax.all_gather(turned[None], 'pol', axis=0, tiled=True)  14.1 us
    gather x2, local copies, waits for them, and re-layouts, body(): turned = jnp.take(turned, station_slot, axis=3)  11.4 us
  transfers between devices with their start and end apart: 6, of which 4 were waited for; matrix products, arithmetic and copies ran while one was open for 0% of the time, Pallas kernels for 0%

commit v1 on v0

v1 whole, which is shorter than its diff:
```python
import functools
import math

import jax
import jax.numpy as jnp
import numpy as np
from jax import lax
from jax.experimental import pallas as pl
from jax.experimental.pallas import tpu as pltpu
from jax.sharding import PartitionSpec as P

TAPS = 16
FL = 4096
CH = 2048
COARSE = 8
RAD = 16
PT = FL // RAD
HALF = PT // 2
LANES = 128

f32 = jnp.float32
bf16 = jnp.bfloat16


def onehot(rows, cols):
    return (rows[:, None] == cols[None, :]).astype(bf16)


@functools.cache
def tables():
    p = np.arange(PT)[:, None]
    wide = []
    for c in range(1, RAD // 2):
        k2 = np.concatenate([np.arange(HALF), PT - 1 - np.arange(HALF)])[None, :]
        phase = (p * (c + RAD * k2) % FL) * (2.0 * math.pi / FL)
        wide.append(np.concatenate([np.cos(phase), -np.sin(phase)], axis=1))
    slim = []
    for c in (0, RAD // 2):
        k2 = np.arange(HALF)[None, :]
        phase = (p * (c + RAD * k2) % FL) * (2.0 * math.pi / FL)
        slim.append(np.concatenate([np.cos(phase), -np.sin(phase)], axis=1))
    out = []
    for table in (np.stack(wide), np.stack(slim)):
        table = table * FL**-0.5
        high = table.astype(np.float32).astype(jnp.bfloat16)
        low = (table - high.astype(np.float64)).astype(np.float32).astype(jnp.bfloat16)
        out += [high, low]
    return out


def real_dft16(x):
    def dft4(a0, a1, a2, a3):
        s02, d02, s13, d13 = a0 + a2, a0 - a2, a1 + a3, a1 - a3
        return s02 + s13, d02, -d13, s02 - s13

    cols = [dft4(x[b], x[4 + b], x[8 + b], x[12 + b]) for b in range(4)]
    out = [None] * 9
    r0, r1, i1, r2 = dft4(*(cols[b][0] for b in range(4)))
    out[0], out[4], out[8] = (r0, None), (r1, i1), (r2, None)
    h = math.sqrt(0.5)
    v0, v1, v2, v3 = (cols[b][3] for b in range(4))
    pr, pi = h * (v1 - v3), -h * (v1 + v3)
    out[2] = (v0 + pr, pi - v2)
    out[6] = (v0 - pr, v2 + pi)
    c1, s1 = math.cos(math.pi / 8), math.sin(math.pi / 8)
    re0, im0 = cols[0][1], cols[0][2]
    re1 = cols[1][1] * c1 + cols[1][2] * s1
    im1 = cols[1][2] * c1 - cols[1][1] * s1
    re2 = (cols[2][1] + cols[2][2]) * h
    im2 = (cols[2][2] - cols[2][1]) * h
    re3 = cols[3][1] * s1 + cols[3][2] * c1
    im3 = cols[3][2] * s1 - cols[3][1] * c1
    ar, ai, br, bi = re0 + re2, im0 + im2, re0 - re2, im0 - im2
    cr, ci, dr, di = re1 + re3, im1 + im3, re1 - re3, im1 - im3
    out[1] = (ar + cr, ai + ci)
    out[5] = (br + di, bi - dr)
    out[7] = (ar - cr, ci - ai)
    out[3] = (br - di, -bi - dr)
    return out


def split(value):
    high = value.astype(bf16)
    return high, (value - high.astype(f32)).astype(bf16)


def filterbank_kernel(frames, where_ref, *refs):
    blocks = refs[:frames]
    fir, flag, wide_hi, wide_lo, slim_hi, slim_lo, select = refs[frames : frames + 7]
    outs = refs[frames + 7 : -4]
    x, u_hi, u_lo, spec = refs[-4:]
    rows = blocks[0].shape[0]
    total = frames * rows
    for d in range(frames):
        x[pl.ds(where_ref[d], 1)] = blocks[d][...][None]
    step = 16
    for f in range(frames):
        for half in range(PT // LANES):

            def unit(i, carry, f=f, half=half):
                at = pl.multiple_of(i * step, step)
                keep = flag[pl.ds(at, step), :]
                filtered = []
                for q in range(RAD):
                    lanes = slice(PT * q + LANES * half, PT * q + LANES * (half + 1))
                    acc = None
                    for lag in range(f + 1):
                        term = fir[TAPS - 1 - lag, lanes][None, :] * x[f - lag, pl.ds(at, step), lanes].astype(f32)
                        acc = term if acc is None else acc + term
                    filtered.append(acc * keep)
                parts = []
                for re, im in real_dft16(filtered):
                    parts += [re] if im is None else [re, im]
                for n, part in enumerate(parts):
                    high, low = split(part)
                    to = (n, pl.ds(pl.multiple_of(f * rows + at, step), step), slice(LANES * half, LANES * (half + 1)))
                    u_hi[to] = high
                    u_lo[to] = low
                return carry

            lax.fori_loop(0, rows // step, unit, 0)

    def three(first, count, hi, lo):
        a = u_hi[first : first + count].reshape(count * total, PT)
        b = u_lo[first : first + count].reshape(count * total, PT)
        out = jnp.dot(a, hi, preferred_element_type=f32)
        out = out + jnp.dot(b, hi, preferred_element_type=f32)
        return out + jnp.dot(a, lo, preferred_element_type=f32)

    for n, c in enumerate((0, RAD // 2)):
        got = three(0 if c == 0 else RAD - 1, 1, slim_hi[n], slim_lo[n])
        spec[:total, c * HALF : (c + 1) * HALF] = got[:, :HALF].astype(bf16)
        spec[total:, c * HALF : (c + 1) * HALF] = got[:, HALF:].astype(bf16)
    for c in range(1, RAD // 2):
        got = three(2 * c - 1, 2, wide_hi[c - 1], wide_lo[c - 1])
        re = got[:total, :PT] - got[total:, PT:]
        im = got[:total, PT:] + got[total:, :PT]
        o = RAD - c
        spec[:total, c * HALF : (c + 1) * HALF] = re[:, :HALF].astype(bf16)
        spec[total:, c * HALF : (c + 1) * HALF] = im[:, :HALF].astype(bf16)
        spec[:total, o * HALF : (o + 1) * HALF] = re[:, HALF:].astype(bf16)
        spec[total:, o * HALF : (o + 1) * HALF] = (-im[:, HALF:]).astype(bf16)
    slots = outs[0].shape[0]
    for d, out in enumerate(outs):
        out[...] = lax.dot_general(
            select[d * slots : (d + 1) * slots, :], spec[...], (((1,), (1,)), ((), ())), preferred_element_type=f32
        ).astype(bf16)


def filterbank(where, blocks, fir, flag, select, pieces, slots):
    frames, rows = len(blocks), blocks[0].shape[0]
    total = frames * rows
    vmem = pl.BlockSpec(memory_space=pltpu.VMEM)
    consts = [jnp.asarray(t) for t in tables()]
    return pl.pallas_call(
        functools.partial(filterbank_kernel, frames),
        out_shape=[jax.ShapeDtypeStruct((slots, 2 * total), bf16)] * pieces,
        in_specs=[pl.BlockSpec(memory_space=pltpu.SMEM)] + [vmem] * (frames + 7),
        out_specs=[vmem] * pieces,
        scratch_shapes=[
            pltpu.VMEM((frames, rows, FL), bf16),
            pltpu.VMEM((RAD, total, PT), bf16),
            pltpu.VMEM((RAD, total, PT), bf16),
            pltpu.VMEM((2 * total, CH), bf16),
        ],
        compiler_params=pltpu.CompilerParams(vmem_limit_bytes=48 << 20),
        name="filterbank",
    )(where, *blocks, fir, flag, *consts, select)


def order_kernel(pieces, *refs):
    place, out, turned = refs[pieces:]
    half = refs[0].shape[1] // 2
    slots = refs[0].shape[0]
    parts = []
    for part in range(2):
        rows = jnp.concatenate([refs[d][:, part * half : (part + 1) * half] for d in range(pieces)], axis=1)
        got = jnp.dot(rows, place[...], preferred_element_type=f32)
        parts.append(got.reshape(slots // COARSE, 1, COARSE, got.shape[1]))
    re, im = parts
    shape = (2 * slots, re.shape[3])
    out[...] = jnp.concatenate([re, im], axis=1).reshape(shape).astype(bf16)
    turned[...] = jnp.concatenate([im, -re], axis=1).reshape(shape).astype(bf16)


def order(blocks, place):
    slots = blocks[0].shape[0]
    vmem = pl.BlockSpec(memory_space=pltpu.VMEM)
    shape = jax.ShapeDtypeStruct((2 * slots, place.shape[1]), bf16)
    return pl.pallas_call(
        functools.partial(order_kernel, len(blocks)),
        out_shape=[shape, shape],
        in_specs=[vmem] * (len(blocks) + 1),
        out_specs=[vmem] * 2,
        compiler_params=pltpu.CompilerParams(vmem_limit_bytes=40 << 20),
        name="order",
    )(*blocks, place)


def gram_kernel(frames, scale, pol_ref, own, turned, other, out):
    stations = own.shape[1] // frames
    first = pol_ref[0] == 0
    turns = (((0,), (0,)), ((), ()))
    for j in range(own.shape[0] // (2 * COARSE)):

        def stack(ref):
            rows = slice(2 * COARSE * j, 2 * COARSE * (j + 1))
            return jnp.concatenate([ref[rows, f * stations : (f + 1) * stations] for f in range(frames)], axis=0)

        mine, mine_turned, theirs = stack(own), stack(turned), stack(other)
        right = jnp.concatenate([jnp.where(first, mine, theirs), jnp.where(first, theirs, mine)], axis=1)
        for part, left in enumerate((mine, mine_turned)):
            got = lax.dot_general(left, right, turns, preferred_element_type=f32) * scale
            tiles = stations // LANES
            for q in range(2):
                for t in range(tiles):
                    at = q * stations + t * LANES
                    out[part, j, pl.ds(2 * t + q, stations, stride=2 * tiles), :] = got[:, at : at + LANES]


def gram(pol, own, turned, other, frames):
    coarse = own.shape[0] // (2 * COARSE)
    stations = own.shape[1] // frames
    tiles = stations // LANES
    per = 2
    rows = pl.BlockSpec((per * 2 * COARSE, own.shape[1]), lambda i: (i, 0))
    return pl.pallas_call(
        functools.partial(gram_kernel, frames, 1.0 / (frames * COARSE)),
        grid=(coarse // per,),
        out_shape=jax.ShapeDtypeStruct((2, coarse, stations * 2 * tiles, LANES), f32),
        in_specs=[pl.BlockSpec(memory_space=pltpu.SMEM), rows, rows, rows],
        out_specs=pl.BlockSpec((2, per, stations * 2 * tiles, LANES), lambda i: (0, i, 0, 0)),
        compiler_params=pltpu.CompilerParams(vmem_limit_bytes=40 << 20),
        name="gram",
    )(pol, own, turned, other)


def rolled(array, axis, start, size):
    return lax.dynamic_slice_in_dim(jnp.concatenate([array, array], axis=axis), start, size, axis=axis)


def fast_body(voltages, fir_coeffs, flags, station_slot, chan_map):
    chans, stns = lax.axis_size("chan"), lax.axis_size("stn")
    chan, stn, pol = lax.axis_index("chan"), lax.axis_index("stn"), lax.axis_index("pol")
    here = voltages.shape[1]
    stations = station_slot.shape[0]
    frames = chans
    rows = here // chans
    owners = chans * stns
    slots = CH // owners
    shares = voltages.reshape(chans, rows, FL)
    blocks = [lax.dynamic_index_in_dim(shares, chan, 0, keepdims=False)]
    for d in range(1, chans):
        share = lax.dynamic_index_in_dim(shares, (chan + d) % chans, 0, keepdims=False)
        blocks.append(lax.ppermute(share, "chan", [(i, (i + d) % chans) for i in range(chans)]))
    where = (chan - jnp.arange(chans, dtype=jnp.int32)) % chans
    keep = lax.dynamic_slice_in_dim(flags[0], chan * rows, rows).astype(f32)
    keep = jnp.broadcast_to(keep[:, None], (rows, LANES))
    lane_of = (chan_map % RAD) * HALF + chan_map // RAD
    lane_of = rolled(rolled(lane_of.reshape(chans, stns, slots), 0, chan, chans), 1, stn, stns)
    select = onehot(lane_of.reshape(CH), jnp.arange(CH, dtype=jnp.int32))
    pieces = filterbank(where, blocks, fir_coeffs, keep, select, owners, slots)
    got = []
    for d in range(owners):
        dc, ds = divmod(d, stns)
        if d == 0:
            got.append(pieces[0])
            continue
        route = [
            (i * stns + j, (i + dc) % chans * stns + (j + ds) % stns) for i in range(chans) for j in range(stns)
        ]
        got.append(lax.ppermute(pieces[d], ("chan", "stn"), route))
    dist = jnp.arange(owners, dtype=jnp.int32)
    row0 = (stn - dist % stns) % stns * here + (chan - dist // stns) % chans * rows
    row = row0[:, None, None] + jnp.arange(rows, dtype=jnp.int32)[None, None, :]
    row = row + stations * jnp.arange(frames, dtype=jnp.int32)[None, :, None]
    col = station_slot[None, :] + stations * jnp.arange(frames, dtype=jnp.int32)[:, None]
    place = onehot(row.reshape(-1), col.reshape(-1))
    own, turned = order(got, place)
    other = lax.ppermute(own, "pol", [(0, 1), (1, 0)])
    out = gram(pol.reshape(1), own, turned, other, frames)
    tiles = stations // LANES
    out = out.reshape(2, -1, stations, tiles, 2, LANES).transpose(0, 1, 2, 4, 3, 5)
    return out.reshape(2, -1, 1, stations, 2, stations)


def general_body(voltages, fir_coeffs, flags, station_slot, chan_map):
    high = lax.Precision.HIGHEST
    here = voltages.shape[1]
    chans, stns = lax.axis_size("chan"), lax.axis_size("stn")
    frames_here = voltages.shape[2] // FL
    frames = voltages.reshape(here, frames_here, FL)
    history = []
    for distance in range(1, (TAPS - 1 + frames_here - 1) // frames_here + 1):
        route = [(i - distance, i) for i in range(distance, chans)]
        history = [lax.ppermute(frames, "chan", route)] + history
    window = jnp.concatenate(history + [frames], axis=1)
    window = window[:, window.shape[1] - frames_here - TAPS + 1 :]
    filtered = jnp.zeros((here, frames_here, FL), f32)
    for tap in range(TAPS):
        filtered = filtered + fir_coeffs[tap][None, None, :] * window[:, tap : tap + frames_here, :].astype(f32)
    side = math.isqrt(FL)

    def angles(rows, cols, period):
        product = jnp.arange(rows, dtype=jnp.int32)[:, None] * jnp.arange(cols, dtype=jnp.int32)[None, :]
        phase = (product % period).astype(f32) * (2.0 * math.pi / period)
        return jnp.cos(phase), jnp.sin(phase)

    grid = filtered.reshape(here, frames_here, side, side)
    cos, sin = angles(side, side, side)
    re = jnp.einsum("sfqp,qc->sfpc", grid, cos, precision=high)
    im = -jnp.einsum("sfqp,qc->sfpc", grid, sin, precision=high)
    cos, sin = angles(side, side, FL)
    re, im = re * cos + im * sin, im * cos - re * sin
    cos, sin = angles(side, side // 2, side)
    form = "sfpc,pk->kcfs"
    out_re = jnp.einsum(form, re, cos, precision=high) + jnp.einsum(form, im, sin, precision=high)
    out_im = jnp.einsum(form, im, cos, precision=high) - jnp.einsum(form, re, sin, precision=high)
    weight = jnp.tile(flags[0].astype(f32), frames_here) * FL**-0.5
    shape = (CH, 1, frames_here * here)
    spectra = jnp.concatenate(
        [(out_re.reshape(shape) * weight).astype(bf16), (out_im.reshape(shape) * weight).astype(bf16)], axis=1
    )
    select = onehot(chan_map, jnp.arange(CH, dtype=jnp.int32))
    spectra = jnp.einsum("sc,cpn->spn", select, spectra, preferred_element_type=f32).astype(bf16)
    pieces = lax.all_to_all(spectra, ("chan", "stn"), split_axis=0, concat_axis=2, tiled=True)
    pieces = pieces.reshape(-1, 2, chans, stns, frames_here, here).transpose(0, 1, 3, 5, 2, 4)
    total = chans * frames_here
    pieces = pieces.reshape(-1, COARSE, 2, stns * here, total)
    place = onehot(station_slot, jnp.arange(stns * here, dtype=jnp.int32))
    own = jnp.einsum("ar,jkprf->jkpaf", place, pieces, preferred_element_type=f32).astype(bf16)
    both = lax.all_gather(own[None], "pol", axis=0, tiled=True)
    form = "jkrf,qjksf->jrqs"

    def dot(left, right):
        return jnp.einsum(form, left, right, preferred_element_type=f32)

    own_re, own_im, re, im = own[:, :, 0], own[:, :, 1], both[:, :, :, 0], both[:, :, :, 1]
    block = jnp.stack([dot(own_re, re) + dot(own_im, im), dot(own_im, re) - dot(own_re, im)], axis=0)
    return (block * (1.0 / (total * COARSE)))[:, :, None]


def body(voltages, fir_coeffs, flags, station_slot, chan_map):
    chans, stns = lax.axis_size("chan"), lax.axis_size("stn")
    here, stations = voltages.shape[1], station_slot.shape[0]
    fits = (
        voltages.shape[2] == FL
        and chans <= TAPS
        and here % chans == 0
        and here // chans % 16 == 0
        and here % LANES == 0
        and stations % LANES == 0
        and CH // (chans * stns) % 16 == 0
    )
    return (fast_body if fits else general_body)(voltages, fir_coeffs, flags, station_slot, chan_map)


def solution(mesh):
    in_specs = (P(("grp", "pol"), "stn", "chan"), P(), P(("grp", "pol"), "stn"), P(), P())
    out_specs = P("grp", ("chan", "stn"), "pol", None, None, None)
    return jax.shard_map(body, mesh=mesh, in_specs=in_specs, out_specs=out_specs, check_vma=False)
```

time: 353 us -> 87.1 us (0.25); the launches traced: 348 us -> 86.9 us
  local copies, waits for them, and re-layouts: 94.2 us -> 5.58 us
  waiting for transfers between devices: 119 us -> 35.1 us
  matrix products: 58.8 us -> 0 us
  other arithmetic: 46.3 us -> 6.29 us
  Pallas kernels: 0 us -> 25.4 us
  between operations: 13.8 us -> 0.15 us
    dot_general x10 -> x0, matrix products: 58.8 us -> none  [the longest x1 14.7 us: body(): jnp.einsum(form, own_im, other_im, preferred_element_type=jnp.float32)]
    mul x1 -> x0, local copies, waits for them, and re-layouts: 54.9 us -> none  [body(): gram = gram * (1.0 / (total_frames * COARSE))]
    ppermute x4 -> x11, waiting for transfers between devices: 82.9 us -> 35.1 us  [the longest x7 18.5 us: fast_body(): got.append(lax.ppermute(pieces[d], ('chan', 'stn'), route))]
    pallas_call x0 -> x3, Pallas kernels: none -> 25.4 us  [the longest x1 14.9 us: gram(): pl.pallas_call(functools.partial(gram_kernel, frames, 1.0 / (frames * COA...]
    all_to_all x1 -> x0, waiting for transfers between devices: 22.1 us -> none  [body(): lax.all_to_all(spectra, ('chan', 'stn'), split_axis=0, concat_axis=2, til...]
    select_n x4 -> x1, other arithmetic: 21 us -> 0.01 us  [fast_body(): where = (chan - jnp.arange(chans, dtype=jnp.int32)) % chans]
    gather x3 -> x0, local copies, waits for them, and re-layouts: 18.5 us -> none  [the longest x2 11.4 us: body(): turned = jnp.take(turned, station_slot, axis=3)]
    mul x2 -> x1, other arithmetic: 18.3 us -> 0.01 us  [fast_body(): row = row + stations * jnp.arange(frames, dtype=jnp.int32)[None, :, None]]
  transfers between devices with their start and end apart: 6 -> 11, of which waited for: 4 -> 7; matrix products, arithmetic and copies ran while one was open for 0% -> 7% of each run, Pallas kernels for 0% -> 0%
where the time goes in v1:
time: 87.1 us; the launch traced here: 86.9 us
  waiting for transfers between devices  35.1 us (40%)
  Pallas kernels  25.4 us (29%)
  starting transfers between devices  14.4 us (17%)
  other arithmetic  6.29 us (7%)
  local copies, waits for them, and re-layouts  5.58 us (6%)
    ppermute x7, waiting for transfers between devices, fast_body(): got.append(lax.ppermute(pieces[d], ('chan', 'stn'), route))  18.5 us
    pallas_call x1, Pallas kernels, gram(): pl.pallas_call(functools.partial(gram_kernel, frames, 1.0 / (frames * COA...  14.9 us
    ppermute x3, waiting for transfers between devices, fast_body(): lax.ppermute(share, 'chan', [(i, (i + d) % chans) for i in range(chans)])  14.3 us
    pallas_call x1, Pallas kernels, filterbank(): pl.pallas_call(functools.partial(filterbank_kernel, frames), out_shape=[j...  9.26 us
    ppermute x7, starting transfers between devices, fast_body(): got.append(lax.ppermute(pieces[d], ('chan', 'stn'), route))  9.18 us
    convert_element_type x2, other arithmetic, onehot(): return (rows[:, None] == cols[None, :]).astype(bf16)  5.22 us
    ppermute x3, starting transfers between devices, fast_body(): lax.ppermute(share, 'chan', [(i, (i + d) % chans) for i in range(chans)])  4.67 us
    unnamed x24, local copies, waits for them, and re-layouts  3.3 us
  transfers between devices with their start and end apart: 11, of which 7 were waited for; matrix products, arithmetic and copies ran while one was open for 7% of the time, Pallas kernels for 0%

profile of v1, /device:TPU:9, one launch (start us, length us, event | category | flops | bytes accessed | tf_op | source)
XLA Modules:
  0.0 86.9 jit_solution(15791013905148829064)
XLA Ops:
  0.0 2.1 %dynamic-slice_bitcast_fusion = (bf16[32,4096]{1,0:T(8,128)(2,1)}, bf16[32,4096]{1,0:T(8,128)(2,1)}, bf16[32,4096]{1,0:T(8,128)(2,1)}, bf16[32,4096]{1,0:T(8,128)(2,1)S(1)}) fusion(bf16[4,32,4096]{2,1,0:T(8,128)(2,1)} %bitcast.23, s32[]{:T(128)S(6)} %select_n.96, s32[]{:T(128)S(6)} %select_n.94, s32[]{:T(128)S(6)} %select_n.92, s32[]{:T(128)S(6)} %select_n.90), kind=kLoop, calls=%fused_computation.3 | loop fusion | bytes 2097168 | tf_op jit(solution)/shard_map/jit(dynamic_index_in_dim)/squeeze | solution.py:254
  2.1 0.0 collective-permute-start.2
  2.1 2.5 %collective-permute-start.1 = (bf16[32,4096]{1,0:T(8,128)(2,1)}, bf16[32,4096]{1,0:T(8,128)(2,1)S(1)}, u32[]{:S(2)}, u32[]{:S(2)}) collective-permute-start(bf16[32,4096]{1,0:T(8,128)(2,1)} %get-tuple-element.26), channel_id=1, source_target_pairs={{0,8},{4,12},{8,0},{12,4},{1,9},{5,13},{9,1},{13,5},{2,10},{6,14},... | collective-permute-start | bytes 786440 | tf_op jit(solution)/shard_map/ppermute | solution.py:255
  4.6 2.2 %collective-permute-start = (bf16[32,4096]{1,0:T(8,128)(2,1)}, bf16[32,4096]{1,0:T(8,128)(2,1)}, u32[]{:S(2)}, u32[]{:S(2)}) collective-permute-start(bf16[32,4096]{1,0:T(8,128)(2,1)} %get-tuple-element.27), channel_id=1, source_target_pairs={{0,4},{4,8},{8,12},{12,0},{1,5},{5,9},{9,13},{13,1},{2,6},{6,10},{... | collective-permute-start | bytes 786440 | tf_op jit(solution)/shard_map/ppermute | solution.py:255
  6.8 0.7 fusion.2
  7.6 0.0 copy-start.9
  7.6 0.0 copy-start.10
  7.7 0.0 copy-start
  7.7 0.0 copy-start.1
  7.7 0.0 copy-start.2
  7.7 0.0 copy-start.3
  7.7 4.8 %fusion.refs_10_ = bf16[2048,2048]{1,0:T(8,128)(2,1)} fusion(s32[2048]{0:T(1024)S(1)} %bitcast.24), kind=kLoop, calls=%fused_computation.1 | loop fusion | flops 8388608 | bytes 8396800 | tf_op jit(solution)/shard_map/convert_element_type | solution.py:26
  12.5 0.0 copy-done.9
  12.5 0.1 add_bitcast_fusion
  12.6 0.0 copy-done.10
  12.6 0.1 fusion.19
  12.7 0.1 iota_add_fusion
  12.7 0.0 collective-permute-done.2.refs_3_
  12.8 8.7 %collective-permute-done.1.refs_2_ = bf16[32,4096]{1,0:T(8,128)(2,1)S(1)} collective-permute-done((bf16[32,4096]{1,0:T(8,128)(2,1)}, bf16[32,4096]{1,0:T(8,128)(2,1)S(1)}, u32[]{:S(2)}, u32[]{:S(2)}) %collective-permute-start.1) | collective-permute-done | bytes 262176 | tf_op jit(solution)/shard_map/ppermute | solution.py:255
  21.4 5.6 %collective-permute-done.refs_1_ = bf16[32,4096]{1,0:T(8,128)(2,1)} collective-permute-done((bf16[32,4096]{1,0:T(8,128)(2,1)}, bf16[32,4096]{1,0:T(8,128)(2,1)}, u32[]{:S(2)}, u32[]{:S(2)}) %collective-permute-start) | collective-permute-done | bytes 262176 | tf_op jit(solution)/shard_map/ppermute | solution.py:255
  27.0 0.1 broadcast_in_dim.2.refs_5_
  27.1 0.0 copy-done
  27.1 0.0 copy-done.1
  27.1 0.0 copy-done.2
  27.1 0.0 copy-done.3
  27.1 9.3 %filterbank.1 = (bf16[256,256]{1,0:T(8,128)(2,1)S(1)}, bf16[256,256]{1,0:T(8,128)(2,1)}, bf16[256,256]{1,0:T(8,128)(2,1)}, bf16[256,256]{1,0:T(8,128)(2,1)S(1)},...) custom-call(s32[4]{0:T(128)S(1)} %and_select_fusion.4.where_ref, ...), custom_call_target="tpu_custom_call" | custom-call | tf_op jit(solution)/shard_map/filterbank/pallas_call | solution.py:155
  36.4 0.0 copy-start.4
  36.4 0.6 copy-done.4
  37.0 0.0 copy-start.5
  37.0 0.7 copy-done.5
  37.7 0.0 copy-start.6
  37.7 0.7 copy-done.6
  38.4 0.0 copy-start.7
  38.4 0.6 copy-done.7
  39.0 0.0 copy-start.8
  39.0 0.7 copy-done.8
  39.7 1.2 %collective-permute-start.3 = (bf16[256,256]{1,0:T(8,128)(2,1)}, bf16[256,256]{1,0:T(8,128)(2,1)S(1)}, u32[]{:S(2)}, u32[]{:S(2)}) collective-permute-start(bf16[256,256]{1,0:T(8,128)(2,1)} %get-tuple-element.16), channel_id=1, source_target_pairs={{0,2},{2,0},{4,6},{6,4},{8,10},{10,8},{12,14},{14,12},{1,3},{3,1},... | collective-permute-start | bytes 393224 | tf_op jit(solution)/shard_map/ppermute | solution.py:272
  40.9 2.2 %collective-permute-start.4 = (bf16[256,256]{1,0:T(8,128)(2,1)}, bf16[256,256]{1,0:T(8,128)(2,1)S(1)}, u32[]{:S(2)}, u32[]{:S(2)}) collective-permute-start(bf16[256,256]{1,0:T(8,128)(2,1)} %get-tuple-element.17), channel_id=1, source_target_pairs={{0,4},{2,6},{4,8},{6,10},{8,12},{10,14},{12,0},{14,2},{1,5},{3,7},... | collective-permute-start | bytes 393224 | tf_op jit(solution)/shard_map/ppermute | solution.py:272
  43.1 0.1 broadcast_add_fusion
  43.1 0.1 add.179
  43.2 0.0 collective-permute-start.5
  43.2 1.3 %collective-permute-start.6 = (bf16[256,256]{1,0:T(8,128)(2,1)}, bf16[256,256]{1,0:T(8,128)(2,1)S(1)}, u32[]{:S(2)}, u32[]{:S(2)}) collective-permute-start(bf16[256,256]{1,0:T(8,128)(2,1)} %copy-done.7), channel_id=1, source_target_pairs={{0,8},{2,10},{4,12},{6,14},{8,0},{10,2},{12,4},{14,6},{1,9},{3,11}... | collective-permute-start | bytes 393224 | tf_op jit(solution)/shard_map/ppermute | solution.py:272
  44.5 1.9 %collective-permute-start.7 = (bf16[256,256]{1,0:T(8,128)(2,1)}, bf16[256,256]{1,0:T(8,128)(2,1)S(1)}, u32[]{:S(2)}, u32[]{:S(2)}) collective-permute-start(bf16[256,256]{1,0:T(8,128)(2,1)} %copy-done.6), channel_id=1, source_target_pairs={{0,10},{2,8},{4,14},{6,12},{8,2},{10,0},{12,6},{14,4},{1,11},{3,9}... | collective-permute-start | bytes 393224 | tf_op jit(solution)/shard_map/ppermute | solution.py:272
  46.5 0.0 collective-permute-done.3.refs_1_
  46.5 1.5 %collective-permute-start.8 = (bf16[256,256]{1,0:T(8,128)(2,1)}, bf16[256,256]{1,0:T(8,128)(2,1)S(1)}, u32[]{:S(2)}, u32[]{:S(2)}) collective-permute-start(bf16[256,256]{1,0:T(8,128)(2,1)} %copy-done.5), channel_id=1, source_target_pairs={{0,12},{2,14},{4,0},{6,2},{8,4},{10,6},{12,8},{14,10},{1,13},{3,15... | collective-permute-start | bytes 393224 | tf_op jit(solution)/shard_map/ppermute | solution.py:272
  48.0 0.0 collective-permute-done.4.refs_2_
  48.0 1.0 %collective-permute-start.9 = (bf16[256,256]{1,0:T(8,128)(2,1)}, bf16[256,256]{1,0:T(8,128)(2,1)S(1)}, u32[]{:S(2)}, u32[]{:S(2)}) collective-permute-start(bf16[256,256]{1,0:T(8,128)(2,1)} %copy-done.4), channel_id=1, source_target_pairs={{0,14},{2,12},{4,2},{6,0},{8,6},{10,4},{12,10},{14,8},{1,15},{3,13... | collective-permute-start | bytes 393224 | tf_op jit(solution)/shard_map/ppermute | solution.py:272
  49.0 0.4 compare_convert_fusion.refs_8_
  49.4 0.0 collective-permute-done.5.refs_3_
  49.4 12.0 %collective-permute-done.6.refs_4_ = bf16[256,256]{1,0:T(8,128)(2,1)S(1)} collective-permute-done((bf16[256,256]{1,0:T(8,128)(2,1)}, bf16[256,256]{1,0:T(8,128)(2,1)S(1)}, u32[]{:S(2)}, u32[]{:S(2)}) %collective-permute-start.6) | collective-permute-done | bytes 131104 | tf_op jit(solution)/shard_map/ppermute | solution.py:272
  61.5 2.8 %collective-permute-done.7.refs_5_ = bf16[256,256]{1,0:T(8,128)(2,1)S(1)} collective-permute-done((bf16[256,256]{1,0:T(8,128)(2,1)}, bf16[256,256]{1,0:T(8,128)(2,1)S(1)}, u32[]{:S(2)}, u32[]{:S(2)}) %collective-permute-start.7) | collective-permute-done | bytes 131104 | tf_op jit(solution)/shard_map/ppermute | solution.py:272
  64.3 0.2 collective-permute-done.8.refs_6_
  64.5 3.4 %collective-permute-done.9.refs_7_ = bf16[256,256]{1,0:T(8,128)(2,1)S(1)} collective-permute-done((bf16[256,256]{1,0:T(8,128)(2,1)}, bf16[256,256]{1,0:T(8,128)(2,1)S(1)}, u32[]{:S(2)}, u32[]{:S(2)}) %collective-permute-start.9) | collective-permute-done | bytes 131104 | tf_op jit(solution)/shard_map/ppermute | solution.py:272
  67.9 1.2 %order.1 = (bf16[512,1024]{1,0:T(8,128)(2,1)S(1)}, bf16[512,1024]{1,0:T(8,128)(2,1)S(1)}) custom-call(bf16[256,256]{1,0:T(8,128)(2,1)S(1)} %get-tuple-element.15.refs_0_, bf16[256,256]{1,0:T(8,128)(2,1)S(1)} %collective-permute-done.3.refs_1_, bf16[256,256]{1,0:T(8,128)(2,1)S(1)} %collective-permute-done.4.refs_2_, ...), custom_call_target="tpu_custom_call" | custom-call | tf_op jit(solution)/shard_map/order/pallas_call | solution.py:190
  69.2 0.6 collective-permute-start.10
  69.7 2.3 %collective-permute-done.10.other = bf16[512,1024]{1,0:T(8,128)(2,1)S(1)} collective-permute-done((bf16[512,1024]{1,0:T(8,128)(2,1)S(1)}, bf16[512,1024]{1,0:T(8,128)(2,1)S(1)}, u32[]{:S(2)}, u32[]{:S(2)}) %collective-permute-start.10) | collective-permute-done | bytes 1048608 | tf_op jit(solution)/shard_map/ppermute | solution.py:280
  72.0 14.9 %gram.1 = f32[2,32,1024,128]{3,2,1,0:T(8,128)} custom-call(s32[1]{0:T(128)} %bitcast.pol_ref, bf16[512,1024]{1,0:T(8,128)(2,1)S(1)} %get-tuple-element.23.own, bf16[512,1024]{1,0:T(8,128)(2,1)S(1)} %get-tuple-element.24.turned, bf16[512,1024]{1,0:T(8,128)(2,1)S(1)} %collective-permute-done.10.other), custom_call_target="tpu_custom_call" | custom-call | tf_op jit(solution)/shard_map/gram/pallas_call | solution.py:227
  (8 shorter events, 0.1 us)
Async XLA Ops:
  2.1 10.6 %collective-permute-start.2 = (bf16[32,4096]{1,0:T(8,128)(2,1)}, bf16[32,4096]{1,0:T(8,128)(2,1)S(1)}, u32[]{:S(2)}, u32[]{:S(2)}) collective-permute-start(bf16[32,4096]{1,0:T(8,128)(2,1)} %get-tuple-element.25), channel_id=1, source_target_pairs={{0,12},{4,0},{8,4},{12,8},{1,13},{5,1},{9,5},{13,9},{2,14},{6,2},{... | collective-permute-start | bytes 786440 | tf_op jit(solution)/shard_map/ppermute | solution.py:255
  2.1 19.3 %collective-permute-start.1 = (bf16[32,4096]{1,0:T(8,128)(2,1)}, bf16[32,4096]{1,0:T(8,128)(2,1)S(1)}, u32[]{:S(2)}, u32[]{:S(2)}) collective-permute-start(bf16[32,4096]{1,0:T(8,128)(2,1)} %get-tuple-element.26), channel_id=1, source_target_pairs={{0,8},{4,12},{8,0},{12,4},{1,9},{5,13},{9,1},{13,5},{2,10},{6,14},... | collective-permute-start | bytes 786440 | tf_op jit(solution)/shard_map/ppermute | solution.py:255
  4.6 22.5 %collective-permute-start = (bf16[32,4096]{1,0:T(8,128)(2,1)}, bf16[32,4096]{1,0:T(8,128)(2,1)}, u32[]{:S(2)}, u32[]{:S(2)}) collective-permute-start(bf16[32,4096]{1,0:T(8,128)(2,1)} %get-tuple-element.27), channel_id=1, source_target_pairs={{0,4},{4,8},{8,12},{12,0},{1,5},{5,9},{9,13},{13,1},{2,6},{6,10},{... | collective-permute-start | bytes 786440 | tf_op jit(solution)/shard_map/ppermute | solution.py:255
  7.6 4.9 %copy-start.9 = (s32[256]{0:T(256)S(1)}, s32[256]{0:T(256)}, u32[]{:S(2)}) copy-start(s32[256]{0:T(256)} %param.12) | copy-start | bytes 3076
  7.6 5.0 %copy-start.10 = (s32[1,128]{1,0:T(1,128)S(1)}, s32[1,128]{1,0:T(1,128)}, u32[]{:S(2)}) copy-start(s32[1,128]{1,0:T(1,128)} %param.11) | copy-start | bytes 1540
  7.7 19.5 %copy-start = (bf16[7,256,512]{2,1,0:T(8,128)(2,1)S(1)}, bf16[7,256,512]{2,1,0:T(8,128)(2,1)}, u32[]{:S(2)}) copy-start(bf16[7,256,512]{2,1,0:T(8,128)(2,1)} %constant.136.clone.refs_6_) | copy-start | bytes 5505028
  7.7 19.4 %copy-start.1 = (f32[16,4096]{1,0:T(8,128)S(1)}, f32[16,4096]{1,0:T(8,128)}, u32[]{:S(2)}) copy-start(f32[16,4096]{1,0:T(8,128)} %refs_4_.1) | copy-start | bytes 786436
  7.7 19.4 %copy-start.2 = (bf16[2,256,256]{2,1,0:T(8,128)(2,1)S(1)}, bf16[2,256,256]{2,1,0:T(8,128)(2,1)}, u32[]{:S(2)}) copy-start(bf16[2,256,256]{2,1,0:T(8,128)(2,1)} %constant.139.clone.refs_9_) | copy-start | bytes 786436
  7.7 19.4 %copy-start.3 = (bf16[2,256,256]{2,1,0:T(8,128)(2,1)S(1)}, bf16[2,256,256]{2,1,0:T(8,128)(2,1)}, u32[]{:S(2)}) copy-start(bf16[2,256,256]{2,1,0:T(8,128)(2,1)} %constant.138.clone.refs_8_) | copy-start | bytes 786436
  36.4 0.6 copy-start.4
  37.0 0.7 copy-start.5
  37.7 0.7 copy-start.6
  38.4 0.7 copy-start.7
  39.0 0.7 copy-start.8
  39.7 6.8 %collective-permute-start.3 = (bf16[256,256]{1,0:T(8,128)(2,1)}, bf16[256,256]{1,0:T(8,128)(2,1)S(1)}, u32[]{:S(2)}, u32[]{:S(2)}) collective-permute-start(bf16[256,256]{1,0:T(8,128)(2,1)} %get-tuple-element.16), channel_id=1, source_target_pairs={{0,2},{2,0},{4,6},{6,4},{8,10},{10,8},{12,14},{14,12},{1,3},{3,1},... | collective-permute-start | bytes 393224 | tf_op jit(solution)/shard_map/ppermute | solution.py:272
  40.9 7.1 %collective-permute-start.4 = (bf16[256,256]{1,0:T(8,128)(2,1)}, bf16[256,256]{1,0:T(8,128)(2,1)S(1)}, u32[]{:S(2)}, u32[]{:S(2)}) collective-permute-start(bf16[256,256]{1,0:T(8,128)(2,1)} %get-tuple-element.17), channel_id=1, source_target_pairs={{0,4},{2,6},{4,8},{6,10},{8,12},{10,14},{12,0},{14,2},{1,5},{3,7},... | collective-permute-start | bytes 393224 | tf_op jit(solution)/shard_map/ppermute | solution.py:272
  43.2 6.2 %collective-permute-start.5 = (bf16[256,256]{1,0:T(8,128)(2,1)}, bf16[256,256]{1,0:T(8,128)(2,1)S(1)}, u32[]{:S(2)}, u32[]{:S(2)}) collective-permute-start(bf16[256,256]{1,0:T(8,128)(2,1)} %copy-done.8), channel_id=1, source_target_pairs={{0,6},{2,4},{4,10},{6,8},{8,14},{10,12},{12,2},{14,0},{1,7},{3,5},... | collective-permute-start | bytes 393224 | tf_op jit(solution)/shard_map/ppermute | solution.py:272
  43.2 18.2 %collective-permute-start.6 = (bf16[256,256]{1,0:T(8,128)(2,1)}, bf16[256,256]{1,0:T(8,128)(2,1)S(1)}, u32[]{:S(2)}, u32[]{:S(2)}) collective-permute-start(bf16[256,256]{1,0:T(8,128)(2,1)} %copy-done.7), channel_id=1, source_target_pairs={{0,8},{2,10},{4,12},{6,14},{8,0},{10,2},{12,4},{14,6},{1,9},{3,11}... | collective-permute-start | bytes 393224 | tf_op jit(solution)/shard_map/ppermute | solution.py:272
  44.5 19.7 %collective-permute-start.7 = (bf16[256,256]{1,0:T(8,128)(2,1)}, bf16[256,256]{1,0:T(8,128)(2,1)S(1)}, u32[]{:S(2)}, u32[]{:S(2)}) collective-permute-start(bf16[256,256]{1,0:T(8,128)(2,1)} %copy-done.6), channel_id=1, source_target_pairs={{0,10},{2,8},{4,14},{6,12},{8,2},{10,0},{12,6},{14,4},{1,11},{3,9}... | collective-permute-start | bytes 393224 | tf_op jit(solution)/shard_map/ppermute | solution.py:272
  46.5 18.0 %collective-permute-start.8 = (bf16[256,256]{1,0:T(8,128)(2,1)}, bf16[256,256]{1,0:T(8,128)(2,1)S(1)}, u32[]{:S(2)}, u32[]{:S(2)}) collective-permute-start(bf16[256,256]{1,0:T(8,128)(2,1)} %copy-done.5), channel_id=1, source_target_pairs={{0,12},{2,14},{4,0},{6,2},{8,4},{10,6},{12,8},{14,10},{1,13},{3,15... | collective-permute-start | bytes 393224 | tf_op jit(solution)/shard_map/ppermute | solution.py:272
  48.0 19.9 %collective-permute-start.9 = (bf16[256,256]{1,0:T(8,128)(2,1)}, bf16[256,256]{1,0:T(8,128)(2,1)S(1)}, u32[]{:S(2)}, u32[]{:S(2)}) collective-permute-start(bf16[256,256]{1,0:T(8,128)(2,1)} %copy-done.4), channel_id=1, source_target_pairs={{0,14},{2,12},{4,2},{6,0},{8,6},{10,4},{12,10},{14,8},{1,15},{3,13... | collective-permute-start | bytes 393224 | tf_op jit(solution)/shard_map/ppermute | solution.py:272
  69.2 2.8 %collective-permute-start.10 = (bf16[512,1024]{1,0:T(8,128)(2,1)S(1)}, bf16[512,1024]{1,0:T(8,128)(2,1)S(1)}, u32[]{:S(2)}, u32[]{:S(2)}) collective-permute-start(bf16[512,1024]{1,0:T(8,128)(2,1)S(1)} %get-tuple-element.23.own), channel_id=1, source_target_pairs={{0,1},{1,0},{2,3},{3,2},{4,5},{5,4},{6,7},{7,6},{8,9},{9,8},{10,11... | collective-permute-start | bytes 3145736 | tf_op jit(solution)/shard_map/ppermute | solution.py:280

commit v2 on v1

v2 whole, which is shorter than its diff:
```python
import functools
import math

import jax
import jax.numpy as jnp
import numpy as np
from jax import lax
from jax.experimental import pallas as pl
from jax.experimental.pallas import tpu as pltpu
from jax.sharding import PartitionSpec as P

TAPS = 16
FL = 4096
CH = 2048
COARSE = 8
RAD = 16
PT = FL // RAD
HALF = PT // 2
LANES = 128
BATCH = 4

f32 = jnp.float32
bf16 = jnp.bfloat16


def onehot(rows, cols):
    return (rows[:, None] == cols[None, :]).astype(bf16)


@functools.cache
def tables():
    p = np.arange(PT)[None, :]
    rows = []
    for k2 in (np.arange(HALF), PT - 1 - np.arange(HALF)):
        phase = (k2[:, None] * p % PT) * (2.0 * math.pi / PT)
        rows += [np.cos(phase), -np.sin(phase)]
    table = np.concatenate(rows) * FL**-0.5
    high = table.astype(np.float32).astype(jnp.bfloat16)
    low = (table - high.astype(np.float64)).astype(np.float32).astype(jnp.bfloat16)
    phase = np.arange(1, RAD // 2 + 1)[:, None] * p * (2.0 * math.pi / FL)
    twiddle = np.concatenate([np.cos(phase), np.sin(phase)]).astype(np.float32)
    return high, low, twiddle


def real_dft16(x):
    def dft4(a0, a1, a2, a3):
        s02, d02, s13, d13 = a0 + a2, a0 - a2, a1 + a3, a1 - a3
        return s02 + s13, d02, -d13, s02 - s13

    cols = [dft4(x[b], x[4 + b], x[8 + b], x[12 + b]) for b in range(4)]
    out = [None] * 9
    r0, r1, i1, r2 = dft4(*(cols[b][0] for b in range(4)))
    out[0], out[4], out[8] = (r0, None), (r1, i1), (r2, None)
    h = math.sqrt(0.5)
    v0, v1, v2, v3 = (cols[b][3] for b in range(4))
    pr, pi = h * (v1 - v3), -h * (v1 + v3)
    out[2] = (v0 + pr, pi - v2)
    out[6] = (v0 - pr, v2 + pi)
    c1, s1 = math.cos(math.pi / 8), math.sin(math.pi / 8)
    re0, im0 = cols[0][1], cols[0][2]
    re1 = cols[1][1] * c1 + cols[1][2] * s1
    im1 = cols[1][2] * c1 - cols[1][1] * s1
    re2 = (cols[2][1] + cols[2][2]) * h
    im2 = (cols[2][2] - cols[2][1]) * h
    re3 = cols[3][1] * s1 + cols[3][2] * c1
    im3 = cols[3][2] * s1 - cols[3][1] * c1
    ar, ai, br, bi = re0 + re2, im0 + im2, re0 - re2, im0 - im2
    cr, ci, dr, di = re1 + re3, im1 + im3, re1 - re3, im1 - im3
    out[1] = (ar + cr, ai + ci)
    out[5] = (br + di, bi - dr)
    out[7] = (ar - cr, ci - ai)
    out[3] = (br - di, -bi - dr)
    return out


def split(value):
    high = value.astype(bf16)
    return high, (value - high.astype(f32)).astype(bf16)


def filterbank_kernel(frames, rows, offset, share, sizes, chan_ref, *refs):
    volts, *blocks = refs[:frames]
    fir_in, flag_in, twiddle_in, high_in, low_in, select_in = refs[frames : frames + 6]
    pieces = len(refs) - frames - 6 - 14
    outs = refs[frames + 6 : frames + 6 + pieces]
    x, fir, flag, twiddle, dft_hi, dft_lo, select, u_hi, u_lo, spec, ready, in_sems, load_sems, out_sems = refs[
        frames + 6 + pieces :
    ]
    total = frames * rows
    chan = chan_ref[0]
    begin = pl.multiple_of(chan * share + offset, rows)
    first = []
    for d in range(frames):
        source = volts.at[0, pl.ds(begin, rows)] if d == 0 else blocks[d - 1]
        first.append(pltpu.make_async_copy(source, x.at[lax.rem(chan + frames - d, frames)], in_sems.at[d]))
    for n, (source, to) in enumerate(((fir_in, fir), (flag_in, flag), (twiddle_in, twiddle))):
        first.append(pltpu.make_async_copy(source, to, in_sems.at[frames + n]))
    loads = [
        pltpu.make_async_copy(source, to, load_sems.at[n])
        for n, (source, to) in enumerate(((high_in, dft_hi), (low_in, dft_lo), (select_in, select)))
    ]
    for copy in first + loads:
        copy.start()
    for copy in first:
        copy.wait()
    step = 16
    halves = PT // LANES
    for f in range(frames):

        def unit(i, carry, f=f):
            at = pl.multiple_of(i // halves * step, step)
            base = pl.multiple_of(i % halves * LANES, LANES)
            filtered = []
            for q in range(RAD):
                lanes = pl.ds(pl.multiple_of(PT * q + base, LANES), LANES)
                acc = None
                for lag in range(f + 1):
                    tap = TAPS - 1 - lag
                    term = fir[tap : tap + 1, lanes] * x[f - lag, pl.ds(at, step), lanes].astype(f32)
                    acc = term if acc is None else acc + term
                filtered.append(acc)
            parts = []
            for c, (re, im) in enumerate(real_dft16(filtered)):
                if c == 0:
                    parts.append(re)
                    continue
                cos = twiddle[c - 1 : c, pl.ds(base, LANES)]
                sin = twiddle[RAD // 2 + c - 1 : RAD // 2 + c, pl.ds(base, LANES)]
                parts += [re * cos, -re * sin] if im is None else [re * cos + im * sin, im * cos - re * sin]
            for n, part in enumerate(parts):
                high, low = split(part)
                to = (n, pl.ds(pl.multiple_of(f * rows + at, step), step), pl.ds(base, LANES))
                u_hi[to] = high
                u_lo[to] = low
            return carry

        lax.fori_loop(0, rows // step * halves, unit, 0)
    for copy in loads[:2]:
        copy.wait()
    contract = (((1,), (1,)), ((), ()))

    def three(at, count, outputs):
        a = u_hi[pl.ds(at, count)].reshape(count * total, PT)
        b = u_lo[pl.ds(at, count)].reshape(count * total, PT)
        hi, lo = dft_hi[:outputs], dft_lo[:outputs]
        out = lax.dot_general(hi, a, contract, preferred_element_type=f32)
        out = out + lax.dot_general(hi, b, contract, preferred_element_type=f32)
        return out + lax.dot_general(lo, a, contract, preferred_element_type=f32)

    lane = lax.broadcasted_iota(jnp.int32, (1, flag.shape[1]), 1)
    mine = pltpu.roll(flag[...].astype(f32), lax.rem(2 * flag.shape[1] - begin, flag.shape[1]), 1)
    keep = mine
    for f in range(1, frames):
        keep = jnp.where(lane >= f * rows, pltpu.roll(mine, f * rows, 1), keep)
    keep = keep[:, :total]

    def put(c, re, im):
        spec[c, :, :total] = (re * keep).astype(bf16)
        spec[c, :, total:] = (im * keep).astype(bf16)

    def pair(c, carry):
        got = three(2 * c - 1, 2, 2 * PT)
        re, im = got[:, :total], got[:, total:]
        put(c, re[:HALF] - im[HALF:PT], re[HALF:PT] + im[:HALF])
        o = PT + HALF
        put(RAD - c, re[PT:o] - im[o:], -(re[o:] + im[PT:o]))
        return carry

    got = three(0, 1, PT)
    put(0, got[:HALF], got[HALF:])
    got = three(RAD - 1, 2, PT)
    re, im = got[:, :total], got[:, total:]
    put(RAD // 2, re[:HALF] - im[HALF:], re[HALF:] + im[:HALF])
    lax.fori_loop(1, RAD // 2, pair, 0, unroll=True)
    loads[2].wait()
    at = 0
    right = spec[...].reshape(CH, 2 * total)
    owners = pieces // len(sizes)
    copies = []
    for h, size in enumerate(sizes):
        batch = BATCH
        some = [
            pltpu.make_async_copy(
                ready.at[pl.ds(at + d * size, size)], outs[h * owners + d], out_sems.at[h * owners + d]
            )
            for d in range(owners)
        ]

        def piece(i, carry, at=at, size=size, batch=batch, some=some):
            rows_of = pl.ds(pl.multiple_of(at + i * (batch * size), size), batch * size)
            ready[rows_of, :] = jnp.dot(select[rows_of, :], right, preferred_element_type=f32).astype(bf16)
            for d, copy in enumerate(some):

                @pl.when(d // batch == i)
                def _(copy=copy):
                    copy.start()

            return carry

        lax.fori_loop(0, owners // batch, piece, 0)
        copies += some
        at += owners * size
    for copy in copies:
        copy.wait()


def filterbank(chan, volts, blocks, fir, flag, select, owners, sizes, offset, share):
    frames, rows = len(blocks) + 1, blocks[0].shape[0]
    total = frames * rows
    hbm = pl.BlockSpec(memory_space=pltpu.HBM)
    high, low, twiddle = (jnp.asarray(t) for t in tables())
    outs = [jax.ShapeDtypeStruct((size, 2 * total), bf16) for size in sizes for _ in range(owners)]
    got = pl.pallas_call(
        functools.partial(filterbank_kernel, frames, rows, offset, share, sizes),
        out_shape=outs,
        in_specs=[pl.BlockSpec(memory_space=pltpu.SMEM)] + [hbm] * (frames + 6),
        out_specs=[hbm] * len(outs),
        scratch_shapes=[
            pltpu.VMEM((frames, rows, FL), bf16),
            pltpu.VMEM(fir.shape, f32),
            pltpu.VMEM(flag.shape, flag.dtype),
            pltpu.VMEM(twiddle.shape, f32),
            pltpu.VMEM(high.shape, bf16),
            pltpu.VMEM(low.shape, bf16),
            pltpu.VMEM(select.shape, bf16),
            pltpu.VMEM((RAD + 1, total, PT), bf16),
            pltpu.VMEM((RAD + 1, total, PT), bf16),
            pltpu.VMEM((RAD, HALF, 2 * total), bf16),
            pltpu.VMEM((CH, 2 * total), bf16),
            pltpu.SemaphoreType.DMA((frames + 3,)),
            pltpu.SemaphoreType.DMA((3,)),
            pltpu.SemaphoreType.DMA((len(outs),)),
        ],
        compiler_params=pltpu.CompilerParams(vmem_limit_bytes=56 << 20),
        name="filterbank",
    )(chan, volts, *blocks, fir, flag, twiddle, high, low, select)
    return [got[h * owners : (h + 1) * owners] for h in range(len(sizes))]


def order_kernel(pieces, *refs):
    place, out, turned = refs[pieces:]
    half = refs[0].shape[1] // 2
    slots = refs[0].shape[0]
    parts = []
    for part in range(2):
        rows = jnp.concatenate([refs[d][:, part * half : (part + 1) * half] for d in range(pieces)], axis=1)
        got = jnp.dot(rows, place[...], preferred_element_type=f32)
        parts.append(got.reshape(slots // COARSE, 1, COARSE, got.shape[1]))
    re, im = parts
    shape = (2 * slots, re.shape[3])
    out[...] = jnp.concatenate([re, im], axis=1).reshape(shape).astype(bf16)
    turned[...] = jnp.concatenate([im, -re], axis=1).reshape(shape).astype(bf16)


def order(blocks, place):
    slots = blocks[0].shape[0]
    vmem = pl.BlockSpec(memory_space=pltpu.VMEM)
    shape = jax.ShapeDtypeStruct((2 * slots, place.shape[1]), bf16)
    return pl.pallas_call(
        functools.partial(order_kernel, len(blocks)),
        out_shape=[shape, shape],
        in_specs=[vmem] * (len(blocks) + 1),
        out_specs=[vmem] * 2,
        compiler_params=pltpu.CompilerParams(vmem_limit_bytes=16 << 20),
        name="order",
    )(*blocks, place)


def gram_kernel(frames, start, scale, pol_ref, own, turned, other, *refs):
    out, ring, sems = refs[-3:]
    stations = own.shape[1] // frames
    tiles = stations // LANES
    first = pol_ref[0] == 0
    turns = (((0,), (0,)), ((), ()))
    count = own.shape[0] // (2 * COARSE)
    depth = ring.shape[0]

    def copies(j):
        slot = lax.rem(j, depth)
        return [
            pltpu.make_async_copy(ring.at[slot, part], out.at[part, start + j], sems.at[slot, part])
            for part in range(2)
        ]

    def one(j, carry):
        slot = lax.rem(j, depth)

        @pl.when(j >= depth)
        def _():
            for copy in copies(j - depth):
                copy.wait()

        def stack(ref):
            rows = pl.ds(pl.multiple_of(2 * COARSE * j, 2 * COARSE), 2 * COARSE)
            return jnp.concatenate([ref[rows, f * stations : (f + 1) * stations] for f in range(frames)], axis=0)

        mine, mine_turned, theirs = stack(own), stack(turned), stack(other)
        right = jnp.concatenate([jnp.where(first, mine, theirs), jnp.where(first, theirs, mine)], axis=1)
        for part, left in enumerate((mine, mine_turned)):
            got = lax.dot_general(left, right, turns, preferred_element_type=f32) * scale
            for q in range(2):
                for t in range(tiles):
                    at = q * stations + t * LANES
                    ring[slot, part, pl.ds(2 * t + q, stations, stride=2 * tiles), :] = got[:, at : at + LANES]
        for copy in copies(j):
            copy.start()
        return carry

    lax.fori_loop(0, count, one, 0)
    for j in range(count - depth, count):
        for copy in copies(j):
            copy.wait()


def gram(pol, own, turned, other, frames, coarse, start, into):
    count = own.shape[0] // (2 * COARSE)
    stations = own.shape[1] // frames
    rows = stations * 2 * (stations // LANES)
    depth = min(4, count)
    vmem, hbm = pl.BlockSpec(memory_space=pltpu.VMEM), pl.BlockSpec(memory_space=pltpu.HBM)
    more = [] if into is None else [into]
    return pl.pallas_call(
        functools.partial(gram_kernel, frames, start, 1.0 / (frames * COARSE)),
        out_shape=jax.ShapeDtypeStruct((2, coarse, rows, LANES), f32),
        in_specs=[pl.BlockSpec(memory_space=pltpu.SMEM), vmem, vmem, vmem] + [hbm] * len(more),
        out_specs=hbm,
        scratch_shapes=[pltpu.VMEM((depth, 2, rows, LANES), f32), pltpu.SemaphoreType.DMA((depth, 2))],
        input_output_aliases={4: 0} if more else {},
        compiler_params=pltpu.CompilerParams(vmem_limit_bytes=16 << 20),
        name="gram",
    )(pol, own, turned, other, *more)


def rolled(array, axis, start, size):
    return lax.dynamic_slice_in_dim(jnp.concatenate([array, array], axis=axis), start, size, axis=axis)


def groups_of(rows):
    return [(0, rows)]


def fast_body(voltages, fir_coeffs, flags, station_slot, chan_map):
    chans, stns = lax.axis_size("chan"), lax.axis_size("stn")
    chan, stn, pol = lax.axis_index("chan"), lax.axis_index("stn"), lax.axis_index("pol")
    here = voltages.shape[1]
    stations = station_slot.shape[0]
    frames = chans
    rows = here // chans
    owners = chans * stns
    slots = CH // owners
    coarse = slots // COARSE
    groups = groups_of(rows)
    shares = voltages.reshape(chans, rows, FL)
    blocks = []
    for offset, size in groups:
        blocks.append([])
        for d in range(1, chans):
            share = lax.dynamic_index_in_dim(shares[:, offset : offset + size], (chan + d) % chans, 0, keepdims=False)
            blocks[-1].append(lax.ppermute(share, "chan", [(i, (i + d) % chans) for i in range(chans)]))
    lane_of = (chan_map % RAD) * HALF + chan_map // RAD
    lane_of = rolled(rolled(lane_of.reshape(chans, stns, slots), 0, chan, chans), 1, stn, stns)
    select = onehot(lane_of.reshape(CH), jnp.arange(CH, dtype=jnp.int32))
    got = []
    place = []
    dist = jnp.arange(owners, dtype=jnp.int32)
    row0 = (stn - dist % stns) % stns * here + (chan - dist // stns) % chans * rows
    col = station_slot[None, :] + stations * jnp.arange(frames, dtype=jnp.int32)[:, None]
    for (offset, size), block in zip(groups, blocks, strict=True):
        [pieces] = filterbank(
            chan.reshape(1), voltages, block, fir_coeffs, flags, select, owners, [slots], offset, rows
        )
        got.append(pieces[0])
        for d in range(1, owners):
            dc, ds = divmod(d, stns)
            route = [
                (i * stns + j, (i + dc) % chans * stns + (j + ds) % stns) for i in range(chans) for j in range(stns)
            ]
            got.append(lax.ppermute(pieces[d], ("chan", "stn"), route))
        row = row0[:, None, None] + offset + jnp.arange(size, dtype=jnp.int32)[None, None, :]
        row = row + stations * jnp.arange(frames, dtype=jnp.int32)[None, :, None]
        place.append(row.reshape(-1))
    place = onehot(jnp.concatenate(place), col.reshape(-1))
    own, turned = order(got, place)
    other = lax.ppermute(own, "pol", [(0, 1), (1, 0)])
    out = gram(pol.reshape(1), own, turned, other, frames, coarse, 0, None)
    tiles = stations // LANES
    out = out.reshape(2, -1, stations, tiles, 2, LANES).transpose(0, 1, 2, 4, 3, 5)
    return out.reshape(2, -1, 1, stations, 2, stations)


def general_body(voltages, fir_coeffs, flags, station_slot, chan_map):
    high = lax.Precision.HIGHEST
    here = voltages.shape[1]
    chans, stns = lax.axis_size("chan"), lax.axis_size("stn")
    frames_here = voltages.shape[2] // FL
    frames = voltages.reshape(here, frames_here, FL)
    history = []
    for distance in range(1, (TAPS - 1 + frames_here - 1) // frames_here + 1):
        route = [(i - distance, i) for i in range(distance, chans)]
        history = [lax.ppermute(frames, "chan", route)] + history
    window = jnp.concatenate(history + [frames], axis=1)
    window = window[:, window.shape[1] - frames_here - TAPS + 1 :]
    filtered = jnp.zeros((here, frames_here, FL), f32)
    for tap in range(TAPS):
        filtered = filtered + fir_coeffs[tap][None, None, :] * window[:, tap : tap + frames_here, :].astype(f32)
    side = math.isqrt(FL)

    def angles(rows, cols, period):
        product = jnp.arange(rows, dtype=jnp.int32)[:, None] * jnp.arange(cols, dtype=jnp.int32)[None, :]
        phase = (product % period).astype(f32) * (2.0 * math.pi / period)
        return jnp.cos(phase), jnp.sin(phase)

    grid = filtered.reshape(here, frames_here, side, side)
    cos, sin = angles(side, side, side)
    re = jnp.einsum("sfqp,qc->sfpc", grid, cos, precision=high)
    im = -jnp.einsum("sfqp,qc->sfpc", grid, sin, precision=high)
    cos, sin = angles(side, side, FL)
    re, im = re * cos + im * sin, im * cos - re * sin
    cos, sin = angles(side, side // 2, side)
    form = "sfpc,pk->kcfs"
    out_re = jnp.einsum(form, re, cos, precision=high) + jnp.einsum(form, im, sin, precision=high)
    out_im = jnp.einsum(form, im, cos, precision=high) - jnp.einsum(form, re, sin, precision=high)
    weight = jnp.tile(flags[0].astype(f32), frames_here) * FL**-0.5
    shape = (CH, 1, frames_here * here)
    spectra = jnp.concatenate(
        [(out_re.reshape(shape) * weight).astype(bf16), (out_im.reshape(shape) * weight).astype(bf16)], axis=1
    )
    select = onehot(chan_map, jnp.arange(CH, dtype=jnp.int32))
    spectra = jnp.einsum("sc,cpn->spn", select, spectra, preferred_element_type=f32).astype(bf16)
    pieces = lax.all_to_all(spectra, ("chan", "stn"), split_axis=0, concat_axis=2, tiled=True)
    pieces = pieces.reshape(-1, 2, chans, stns, frames_here, here).transpose(0, 1, 3, 5, 2, 4)
    total = chans * frames_here
    pieces = pieces.reshape(-1, COARSE, 2, stns * here, total)
    place = onehot(station_slot, jnp.arange(stns * here, dtype=jnp.int32))
    own = jnp.einsum("ar,jkprf->jkpaf", place, pieces, preferred_element_type=f32).astype(bf16)
    both = lax.all_gather(own[None], "pol", axis=0, tiled=True)
    form = "jkrf,qjksf->jrqs"

    def dot(left, right):
        return jnp.einsum(form, left, right, preferred_element_type=f32)

    own_re, own_im, re, im = own[:, :, 0], own[:, :, 1], both[:, :, :, 0], both[:, :, :, 1]
    block = jnp.stack([dot(own_re, re) + dot(own_im, im), dot(own_im, re) - dot(own_re, im)], axis=0)
    return (block * (1.0 / (total * COARSE)))[:, :, None]


def body(voltages, fir_coeffs, flags, station_slot, chan_map):
    chans, stns = lax.axis_size("chan"), lax.axis_size("stn")
    here, stations = voltages.shape[1], station_slot.shape[0]
    fits = (
        voltages.shape[2] == FL
        and chans <= TAPS
        and here % chans == 0
        and here // chans % 16 == 0
        and here == LANES
        and stations % LANES == 0
        and CH // (chans * stns) % 16 == 0
    )
    return (fast_body if fits else general_body)(voltages, fir_coeffs, flags, station_slot, chan_map)


def solution(mesh):
    in_specs = (P(("grp", "pol"), "stn", "chan"), P(), P(("grp", "pol"), "stn"), P(), P())
    out_specs = P("grp", ("chan", "stn"), "pol", None, None, None)
    return jax.shard_map(body, mesh=mesh, in_specs=in_specs, out_specs=out_specs, check_vma=False)
```

time: 87.1 us -> 79.9 us (0.917)
  Pallas kernels: 25.4 us -> 21.1 us
  local copies, waits for them, and re-layouts: 5.58 us -> 2.89 us
    pallas_call x2, Pallas kernels: 24.2 us -> 19.8 us  [the longest x1 11.4 us: gram(): pl.pallas_call(functools.partial(gram_kernel, frames, start, 1.0 / (frame...]
    unnamed x24 -> x12, local copies, waits for them, and re-layouts: 3.3 us -> 1.62 us
    squeeze x1, local copies, waits for them, and re-layouts: 2.11 us -> 1.17 us  [fast_body(): lax.dynamic_index_in_dim(shares[:, offset:offset + size], (chan + d) % ch...]
  transfers between devices with their start and end apart: 11 -> 11, of which waited for: 7 -> 7; matrix products, arithmetic and copies ran while one was open for 7% -> 8% of each run, Pallas kernels for 0% -> 0%
where the time goes in v2:
time: 79.9 us; the launch traced here: 79.7 us
  waiting for transfers between devices  34.9 us (44%)
  Pallas kernels  21.1 us (26%)
  starting transfers between devices  14.5 us (18%)
  other arithmetic  6.21 us (8%)
  local copies, waits for them, and re-layouts  2.89 us (4%)
    ppermute x7, waiting for transfers between devices, fast_body(): got.append(lax.ppermute(pieces[d], ('chan', 'stn'), route))  18.5 us
    ppermute x3, waiting for transfers between devices, fast_body(): lax.ppermute(share, 'chan', [(i, (i + d) % chans) for i in range(chans)])  14.1 us
    pallas_call x1, Pallas kernels, gram(): pl.pallas_call(functools.partial(gram_kernel, frames, start, 1.0 / (frame...  11.4 us
    ppermute x7, starting transfers between devices, fast_body(): got.append(lax.ppermute(pieces[d], ('chan', 'stn'), route))  9.24 us
    pallas_call x1, Pallas kernels, filterbank(): pl.pallas_call(functools.partial(filterbank_kernel, frames, rows, offset,...  8.36 us
    convert_element_type x2, other arithmetic, onehot(): return (rows[:, None] == cols[None, :]).astype(bf16)  5.22 us
    ppermute x3, starting transfers between devices, fast_body(): lax.ppermute(share, 'chan', [(i, (i + d) % chans) for i in range(chans)])  4.72 us
    ppermute x1, waiting for transfers between devices, fast_body(): other = lax.ppermute(own, 'pol', [(0, 1), (1, 0)])  2.29 us
  transfers between devices with their start and end apart: 11, of which 7 were waited for; matrix products, arithmetic and copies ran while one was open for 8% of the time, Pallas kernels for 0%

profile of v2, /device:TPU:9, one launch (start us, length us, event | category | flops | bytes accessed | tf_op | source)
XLA Modules:
  0.0 79.7 jit_solution(1256421419427458667)
XLA Ops:
  0.0 0.0 copy-start.4
  0.0 1.2 %dynamic-slice_bitcast_fusion = (bf16[32,4096]{1,0:T(8,128)(2,1)S(1)}, bf16[32,4096]{1,0:T(8,128)(2,1)S(1)}, bf16[32,4096]{1,0:T(8,128)(2,1)S(1)}) fusion(bf16[4,32,4096]{2,1,0:T(8,128)(2,1)} %bitcast.20, s32[]{:T(128)S(6)} %select_n.82, s32[]{:T(128)S(6)} %select_n.80, s32[]{:T(128)S(6)} %select_n.78), kind=kLoop, calls=%fused_computation.3 | loop fusion | bytes 1572876 | tf_op jit(solution)/shard_map/jit(dynamic_index_in_dim)/squeeze | solution.py:358
  1.2 0.1 collective-permute-start.2
  1.2 2.5 %collective-permute-start.1 = (bf16[32,4096]{1,0:T(8,128)(2,1)S(1)}, bf16[32,4096]{1,0:T(8,128)(2,1)S(1)}, u32[]{:S(2)}, u32[]{:S(2)}) collective-permute-start(bf16[32,4096]{1,0:T(8,128)(2,1)S(1)} %get-tuple-element.26), channel_id=1, source_target_pairs={{0,8},{4,12},{8,0},{12,4},{1,9},{5,13},{9,1},{13,5},{2,10},{6,14},... | collective-permute-start | bytes 786440 | tf_op jit(solution)/shard_map/ppermute | solution.py:359
  3.7 2.2 %collective-permute-start = (bf16[32,4096]{1,0:T(8,128)(2,1)S(1)}, bf16[32,4096]{1,0:T(8,128)(2,1)S(1)}, u32[]{:S(2)}, u32[]{:S(2)}) collective-permute-start(bf16[32,4096]{1,0:T(8,128)(2,1)S(1)} %get-tuple-element.27), channel_id=1, source_target_pairs={{0,4},{4,8},{8,12},{12,0},{1,5},{5,9},{9,13},{13,1},{2,6},{6,10},{... | collective-permute-start | bytes 786440 | tf_op jit(solution)/shard_map/ppermute | solution.py:359
  5.9 0.7 fusion.2
  6.7 4.8 %fusion.refs_9_ = bf16[2048,2048]{1,0:T(8,128)(2,1)} fusion(s32[2048]{0:T(1024)S(1)} %bitcast.21), kind=kLoop, calls=%fused_computation.1 | loop fusion | flops 8388608 | bytes 8396800 | tf_op jit(solution)/shard_map/convert_element_type | solution.py:27
  11.5 0.0 copy-done.4
  11.5 0.1 add_bitcast_fusion
  11.6 0.1 iota_add_fusion
  11.7 0.0 collective-permute-done.2.refs_3_
  11.7 0.0 copy-start.1
  11.7 8.5 %collective-permute-done.1.refs_2_ = bf16[32,4096]{1,0:T(8,128)(2,1)S(1)} collective-permute-done((bf16[32,4096]{1,0:T(8,128)(2,1)S(1)}, bf16[32,4096]{1,0:T(8,128)(2,1)S(1)}, u32[]{:S(2)}, u32[]{:S(2)}) %collective-permute-start.1) | collective-permute-done | bytes 262176 | tf_op jit(solution)/shard_map/ppermute | solution.py:359
  20.2 0.0 copy-start.2
  20.2 5.6 %collective-permute-done.refs_1_ = bf16[32,4096]{1,0:T(8,128)(2,1)S(1)} collective-permute-done((bf16[32,4096]{1,0:T(8,128)(2,1)S(1)}, bf16[32,4096]{1,0:T(8,128)(2,1)S(1)}, u32[]{:S(2)}, u32[]{:S(2)}) %collective-permute-start) | collective-permute-done | bytes 262176 | tf_op jit(solution)/shard_map/ppermute | solution.py:359
  25.8 0.0 copy-start.3
  25.9 0.0 copy-done.1
  25.9 0.0 copy-done.2
  25.9 0.7 copy-done.3
  26.6 8.4 %filterbank.1 = (bf16[256,256]{1,0:T(8,128)(2,1)}, bf16[256,256]{1,0:T(8,128)(2,1)}, bf16[256,256]{1,0:T(8,128)(2,1)}, bf16[256,256]{1,0:T(8,128)(2,1)}, bf16[25...) custom-call(s32[1]{0:T(128)} %bitcast.1.chan_ref, ...), custom_call_target="tpu_custom_call" | custom-call | tf_op jit(solution)/shard_map/filterbank/pallas_call | solution.py:213
  34.9 1.3 %collective-permute-start.3 = (bf16[256,256]{1,0:T(8,128)(2,1)}, bf16[256,256]{1,0:T(8,128)(2,1)S(1)}, u32[]{:S(2)}, u32[]{:S(2)}) collective-permute-start(bf16[256,256]{1,0:T(8,128)(2,1)} %get-tuple-element.16), channel_id=1, source_target_pairs={{0,2},{2,0},{4,6},{6,4},{8,10},{10,8},{12,14},{14,12},{1,3},{3,1},... | collective-permute-start | bytes 393224 | tf_op jit(solution)/shard_map/ppermute | solution.py:378
  36.2 2.2 %collective-permute-start.4 = (bf16[256,256]{1,0:T(8,128)(2,1)}, bf16[256,256]{1,0:T(8,128)(2,1)S(1)}, u32[]{:S(2)}, u32[]{:S(2)}) collective-permute-start(bf16[256,256]{1,0:T(8,128)(2,1)} %get-tuple-element.17), channel_id=1, source_target_pairs={{0,4},{2,6},{4,8},{6,10},{8,12},{10,14},{12,0},{14,2},{1,5},{3,7},... | collective-permute-start | bytes 393224 | tf_op jit(solution)/shard_map/ppermute | solution.py:378
  38.4 0.1 broadcast_add_fusion
  38.5 0.1 add.164
  38.6 0.0 collective-permute-start.5
  38.6 1.3 %collective-permute-start.6 = (bf16[256,256]{1,0:T(8,128)(2,1)}, bf16[256,256]{1,0:T(8,128)(2,1)S(1)}, u32[]{:S(2)}, u32[]{:S(2)}) collective-permute-start(bf16[256,256]{1,0:T(8,128)(2,1)} %get-tuple-element.19), channel_id=1, source_target_pairs={{0,8},{2,10},{4,12},{6,14},{8,0},{10,2},{12,4},{14,6},{1,9},{3,11}... | collective-permute-start | bytes 393224 | tf_op jit(solution)/shard_map/ppermute | solution.py:378
  39.9 1.9 %collective-permute-start.7 = (bf16[256,256]{1,0:T(8,128)(2,1)}, bf16[256,256]{1,0:T(8,128)(2,1)S(1)}, u32[]{:S(2)}, u32[]{:S(2)}) collective-permute-start(bf16[256,256]{1,0:T(8,128)(2,1)} %get-tuple-element.20), channel_id=1, source_target_pairs={{0,10},{2,8},{4,14},{6,12},{8,2},{10,0},{12,6},{14,4},{1,11},{3,9}... | collective-permute-start | bytes 393224 | tf_op jit(solution)/shard_map/ppermute | solution.py:378
  41.8 0.0 collective-permute-done.3.refs_1_
  41.8 1.5 %collective-permute-start.8 = (bf16[256,256]{1,0:T(8,128)(2,1)}, bf16[256,256]{1,0:T(8,128)(2,1)S(1)}, u32[]{:S(2)}, u32[]{:S(2)}) collective-permute-start(bf16[256,256]{1,0:T(8,128)(2,1)} %get-tuple-element.21), channel_id=1, source_target_pairs={{0,12},{2,14},{4,0},{6,2},{8,4},{10,6},{12,8},{14,10},{1,13},{3,15... | collective-permute-start | bytes 393224 | tf_op jit(solution)/shard_map/ppermute | solution.py:378
  43.3 0.0 collective-permute-done.4.refs_2_
  43.3 1.0 %collective-permute-start.9 = (bf16[256,256]{1,0:T(8,128)(2,1)}, bf16[256,256]{1,0:T(8,128)(2,1)S(1)}, u32[]{:S(2)}, u32[]{:S(2)}) collective-permute-start(bf16[256,256]{1,0:T(8,128)(2,1)} %get-tuple-element.22), channel_id=1, source_target_pairs={{0,14},{2,12},{4,2},{6,0},{8,6},{10,4},{12,10},{14,8},{1,15},{3,13... | collective-permute-start | bytes 393224 | tf_op jit(solution)/shard_map/ppermute | solution.py:378
  44.3 0.4 compare_convert_fusion.refs_8_
  44.7 0.0 collective-permute-done.5.refs_3_
  44.8 12.0 %collective-permute-done.6.refs_4_ = bf16[256,256]{1,0:T(8,128)(2,1)S(1)} collective-permute-done((bf16[256,256]{1,0:T(8,128)(2,1)}, bf16[256,256]{1,0:T(8,128)(2,1)S(1)}, u32[]{:S(2)}, u32[]{:S(2)}) %collective-permute-start.6) | collective-permute-done | bytes 131104 | tf_op jit(solution)/shard_map/ppermute | solution.py:378
  56.8 2.8 %collective-permute-done.7.refs_5_ = bf16[256,256]{1,0:T(8,128)(2,1)S(1)} collective-permute-done((bf16[256,256]{1,0:T(8,128)(2,1)}, bf16[256,256]{1,0:T(8,128)(2,1)S(1)}, u32[]{:S(2)}, u32[]{:S(2)}) %collective-permute-start.7) | collective-permute-done | bytes 131104 | tf_op jit(solution)/shard_map/ppermute | solution.py:378
  59.6 0.4 collective-permute-done.8.refs_6_
  60.0 3.2 %collective-permute-done.9.refs_7_ = bf16[256,256]{1,0:T(8,128)(2,1)S(1)} collective-permute-done((bf16[256,256]{1,0:T(8,128)(2,1)}, bf16[256,256]{1,0:T(8,128)(2,1)S(1)}, u32[]{:S(2)}, u32[]{:S(2)}) %collective-permute-start.9) | collective-permute-done | bytes 131104 | tf_op jit(solution)/shard_map/ppermute | solution.py:378
  63.3 0.0 copy-start
  63.3 0.9 %copy-done = bf16[256,256]{1,0:T(8,128)(2,1)S(1)} copy-done((bf16[256,256]{1,0:T(8,128)(2,1)S(1)}, bf16[256,256]{1,0:T(8,128)(2,1)}, u32[]{:S(2)}) %copy-start) | copy-done | bytes 131096
  64.2 1.3 %order.1 = (bf16[512,1024]{1,0:T(8,128)(2,1)S(1)}, bf16[512,1024]{1,0:T(8,128)(2,1)S(1)}) custom-call(bf16[256,256]{1,0:T(8,128)(2,1)S(1)} %copy-done, bf16[256,256]{1,0:T(8,128)(2,1)S(1)} %collective-permute-done.3.refs_1_, bf16[256,256]{1,0:T(8,128)(2,1)S(1)} %collective-permute-done.4.refs_2_, bf16[256,256]{1,0:T(8,128)(2,1)S(1)} %collective-permute-done.5.refs_3_, ...), custom_call_target="tpu_custom_call" | custom-call | tf_op jit(solution)/shard_map/order/pallas_call | solution.py:259
  65.4 0.6 collective-permute-start.10
  66.0 2.3 %collective-permute-done.10.other = bf16[512,1024]{1,0:T(8,128)(2,1)S(1)} collective-permute-done((bf16[512,1024]{1,0:T(8,128)(2,1)S(1)}, bf16[512,1024]{1,0:T(8,128)(2,1)S(1)}, u32[]{:S(2)}, u32[]{:S(2)}) %collective-permute-start.10) | collective-permute-done | bytes 1048608 | tf_op jit(solution)/shard_map/ppermute | solution.py:384
  68.3 11.4 %gram.1 = f32[2,32,1024,128]{3,2,1,0:T(8,128)} custom-call(s32[1]{0:T(128)} %bitcast.pol_ref, bf16[512,1024]{1,0:T(8,128)(2,1)S(1)} %get-tuple-element.23.own, bf16[512,1024]{1,0:T(8,128)(2,1)S(1)} %get-tuple-element.24.turned, bf16[512,1024]{1,0:T(8,128)(2,1)S(1)} %collective-permute-done.10.other), custom_call_target="tpu_custom_call" | custom-call | tf_op jit(solution)/shard_map/gram/pallas_call | solution.py:322
  (7 shorter events, 0.1 us)
Async XLA Ops:
  0.0 11.5 %copy-start.4 = (s32[256]{0:T(256)S(1)}, s32[256]{0:T(256)}, u32[]{:S(2)}) copy-start(s32[256]{0:T(256)} %param.11) | copy-start | bytes 3076
  1.2 10.5 %collective-permute-start.2 = (bf16[32,4096]{1,0:T(8,128)(2,1)S(1)}, bf16[32,4096]{1,0:T(8,128)(2,1)S(1)}, u32[]{:S(2)}, u32[]{:S(2)}) collective-permute-start(bf16[32,4096]{1,0:T(8,128)(2,1)S(1)} %get-tuple-element.25), channel_id=1, source_target_pairs={{0,12},{4,0},{8,4},{12,8},{1,13},{5,1},{9,5},{13,9},{2,14},{6,2},{... | collective-permute-start | bytes 786440 | tf_op jit(solution)/shard_map/ppermute | solution.py:359
  1.2 19.0 %collective-permute-start.1 = (bf16[32,4096]{1,0:T(8,128)(2,1)S(1)}, bf16[32,4096]{1,0:T(8,128)(2,1)S(1)}, u32[]{:S(2)}, u32[]{:S(2)}) collective-permute-start(bf16[32,4096]{1,0:T(8,128)(2,1)S(1)} %get-tuple-element.26), channel_id=1, source_target_pairs={{0,8},{4,12},{8,0},{12,4},{1,9},{5,13},{9,1},{13,5},{2,10},{6,14},... | collective-permute-start | bytes 786440 | tf_op jit(solution)/shard_map/ppermute | solution.py:359
  3.7 22.1 %collective-permute-start = (bf16[32,4096]{1,0:T(8,128)(2,1)S(1)}, bf16[32,4096]{1,0:T(8,128)(2,1)S(1)}, u32[]{:S(2)}, u32[]{:S(2)}) collective-permute-start(bf16[32,4096]{1,0:T(8,128)(2,1)S(1)} %get-tuple-element.27), channel_id=1, source_target_pairs={{0,4},{4,8},{8,12},{12,0},{1,5},{5,9},{9,13},{13,1},{2,6},{6,10},{... | collective-permute-start | bytes 786440 | tf_op jit(solution)/shard_map/ppermute | solution.py:359
  11.7 14.2 %copy-start.1 = (bf16[32,4096]{1,0:T(8,128)(2,1)}, bf16[32,4096]{1,0:T(8,128)(2,1)S(1)}, u32[]{:S(2)}) copy-start(bf16[32,4096]{1,0:T(8,128)(2,1)S(1)} %collective-permute-done.2.refs_3_) | copy-start | bytes 786436
  20.2 5.6 %copy-start.2 = (bf16[32,4096]{1,0:T(8,128)(2,1)}, bf16[32,4096]{1,0:T(8,128)(2,1)S(1)}, u32[]{:S(2)}) copy-start(bf16[32,4096]{1,0:T(8,128)(2,1)S(1)} %collective-permute-done.1.refs_2_) | copy-start | bytes 786436
  25.8 0.7 copy-start.3
  34.9 6.9 %collective-permute-start.3 = (bf16[256,256]{1,0:T(8,128)(2,1)}, bf16[256,256]{1,0:T(8,128)(2,1)S(1)}, u32[]{:S(2)}, u32[]{:S(2)}) collective-permute-start(bf16[256,256]{1,0:T(8,128)(2,1)} %get-tuple-element.16), channel_id=1, source_target_pairs={{0,2},{2,0},{4,6},{6,4},{8,10},{10,8},{12,14},{14,12},{1,3},{3,1},... | collective-permute-start | bytes 393224 | tf_op jit(solution)/shard_map/ppermute | solution.py:378
  36.2 7.1 %collective-permute-start.4 = (bf16[256,256]{1,0:T(8,128)(2,1)}, bf16[256,256]{1,0:T(8,128)(2,1)S(1)}, u32[]{:S(2)}, u32[]{:S(2)}) collective-permute-start(bf16[256,256]{1,0:T(8,128)(2,1)} %get-tuple-element.17), channel_id=1, source_target_pairs={{0,4},{2,6},{4,8},{6,10},{8,12},{10,14},{12,0},{14,2},{1,5},{3,7},... | collective-permute-start | bytes 393224 | tf_op jit(solution)/shard_map/ppermute | solution.py:378
  38.6 6.2 %collective-permute-start.5 = (bf16[256,256]{1,0:T(8,128)(2,1)}, bf16[256,256]{1,0:T(8,128)(2,1)S(1)}, u32[]{:S(2)}, u32[]{:S(2)}) collective-permute-start(bf16[256,256]{1,0:T(8,128)(2,1)} %get-tuple-element.18), channel_id=1, source_target_pairs={{0,6},{2,4},{4,10},{6,8},{8,14},{10,12},{12,2},{14,0},{1,7},{3,5},... | collective-permute-start | bytes 393224 | tf_op jit(solution)/shard_map/ppermute | solution.py:378
  38.6 18.2 %collective-permute-start.6 = (bf16[256,256]{1,0:T(8,128)(2,1)}, bf16[256,256]{1,0:T(8,128)(2,1)S(1)}, u32[]{:S(2)}, u32[]{:S(2)}) collective-permute-start(bf16[256,256]{1,0:T(8,128)(2,1)} %get-tuple-element.19), channel_id=1, source_target_pairs={{0,8},{2,10},{4,12},{6,14},{8,0},{10,2},{12,4},{14,6},{1,9},{3,11}... | collective-permute-start | bytes 393224 | tf_op jit(solution)/shard_map/ppermute | solution.py:378
  39.9 19.7 %collective-permute-start.7 = (bf16[256,256]{1,0:T(8,128)(2,1)}, bf16[256,256]{1,0:T(8,128)(2,1)S(1)}, u32[]{:S(2)}, u32[]{:S(2)}) collective-permute-start(bf16[256,256]{1,0:T(8,128)(2,1)} %get-tuple-element.20), channel_id=1, source_target_pairs={{0,10},{2,8},{4,14},{6,12},{8,2},{10,0},{12,6},{14,4},{1,11},{3,9}... | collective-permute-start | bytes 393224 | tf_op jit(solution)/shard_map/ppermute | solution.py:378
  41.8 18.2 %collective-permute-start.8 = (bf16[256,256]{1,0:T(8,128)(2,1)}, bf16[256,256]{1,0:T(8,128)(2,1)S(1)}, u32[]{:S(2)}, u32[]{:S(2)}) collective-permute-start(bf16[256,256]{1,0:T(8,128)(2,1)} %get-tuple-element.21), channel_id=1, source_target_pairs={{0,12},{2,14},{4,0},{6,2},{8,4},{10,6},{12,8},{14,10},{1,13},{3,15... | collective-permute-start | bytes 393224 | tf_op jit(solution)/shard_map/ppermute | solution.py:378
  43.3 20.0 %collective-permute-start.9 = (bf16[256,256]{1,0:T(8,128)(2,1)}, bf16[256,256]{1,0:T(8,128)(2,1)S(1)}, u32[]{:S(2)}, u32[]{:S(2)}) collective-permute-start(bf16[256,256]{1,0:T(8,128)(2,1)} %get-tuple-element.22), channel_id=1, source_target_pairs={{0,14},{2,12},{4,2},{6,0},{8,6},{10,4},{12,10},{14,8},{1,15},{3,13... | collective-permute-start | bytes 393224 | tf_op jit(solution)/shard_map/ppermute | solution.py:378
  63.3 0.9 %copy-start = (bf16[256,256]{1,0:T(8,128)(2,1)S(1)}, bf16[256,256]{1,0:T(8,128)(2,1)}, u32[]{:S(2)}) copy-start(bf16[256,256]{1,0:T(8,128)(2,1)} %get-tuple-element.15.refs_0_) | copy-start | bytes 393220
  65.4 2.8 %collective-permute-start.10 = (bf16[512,1024]{1,0:T(8,128)(2,1)S(1)}, bf16[512,1024]{1,0:T(8,128)(2,1)S(1)}, u32[]{:S(2)}, u32[]{:S(2)}) collective-permute-start(bf16[512,1024]{1,0:T(8,128)(2,1)S(1)} %get-tuple-element.23.own), channel_id=1, source_target_pairs={{0,1},{1,0},{2,3},{3,2},{4,5},{5,4},{6,7},{7,6},{8,9},{9,8},{10,11... | collective-permute-start | bytes 3145736 | tf_op jit(solution)/shard_map/ppermute | solution.py:384

commit v3 on v2

--- a/solution.py
+++ b/solution.py
@@ -78,31 +78,19 @@
     return high, (value - high.astype(f32)).astype(bf16)
 
 
-def filterbank_kernel(frames, rows, offset, share, sizes, chan_ref, *refs):
+def filterbank_kernel(frames, rows, offset, share, chan_ref, *refs):
     volts, *blocks = refs[:frames]
-    fir_in, flag_in, twiddle_in, high_in, low_in, select_in = refs[frames : frames + 6]
-    pieces = len(refs) - frames - 6 - 14
-    outs = refs[frames + 6 : frames + 6 + pieces]
-    x, fir, flag, twiddle, dft_hi, dft_lo, select, u_hi, u_lo, spec, ready, in_sems, load_sems, out_sems = refs[
-        frames + 6 + pieces :
-    ]
+    fir, flag, twiddle, dft_hi, dft_lo, select = refs[frames : frames + 6]
+    outs = refs[frames + 6 : -5]
+    x, u_hi, u_lo, spec, sem = refs[-5:]
     total = frames * rows
     chan = chan_ref[0]
     begin = pl.multiple_of(chan * share + offset, rows)
-    first = []
-    for d in range(frames):
-        source = volts.at[0, pl.ds(begin, rows)] if d == 0 else blocks[d - 1]
-        first.append(pltpu.make_async_copy(source, x.at[lax.rem(chan + frames - d, frames)], in_sems.at[d]))
-    for n, (source, to) in enumerate(((fir_in, fir), (flag_in, flag), (twiddle_in, twiddle))):
-        first.append(pltpu.make_async_copy(source, to, in_sems.at[frames + n]))
-    loads = [
-        pltpu.make_async_copy(source, to, load_sems.at[n])
-        for n, (source, to) in enumerate(((high_in, dft_hi), (low_in, dft_lo), (select_in, select)))
-    ]
-    for copy in first + loads:
-        copy.start()
-    for copy in first:
-        copy.wait()
+    load = pltpu.make_async_copy(volts.at[0, pl.ds(begin, rows)], x.at[chan], sem)
+    load.start()
+    for d in range(1, frames):
+        x[lax.rem(chan + frames - d, frames)] = blocks[d - 1][...]
+    load.wait()
     step = 16
     halves = PT // LANES
     for f in range(frames):
@@ -135,8 +123,6 @@
             return carry
 
         lax.fori_loop(0, rows // step * halves, unit, 0)
-    for copy in loads[:2]:
-        copy.wait()
     contract = (((1,), (1,)), ((), ()))
 
     def three(at, count, outputs):
@@ -172,69 +158,34 @@
     re, im = got[:, :total], got[:, total:]
     put(RAD // 2, re[:HALF] - im[HALF:], re[HALF:] + im[:HALF])
     lax.fori_loop(1, RAD // 2, pair, 0, unroll=True)
-    loads[2].wait()
-    at = 0
     right = spec[...].reshape(CH, 2 * total)
-    owners = pieces // len(sizes)
-    copies = []
-    for h, size in enumerate(sizes):
-        batch = BATCH
-        some = [
-            pltpu.make_async_copy(
-                ready.at[pl.ds(at + d * size, size)], outs[h * owners + d], out_sems.at[h * owners + d]
-            )
-            for d in range(owners)
-        ]
-
-        def piece(i, carry, at=at, size=size, batch=batch, some=some):
-            rows_of = pl.ds(pl.multiple_of(at + i * (batch * size), size), batch * size)
-            ready[rows_of, :] = jnp.dot(select[rows_of, :], right, preferred_element_type=f32).astype(bf16)
-            for d, copy in enumerate(some):
-
-                @pl.when(d // batch == i)
-                def _(copy=copy):
-                    copy.start()
-
-            return carry
-
-        lax.fori_loop(0, owners // batch, piece, 0)
-        copies += some
-        at += owners * size
-    for copy in copies:
-        copy.wait()
-
-
-def filterbank(chan, volts, blocks, fir, flag, select, owners, sizes, offset, share):
+    size = CH // len(outs)
+    for first in range(0, len(outs), BATCH):
+        got = jnp.dot(select[first * size : (first + BATCH) * size], right, preferred_element_type=f32).astype(bf16)
+        for d in range(BATCH):
+            outs[first + d][...] = got[d * size : (d + 1) * size]
+
+
+def filterbank(chan, volts, blocks, fir, flag, select, owners, offset, share):
     frames, rows = len(blocks) + 1, blocks[0].shape[0]
     total = frames * rows
-    hbm = pl.BlockSpec(memory_space=pltpu.HBM)
+    vmem = pl.BlockSpec(memory_space=pltpu.VMEM)
     high, low, twiddle = (jnp.asarray(t) for t in tables())
-    outs = [jax.ShapeDtypeStruct((size, 2 * total), bf16) for size in sizes for _ in range(owners)]
-    got = pl.pallas_call(
-        functools.partial(filterbank_kernel, frames, rows, offset, share, sizes),
-        out_shape=outs,
-        in_specs=[pl.BlockSpec(memory_space=pltpu.SMEM)] + [hbm] * (frames + 6),
-        out_specs=[hbm] * len(outs),
+    return pl.pallas_call(
+        functools.partial(filterbank_kernel, frames, rows, offset, share),
+        out_shape=[jax.ShapeDtypeStruct((CH // owners, 2 * total), bf16)] * owners,
+        in_specs=[pl.BlockSpec(memory_space=pltpu.SMEM), pl.BlockSpec(memory_space=pl.ANY)] + [vmem] * (frames + 5),
+        out_specs=[vmem] * owners,
         scratch_shapes=[
             pltpu.VMEM((frames, rows, FL), bf16),
-            pltpu.VMEM(fir.shape, f32),
-            pltpu.VMEM(flag.shape, flag.dtype),
-            pltpu.VMEM(twiddle.shape, f32),
-            pltpu.VMEM(high.shape, bf16),
-            pltpu.VMEM(low.shape, bf16),
-            pltpu.VMEM(select.shape, bf16),
             pltpu.VMEM((RAD + 1, total, PT), bf16),
             pltpu.VMEM((RAD + 1, total, PT), bf16),
             pltpu.VMEM((RAD, HALF, 2 * total), bf16),
-            pltpu.VMEM((CH, 2 * total), bf16),
-            pltpu.SemaphoreType.DMA((frames + 3,)),
-            pltpu.SemaphoreType.DMA((3,)),
-            pltpu.SemaphoreType.DMA((len(outs),)),
+            pltpu.SemaphoreType.DMA,
         ],
-        compiler_params=pltpu.CompilerParams(vmem_limit_bytes=56 << 20),
+        compiler_params=pltpu.CompilerParams(vmem_limit_bytes=24 << 20),
         name="filterbank",
     )(chan, volts, *blocks, fir, flag, twiddle, high, low, select)
-    return [got[h * owners : (h + 1) * owners] for h in range(len(sizes))]
 
 
 def order_kernel(pieces, *refs):
@@ -366,8 +317,8 @@
     row0 = (stn - dist % stns) % stns * here + (chan - dist // stns) % chans * rows
     col = station_slot[None, :] + stations * jnp.arange(frames, dtype=jnp.int32)[:, None]
     for (offset, size), block in zip(groups, blocks, strict=True):
-        [pieces] = filterbank(
-            chan.reshape(1), voltages, block, fir_coeffs, flags, select, owners, [slots], offset, rows
+        pieces = filterbank(
+            chan.reshape(1), voltages, block, fir_coeffs, flags, select, owners, offset, rows
         )
         got.append(pieces[0])
         for d in range(1, owners):

time: 79.9 us -> 76.9 us (0.962)
  other arithmetic: 6.21 us -> 2.81 us
  waiting for transfers between devices: 34.9 us -> 38 us
  Pallas kernels: 21.1 us -> 19.1 us
    convert_element_type x2, other arithmetic: 5.22 us -> 1.82 us  [onehot(): return (rows[:, None] == cols[None, :]).astype(bf16)]
    ppermute x3, waiting for transfers between devices: 14.1 us -> 17.3 us  [fast_body(): lax.ppermute(share, 'chan', [(i, (i + d) % chans) for i in range(chans)])]
    pallas_call x1, Pallas kernels: 8.36 us -> 6.43 us  [filterbank(): pl.pallas_call(functools.partial(filterbank_kernel, frames, rows, offset,...]
    unnamed x12 -> x16, local copies, waits for them, and re-layouts: 1.62 us -> 0.04 us
    squeeze x1, local copies, waits for them, and re-layouts: 1.17 us -> 1.99 us  [fast_body(): lax.dynamic_index_in_dim(shares[:, offset:offset + size], (chan + d) % ch...]
  transfers between devices with their start and end apart: 11 -> 11, of which waited for: 7 -> 8; matrix products, arithmetic and copies ran while one was open for 8% -> 4% of each run, Pallas kernels for 0% -> 0%
where the time goes in v3:
time: 76.9 us; the launch traced here: 76.7 us
  waiting for transfers between devices  38 us (49%)
  Pallas kernels  19.1 us (25%)
  starting transfers between devices  14.5 us (19%)
  other arithmetic  2.81 us (4%)
  local copies, waits for them, and re-layouts  2.12 us (3%)
    ppermute x7, waiting for transfers between devices, fast_body(): got.append(lax.ppermute(pieces[d], ('chan', 'stn'), route))  18.4 us
    ppermute x3, waiting for transfers between devices, fast_body(): lax.ppermute(share, 'chan', [(i, (i + d) % chans) for i in range(chans)])  17.3 us
    pallas_call x1, Pallas kernels, gram(): pl.pallas_call(functools.partial(gram_kernel, frames, start, 1.0 / (frame...  11.4 us
    ppermute x7, starting transfers between devices, fast_body(): got.append(lax.ppermute(pieces[d], ('chan', 'stn'), route))  9.24 us
    pallas_call x1, Pallas kernels, filterbank(): pl.pallas_call(functools.partial(filterbank_kernel, frames, rows, offset,...  6.43 us
    ppermute x3, starting transfers between devices, fast_body(): lax.ppermute(share, 'chan', [(i, (i + d) % chans) for i in range(chans)])  4.67 us
    ppermute x1, waiting for transfers between devices, fast_body(): other = lax.ppermute(own, 'pol', [(0, 1), (1, 0)])  2.29 us
    squeeze x1, local copies, waits for them, and re-layouts, fast_body(): lax.dynamic_index_in_dim(shares[:, offset:offset + size], (chan + d) % ch...  1.99 us
  transfers between devices with their start and end apart: 11, of which 8 were waited for; matrix products, arithmetic and copies ran while one was open for 4% of the time, Pallas kernels for 0%

profile of v3, /device:TPU:9, one launch (start us, length us, event | category | flops | bytes accessed | tf_op | source)
XLA Modules:
  0.0 76.7 jit_solution(3095690852231150555)
XLA Ops:
  0.0 0.0 copy-start.4
  0.0 0.0 copy-start.2
  0.0 0.0 copy-start.3
  0.0 0.0 copy-start
  0.0 0.0 copy-start.6
  0.0 0.0 copy-start.5
  0.0 0.0 copy-start.1
  0.1 2.0 %dynamic-slice_bitcast_fusion = (bf16[32,4096]{1,0:T(8,128)(2,1)}, bf16[32,4096]{1,0:T(8,128)(2,1)S(1)}, bf16[32,4096]{1,0:T(8,128)(2,1)S(1)}) fusion(bf16[4,32,4096]{2,1,0:T(8,128)(2,1)} %bitcast.20, s32[]{:T(128)S(6)} %select_n.82, s32[]{:T(128)S(6)} %select_n.80, s32[]{:T(128)S(6)} %select_n.78), kind=kLoop, calls=%fused_computation.3 | loop fusion | bytes 1572876 | tf_op jit(solution)/shard_map/jit(dynamic_index_in_dim)/squeeze | solution.py:309
  2.1 0.0 collective-permute-start.2
  2.1 2.5 %collective-permute-start.1 = (bf16[32,4096]{1,0:T(8,128)(2,1)S(1)}, bf16[32,4096]{1,0:T(8,128)(2,1)S(1)}, u32[]{:S(2)}, u32[]{:S(2)}) collective-permute-start(bf16[32,4096]{1,0:T(8,128)(2,1)S(1)} %get-tuple-element.26), channel_id=1, source_target_pairs={{0,8},{4,12},{8,0},{12,4},{1,9},{5,13},{9,1},{13,5},{2,10},{6,14},... | collective-permute-start | bytes 786440 | tf_op jit(solution)/shard_map/ppermute | solution.py:310
  4.6 2.2 %collective-permute-start = (bf16[32,4096]{1,0:T(8,128)(2,1)S(1)}, bf16[32,4096]{1,0:T(8,128)(2,1)S(1)}, u32[]{:S(2)}, u32[]{:S(2)}) collective-permute-start(bf16[32,4096]{1,0:T(8,128)(2,1)S(1)} %get-tuple-element.27), channel_id=1, source_target_pairs={{0,4},{4,8},{8,12},{12,0},{1,5},{5,9},{9,13},{13,1},{2,6},{6,10},{... | collective-permute-start | bytes 786440 | tf_op jit(solution)/shard_map/ppermute | solution.py:310
  6.8 0.7 fusion.2
  7.6 1.4 %fusion.refs_9_ = bf16[2048,2048]{1,0:T(8,128)(2,1)S(1)} fusion(s32[2048]{0:T(1024)S(1)} %bitcast.21), kind=kLoop, calls=%fused_computation.1 | loop fusion | flops 8388608 | bytes 8396800 | tf_op jit(solution)/shard_map/convert_element_type | solution.py:27
  9.0 0.0 copy-done.6
  9.0 0.1 add_bitcast_fusion
  9.1 0.1 iota_add_fusion
  9.2 0.3 collective-permute-done.2.refs_3_
  9.5 11.4 %collective-permute-done.1.refs_2_ = bf16[32,4096]{1,0:T(8,128)(2,1)S(1)} collective-permute-done((bf16[32,4096]{1,0:T(8,128)(2,1)S(1)}, bf16[32,4096]{1,0:T(8,128)(2,1)S(1)}, u32[]{:S(2)}, u32[]{:S(2)}) %collective-permute-start.1) | collective-permute-done | bytes 262176 | tf_op jit(solution)/shard_map/ppermute | solution.py:310
  20.9 5.6 %collective-permute-done.refs_1_ = bf16[32,4096]{1,0:T(8,128)(2,1)S(1)} collective-permute-done((bf16[32,4096]{1,0:T(8,128)(2,1)S(1)}, bf16[32,4096]{1,0:T(8,128)(2,1)S(1)}, u32[]{:S(2)}, u32[]{:S(2)}) %collective-permute-start) | collective-permute-done | bytes 262176 | tf_op jit(solution)/shard_map/ppermute | solution.py:310
  26.5 0.0 copy-done.4
  26.5 0.0 copy-done.2
  26.5 0.0 copy-done.3
  26.5 0.0 copy-done
  26.5 0.0 copy-done.5
  26.5 0.0 copy-done.1
  26.5 6.4 %filterbank.1 = (bf16[256,256]{1,0:T(8,128)(2,1)S(1)}, bf16[256,256]{1,0:T(8,128)(2,1)}, bf16[256,256]{1,0:T(8,128)(2,1)}, bf16[256,256]{1,0:T(8,128)(2,1)S(1)},...) custom-call(s32[1]{0:T(128)} %bitcast.1.chan_ref, ...), custom_call_target="tpu_custom_call" | custom-call | tf_op jit(solution)/shard_map/filterbank/pallas_call | solution.py:174
  33.0 1.3 %collective-permute-start.3 = (bf16[256,256]{1,0:T(8,128)(2,1)}, bf16[256,256]{1,0:T(8,128)(2,1)S(1)}, u32[]{:S(2)}, u32[]{:S(2)}) collective-permute-start(bf16[256,256]{1,0:T(8,128)(2,1)} %get-tuple-element.16), channel_id=1, source_target_pairs={{0,2},{2,0},{4,6},{6,4},{8,10},{10,8},{12,14},{14,12},{1,3},{3,1},... | collective-permute-start | bytes 393224 | tf_op jit(solution)/shard_map/ppermute | solution.py:329
  34.2 2.2 %collective-permute-start.4 = (bf16[256,256]{1,0:T(8,128)(2,1)}, bf16[256,256]{1,0:T(8,128)(2,1)S(1)}, u32[]{:S(2)}, u32[]{:S(2)}) collective-permute-start(bf16[256,256]{1,0:T(8,128)(2,1)} %get-tuple-element.17), channel_id=1, source_target_pairs={{0,4},{2,6},{4,8},{6,10},{8,12},{10,14},{12,0},{14,2},{1,5},{3,7},... | collective-permute-start | bytes 393224 | tf_op jit(solution)/shard_map/ppermute | solution.py:329
  36.4 0.1 broadcast_add_fusion
  36.5 0.1 add.164
  36.6 0.0 collective-permute-start.5
  36.6 1.3 %collective-permute-start.6 = (bf16[256,256]{1,0:T(8,128)(2,1)S(1)}, bf16[256,256]{1,0:T(8,128)(2,1)S(1)}, u32[]{:S(2)}, u32[]{:S(2)}) collective-permute-start(bf16[256,256]{1,0:T(8,128)(2,1)S(1)} %get-tuple-element.19), channel_id=1, source_target_pairs={{0,8},{2,10},{4,12},{6,14},{8,0},{10,2},{12,4},{14,6},{1,9},{3,11}... | collective-permute-start | bytes 393224 | tf_op jit(solution)/shard_map/ppermute | solution.py:329
  37.9 2.0 %collective-permute-start.7 = (bf16[256,256]{1,0:T(8,128)(2,1)S(1)}, bf16[256,256]{1,0:T(8,128)(2,1)S(1)}, u32[]{:S(2)}, u32[]{:S(2)}) collective-permute-start(bf16[256,256]{1,0:T(8,128)(2,1)S(1)} %get-tuple-element.20), channel_id=1, source_target_pairs={{0,10},{2,8},{4,14},{6,12},{8,2},{10,0},{12,6},{14,4},{1,11},{3,9}... | collective-permute-start | bytes 393224 | tf_op jit(solution)/shard_map/ppermute | solution.py:329
  39.9 0.0 collective-permute-done.3.refs_1_
  39.9 1.5 %collective-permute-start.8 = (bf16[256,256]{1,0:T(8,128)(2,1)S(1)}, bf16[256,256]{1,0:T(8,128)(2,1)S(1)}, u32[]{:S(2)}, u32[]{:S(2)}) collective-permute-start(bf16[256,256]{1,0:T(8,128)(2,1)S(1)} %get-tuple-element.21), channel_id=1, source_target_pairs={{0,12},{2,14},{4,0},{6,2},{8,4},{10,6},{12,8},{14,10},{1,13},{3,15... | collective-permute-start | bytes 393224 | tf_op jit(solution)/shard_map/ppermute | solution.py:329
  41.3 0.0 collective-permute-done.4.refs_2_
  41.3 1.0 %collective-permute-start.9 = (bf16[256,256]{1,0:T(8,128)(2,1)S(1)}, bf16[256,256]{1,0:T(8,128)(2,1)S(1)}, u32[]{:S(2)}, u32[]{:S(2)}) collective-permute-start(bf16[256,256]{1,0:T(8,128)(2,1)S(1)} %get-tuple-element.22), channel_id=1, source_target_pairs={{0,14},{2,12},{4,2},{6,0},{8,6},{10,4},{12,10},{14,8},{1,15},{3,13... | collective-permute-start | bytes 393224 | tf_op jit(solution)/shard_map/ppermute | solution.py:329
  42.4 0.4 compare_convert_fusion.refs_8_
  42.8 0.0 collective-permute-done.5.refs_3_
  42.8 11.6 %collective-permute-done.6.refs_4_ = bf16[256,256]{1,0:T(8,128)(2,1)S(1)} collective-permute-done((bf16[256,256]{1,0:T(8,128)(2,1)S(1)}, bf16[256,256]{1,0:T(8,128)(2,1)S(1)}, u32[]{:S(2)}, u32[]{:S(2)}) %collective-permute-start.6) | collective-permute-done | bytes 131104 | tf_op jit(solution)/shard_map/ppermute | solution.py:329
  54.4 3.0 %collective-permute-done.7.refs_5_ = bf16[256,256]{1,0:T(8,128)(2,1)S(1)} collective-permute-done((bf16[256,256]{1,0:T(8,128)(2,1)S(1)}, bf16[256,256]{1,0:T(8,128)(2,1)S(1)}, u32[]{:S(2)}, u32[]{:S(2)}) %collective-permute-start.7) | collective-permute-done | bytes 131104 | tf_op jit(solution)/shard_map/ppermute | solution.py:329
  57.3 1.1 %collective-permute-done.8.refs_6_ = bf16[256,256]{1,0:T(8,128)(2,1)S(1)} collective-permute-done((bf16[256,256]{1,0:T(8,128)(2,1)S(1)}, bf16[256,256]{1,0:T(8,128)(2,1)S(1)}, u32[]{:S(2)}, u32[]{:S(2)}) %collective-permute-start.8) | collective-permute-done | bytes 131104 | tf_op jit(solution)/shard_map/ppermute | solution.py:329
  58.4 2.8 %collective-permute-done.9.refs_7_ = bf16[256,256]{1,0:T(8,128)(2,1)S(1)} collective-permute-done((bf16[256,256]{1,0:T(8,128)(2,1)S(1)}, bf16[256,256]{1,0:T(8,128)(2,1)S(1)}, u32[]{:S(2)}, u32[]{:S(2)}) %collective-permute-start.9) | collective-permute-done | bytes 131104 | tf_op jit(solution)/shard_map/ppermute | solution.py:329
  61.2 1.3 %order.1 = (bf16[512,1024]{1,0:T(8,128)(2,1)S(1)}, bf16[512,1024]{1,0:T(8,128)(2,1)S(1)}) custom-call(bf16[256,256]{1,0:T(8,128)(2,1)S(1)} %get-tuple-element.15.refs_0_, bf16[256,256]{1,0:T(8,128)(2,1)S(1)} %collective-permute-done.3.refs_1_, bf16[256,256]{1,0:T(8,128)(2,1)S(1)} %collective-permute-done.4.refs_2_, ...), custom_call_target="tpu_custom_call" | custom-call | tf_op jit(solution)/shard_map/order/pallas_call | solution.py:210
  62.5 0.6 collective-permute-start.10
  63.0 2.3 %collective-permute-done.10.other = bf16[512,1024]{1,0:T(8,128)(2,1)S(1)} collective-permute-done((bf16[512,1024]{1,0:T(8,128)(2,1)S(1)}, bf16[512,1024]{1,0:T(8,128)(2,1)S(1)}, u32[]{:S(2)}, u32[]{:S(2)}) %collective-permute-start.10) | collective-permute-done | bytes 1048608 | tf_op jit(solution)/shard_map/ppermute | solution.py:335
  65.3 11.4 %gram.1 = f32[2,32,1024,128]{3,2,1,0:T(8,128)} custom-call(s32[1]{0:T(128)} %bitcast.pol_ref, bf16[512,1024]{1,0:T(8,128)(2,1)S(1)} %get-tuple-element.23.own, bf16[512,1024]{1,0:T(8,128)(2,1)S(1)} %get-tuple-element.24.turned, bf16[512,1024]{1,0:T(8,128)(2,1)S(1)} %collective-permute-done.10.other), custom_call_target="tpu_custom_call" | custom-call | tf_op jit(solution)/shard_map/gram/pallas_call | solution.py:273
  (7 shorter events, 0.1 us)
Async XLA Ops:
  0.0 26.5 %copy-start.4 = (f32[16,256]{1,0:T(8,128)S(1)}, f32[16,256]{1,0:T(8,128)}, u32[]{:S(2)}) copy-start(f32[16,256]{1,0:T(8,128)} %constant.123.clone.refs_6_) | copy-start | bytes 49156
  0.0 26.5 %copy-start.2 = (bf16[512,256]{1,0:T(8,128)(2,1)S(1)}, bf16[512,256]{1,0:T(8,128)(2,1)}, u32[]{:S(2)}) copy-start(bf16[512,256]{1,0:T(8,128)(2,1)} %constant.122.clone.refs_8_) | copy-start | bytes 786436
  0.0 26.5 %copy-start.3 = (bf16[512,256]{1,0:T(8,128)(2,1)S(1)}, bf16[512,256]{1,0:T(8,128)(2,1)}, u32[]{:S(2)}) copy-start(bf16[512,256]{1,0:T(8,128)(2,1)} %constant.121.clone.refs_7_) | copy-start | bytes 786436
  0.0 26.5 %copy-start = (bf16[1,128,4096]{2,1,0:T(8,128)(2,1)S(1)}, bf16[1,128,4096]{2,1,0:T(8,128)(2,1)}, u32[]{:S(2)}) copy-start(bf16[1,128,4096]{2,1,0:T(8,128)(2,1)} %refs_0_.1) | copy-start | bytes 3145732
  0.0 9.0 %copy-start.6 = (s32[256]{0:T(256)S(1)}, s32[256]{0:T(256)}, u32[]{:S(2)}) copy-start(s32[256]{0:T(256)} %param.11) | copy-start | bytes 3076
  0.0 26.5 %copy-start.5 = (s32[1,128]{1,0:T(1,128)S(1)}, s32[1,128]{1,0:T(1,128)}, u32[]{:S(2)}) copy-start(s32[1,128]{1,0:T(1,128)} %refs_5_.1) | copy-start | bytes 1540
  0.0 26.5 %copy-start.1 = (f32[16,4096]{1,0:T(8,128)S(1)}, f32[16,4096]{1,0:T(8,128)}, u32[]{:S(2)}) copy-start(f32[16,4096]{1,0:T(8,128)} %refs_4_.1) | copy-start | bytes 786436
  2.1 7.4 %collective-permute-start.2 = (bf16[32,4096]{1,0:T(8,128)(2,1)}, bf16[32,4096]{1,0:T(8,128)(2,1)S(1)}, u32[]{:S(2)}, u32[]{:S(2)}) collective-permute-start(bf16[32,4096]{1,0:T(8,128)(2,1)} %get-tuple-element.25), channel_id=1, source_target_pairs={{0,12},{4,0},{8,4},{12,8},{1,13},{5,1},{9,5},{13,9},{2,14},{6,2},{... | collective-permute-start | bytes 786440 | tf_op jit(solution)/shard_map/ppermute | solution.py:310
  2.1 18.8 %collective-permute-start.1 = (bf16[32,4096]{1,0:T(8,128)(2,1)S(1)}, bf16[32,4096]{1,0:T(8,128)(2,1)S(1)}, u32[]{:S(2)}, u32[]{:S(2)}) collective-permute-start(bf16[32,4096]{1,0:T(8,128)(2,1)S(1)} %get-tuple-element.26), channel_id=1, source_target_pairs={{0,8},{4,12},{8,0},{12,4},{1,9},{5,13},{9,1},{13,5},{2,10},{6,14},... | collective-permute-start | bytes 786440 | tf_op jit(solution)/shard_map/ppermute | solution.py:310
  4.6 21.9 %collective-permute-start = (bf16[32,4096]{1,0:T(8,128)(2,1)S(1)}, bf16[32,4096]{1,0:T(8,128)(2,1)S(1)}, u32[]{:S(2)}, u32[]{:S(2)}) collective-permute-start(bf16[32,4096]{1,0:T(8,128)(2,1)S(1)} %get-tuple-element.27), channel_id=1, source_target_pairs={{0,4},{4,8},{8,12},{12,0},{1,5},{5,9},{9,13},{13,1},{2,6},{6,10},{... | collective-permute-start | bytes 786440 | tf_op jit(solution)/shard_map/ppermute | solution.py:310
  33.0 6.9 %collective-permute-start.3 = (bf16[256,256]{1,0:T(8,128)(2,1)}, bf16[256,256]{1,0:T(8,128)(2,1)S(1)}, u32[]{:S(2)}, u32[]{:S(2)}) collective-permute-start(bf16[256,256]{1,0:T(8,128)(2,1)} %get-tuple-element.16), channel_id=1, source_target_pairs={{0,2},{2,0},{4,6},{6,4},{8,10},{10,8},{12,14},{14,12},{1,3},{3,1},... | collective-permute-start | bytes 393224 | tf_op jit(solution)/shard_map/ppermute | solution.py:329
  34.2 7.1 %collective-permute-start.4 = (bf16[256,256]{1,0:T(8,128)(2,1)}, bf16[256,256]{1,0:T(8,128)(2,1)S(1)}, u32[]{:S(2)}, u32[]{:S(2)}) collective-permute-start(bf16[256,256]{1,0:T(8,128)(2,1)} %get-tuple-element.17), channel_id=1, source_target_pairs={{0,4},{2,6},{4,8},{6,10},{8,12},{10,14},{12,0},{14,2},{1,5},{3,7},... | collective-permute-start | bytes 393224 | tf_op jit(solution)/shard_map/ppermute | solution.py:329
  36.6 6.2 %collective-permute-start.5 = (bf16[256,256]{1,0:T(8,128)(2,1)S(1)}, bf16[256,256]{1,0:T(8,128)(2,1)S(1)}, u32[]{:S(2)}, u32[]{:S(2)}) collective-permute-start(bf16[256,256]{1,0:T(8,128)(2,1)S(1)} %get-tuple-element.18), channel_id=1, source_target_pairs={{0,6},{2,4},{4,10},{6,8},{8,14},{10,12},{12,2},{14,0},{1,7},{3,5},... | collective-permute-start | bytes 393224 | tf_op jit(solution)/shard_map/ppermute | solution.py:329
  36.6 17.8 %collective-permute-start.6 = (bf16[256,256]{1,0:T(8,128)(2,1)S(1)}, bf16[256,256]{1,0:T(8,128)(2,1)S(1)}, u32[]{:S(2)}, u32[]{:S(2)}) collective-permute-start(bf16[256,256]{1,0:T(8,128)(2,1)S(1)} %get-tuple-element.19), channel_id=1, source_target_pairs={{0,8},{2,10},{4,12},{6,14},{8,0},{10,2},{12,4},{14,6},{1,9},{3,11}... | collective-permute-start | bytes 393224 | tf_op jit(solution)/shard_map/ppermute | solution.py:329
  37.9 19.4 %collective-permute-start.7 = (bf16[256,256]{1,0:T(8,128)(2,1)S(1)}, bf16[256,256]{1,0:T(8,128)(2,1)S(1)}, u32[]{:S(2)}, u32[]{:S(2)}) collective-permute-start(bf16[256,256]{1,0:T(8,128)(2,1)S(1)} %get-tuple-element.20), channel_id=1, source_target_pairs={{0,10},{2,8},{4,14},{6,12},{8,2},{10,0},{12,6},{14,4},{1,11},{3,9}... | collective-permute-start | bytes 393224 | tf_op jit(solution)/shard_map/ppermute | solution.py:329
  39.9 18.5 %collective-permute-start.8 = (bf16[256,256]{1,0:T(8,128)(2,1)S(1)}, bf16[256,256]{1,0:T(8,128)(2,1)S(1)}, u32[]{:S(2)}, u32[]{:S(2)}) collective-permute-start(bf16[256,256]{1,0:T(8,128)(2,1)S(1)} %get-tuple-element.21), channel_id=1, source_target_pairs={{0,12},{2,14},{4,0},{6,2},{8,4},{10,6},{12,8},{14,10},{1,13},{3,15... | collective-permute-start | bytes 393224 | tf_op jit(solution)/shard_map/ppermute | solution.py:329
  41.3 19.8 %collective-permute-start.9 = (bf16[256,256]{1,0:T(8,128)(2,1)S(1)}, bf16[256,256]{1,0:T(8,128)(2,1)S(1)}, u32[]{:S(2)}, u32[]{:S(2)}) collective-permute-start(bf16[256,256]{1,0:T(8,128)(2,1)S(1)} %get-tuple-element.22), channel_id=1, source_target_pairs={{0,14},{2,12},{4,2},{6,0},{8,6},{10,4},{12,10},{14,8},{1,15},{3,13... | collective-permute-start | bytes 393224 | tf_op jit(solution)/shard_map/ppermute | solution.py:329
  62.5 2.8 %collective-permute-start.10 = (bf16[512,1024]{1,0:T(8,128)(2,1)S(1)}, bf16[512,1024]{1,0:T(8,128)(2,1)S(1)}, u32[]{:S(2)}, u32[]{:S(2)}) collective-permute-start(bf16[512,1024]{1,0:T(8,128)(2,1)S(1)} %get-tuple-element.23.own), channel_id=1, source_target_pairs={{0,1},{1,0},{2,3},{3,2},{4,5},{5,4},{6,7},{7,6},{8,9},{9,8},{10,11... | collective-permute-start | bytes 3145736 | tf_op jit(solution)/shard_map/ppermute | solution.py:335

commit v4 on v3

--- a/solution.py
+++ b/solution.py
@@ -80,6 +80,7 @@
 
 def filterbank_kernel(frames, rows, offset, share, chan_ref, *refs):
     volts, *blocks = refs[:frames]
+    blocks = blocks[::-1]
     fir, flag, twiddle, dft_hi, dft_lo, select = refs[frames : frames + 6]
     outs = refs[frames + 6 : -5]
     x, u_hi, u_lo, spec, sem = refs[-5:]
@@ -89,7 +90,7 @@
     load = pltpu.make_async_copy(volts.at[0, pl.ds(begin, rows)], x.at[chan], sem)
     load.start()
     for d in range(1, frames):
-        x[lax.rem(chan + frames - d, frames)] = blocks[d - 1][...]
+        x[jnp.bitwise_xor(chan, d)] = blocks[d - 1][...]
     load.wait()
     step = 16
     halves = PT // LANES
@@ -185,7 +186,7 @@
         ],
         compiler_params=pltpu.CompilerParams(vmem_limit_bytes=24 << 20),
         name="filterbank",
-    )(chan, volts, *blocks, fir, flag, twiddle, high, low, select)
+    )(chan, volts, *blocks[::-1], fir, flag, twiddle, high, low, select)
 
 
 def order_kernel(pieces, *refs):
@@ -306,8 +307,8 @@
     for offset, size in groups:
         blocks.append([])
         for d in range(1, chans):
-            share = lax.dynamic_index_in_dim(shares[:, offset : offset + size], (chan + d) % chans, 0, keepdims=False)
-            blocks[-1].append(lax.ppermute(share, "chan", [(i, (i + d) % chans) for i in range(chans)]))
+            share = lax.dynamic_index_in_dim(shares[:, offset : offset + size], chan ^ d, 0, keepdims=False)
+            blocks[-1].append(lax.ppermute(share, "chan", [(i, i ^ d) for i in range(chans)]))
     lane_of = (chan_map % RAD) * HALF + chan_map // RAD
     lane_of = rolled(rolled(lane_of.reshape(chans, stns, slots), 0, chan, chans), 1, stn, stns)
     select = onehot(lane_of.reshape(CH), jnp.arange(CH, dtype=jnp.int32))
@@ -401,6 +402,7 @@
     fits = (
         voltages.shape[2] == FL
         and chans <= TAPS
+        and chans & (chans - 1) == 0
         and here % chans == 0
         and here // chans % 16 == 0
         and here == LANES

time: 76.9 us -> 76 us (0.988)
  starting transfers between devices: 14.5 us -> 12.5 us
  waiting for transfers between devices: 38 us -> 39.1 us
    ppermute x3, waiting for transfers between devices: 17.3 us -> 19.9 us  [fast_body(): lax.ppermute(share, 'chan', [(i, i ^ d) for i in range(chans)])]
    ppermute x3, starting transfers between devices: 4.67 us -> 2.65 us  [fast_body(): lax.ppermute(share, 'chan', [(i, i ^ d) for i in range(chans)])]
    ppermute x7, waiting for transfers between devices: 18.4 us -> 16.9 us  [fast_body(): got.append(lax.ppermute(pieces[d], ('chan', 'stn'), route))]
  transfers between devices with their start and end apart: 11 -> 11, of which waited for: 8 -> 7; matrix products, arithmetic and copies ran while one was open for 4% -> 4% of each run, Pallas kernels for 0% -> 0%
where the time goes in v4:
time: 76 us; the launch traced here: 75.8 us
  waiting for transfers between devices  39.1 us (51%)
  Pallas kernels  19.1 us (25%)
  starting transfers between devices  12.5 us (16%)
  other arithmetic  2.81 us (4%)
  local copies, waits for them, and re-layouts  2.12 us (3%)
    ppermute x3, waiting for transfers between devices, fast_body(): lax.ppermute(share, 'chan', [(i, i ^ d) for i in range(chans)])  19.9 us
    ppermute x7, waiting for transfers between devices, fast_body(): got.append(lax.ppermute(pieces[d], ('chan', 'stn'), route))  16.9 us
    pallas_call x1, Pallas kernels, gram(): pl.pallas_call(functools.partial(gram_kernel, frames, start, 1.0 / (frame...  11.4 us
    ppermute x7, starting transfers between devices, fast_body(): got.append(lax.ppermute(pieces[d], ('chan', 'stn'), route))  9.24 us
    pallas_call x1, Pallas kernels, filterbank(): pl.pallas_call(functools.partial(filterbank_kernel, frames, rows, offset,...  6.43 us
    ppermute x3, starting transfers between devices, fast_body(): lax.ppermute(share, 'chan', [(i, i ^ d) for i in range(chans)])  2.65 us
    ppermute x1, waiting for transfers between devices, fast_body(): other = lax.ppermute(own, 'pol', [(0, 1), (1, 0)])  2.29 us
    squeeze x1, local copies, waits for them, and re-layouts, fast_body(): lax.dynamic_index_in_dim(shares[:, offset:offset + size], chan ^ d, 0, ke...  1.99 us
  transfers between devices with their start and end apart: 11, of which 7 were waited for; matrix products, arithmetic and copies ran while one was open for 4% of the time, Pallas kernels for 0%

profile of v4, /device:TPU:9, one launch (start us, length us, event | category | flops | bytes accessed | tf_op | source)
XLA Modules:
  0.0 75.8 jit_solution(1590135448927964641)
XLA Ops:
  0.0 0.0 copy-start.4
  0.0 0.0 copy-start.2
  0.0 0.0 copy-start.3
  0.0 0.0 copy-start
  0.0 0.0 copy-start.6
  0.0 0.0 copy-start.5
  0.0 0.0 copy-start.1
  0.1 2.0 %dynamic-slice_bitcast_fusion = (bf16[32,4096]{1,0:T(8,128)(2,1)}, bf16[32,4096]{1,0:T(8,128)(2,1)S(1)}, bf16[32,4096]{1,0:T(8,128)(2,1)S(1)}) fusion(bf16[4,32,4096]{2,1,0:T(8,128)(2,1)} %bitcast.20, s32[]{:T(128)S(6)} %select_n.65, s32[]{:T(128)S(6)} %select_n.64, s32[]{:T(128)S(6)} %select_n.63), kind=kLoop, calls=%fused_computation.3 | loop fusion | bytes 1572876 | tf_op jit(solution)/shard_map/jit(dynamic_index_in_dim)/squeeze | solution.py:310
  2.1 0.0 collective-permute-start.2
  2.1 2.5 %collective-permute-start.1 = (bf16[32,4096]{1,0:T(8,128)(2,1)S(1)}, bf16[32,4096]{1,0:T(8,128)(2,1)S(1)}, u32[]{:S(2)}, u32[]{:S(2)}) collective-permute-start(bf16[32,4096]{1,0:T(8,128)(2,1)S(1)} %get-tuple-element.26), channel_id=1, source_target_pairs={{0,8},{4,12},{8,0},{12,4},{1,9},{5,13},{9,1},{13,5},{2,10},{6,14},... | collective-permute-start | bytes 786440 | tf_op jit(solution)/shard_map/ppermute | solution.py:311
  4.5 0.2 collective-permute-start
  4.7 0.7 fusion.2
  5.5 1.4 %fusion.refs_9_ = bf16[2048,2048]{1,0:T(8,128)(2,1)S(1)} fusion(s32[2048]{0:T(1024)S(1)} %bitcast.21), kind=kLoop, calls=%fused_computation.1 | loop fusion | flops 8388608 | bytes 8396800 | tf_op jit(solution)/shard_map/convert_element_type | solution.py:27
  6.9 0.0 copy-done.6
  7.0 0.1 add_bitcast_fusion
  7.1 0.1 iota_add_fusion
  7.1 5.4 %collective-permute-done.2.refs_3_ = bf16[32,4096]{1,0:T(8,128)(2,1)S(1)} collective-permute-done((bf16[32,4096]{1,0:T(8,128)(2,1)}, bf16[32,4096]{1,0:T(8,128)(2,1)S(1)}, u32[]{:S(2)}, u32[]{:S(2)}) %collective-permute-start.2) | collective-permute-done | bytes 262176 | tf_op jit(solution)/shard_map/ppermute | solution.py:311
  12.5 3.6 %collective-permute-done.1.refs_2_ = bf16[32,4096]{1,0:T(8,128)(2,1)S(1)} collective-permute-done((bf16[32,4096]{1,0:T(8,128)(2,1)S(1)}, bf16[32,4096]{1,0:T(8,128)(2,1)S(1)}, u32[]{:S(2)}, u32[]{:S(2)}) %collective-permute-start.1) | collective-permute-done | bytes 262176 | tf_op jit(solution)/shard_map/ppermute | solution.py:311
  16.1 10.9 %collective-permute-done.refs_1_ = bf16[32,4096]{1,0:T(8,128)(2,1)S(1)} collective-permute-done((bf16[32,4096]{1,0:T(8,128)(2,1)S(1)}, bf16[32,4096]{1,0:T(8,128)(2,1)S(1)}, u32[]{:S(2)}, u32[]{:S(2)}) %collective-permute-start) | collective-permute-done | bytes 262176 | tf_op jit(solution)/shard_map/ppermute | solution.py:311
  27.0 0.0 copy-done.4
  27.1 0.0 copy-done.2
  27.1 0.0 copy-done.3
  27.1 0.0 copy-done
  27.1 0.0 copy-done.5
  27.1 0.0 copy-done.1
  27.1 6.4 %filterbank.1 = (bf16[256,256]{1,0:T(8,128)(2,1)S(1)}, bf16[256,256]{1,0:T(8,128)(2,1)}, bf16[256,256]{1,0:T(8,128)(2,1)}, bf16[256,256]{1,0:T(8,128)(2,1)S(1)},...) custom-call(s32[1]{0:T(128)} %bitcast.1.chan_ref, ...), custom_call_target="tpu_custom_call" | custom-call | tf_op jit(solution)/shard_map/filterbank/pallas_call | solution.py:175
  33.5 1.3 %collective-permute-start.3 = (bf16[256,256]{1,0:T(8,128)(2,1)}, bf16[256,256]{1,0:T(8,128)(2,1)S(1)}, u32[]{:S(2)}, u32[]{:S(2)}) collective-permute-start(bf16[256,256]{1,0:T(8,128)(2,1)} %get-tuple-element.16), channel_id=1, source_target_pairs={{0,2},{2,0},{4,6},{6,4},{8,10},{10,8},{12,14},{14,12},{1,3},{3,1},... | collective-permute-start | bytes 393224 | tf_op jit(solution)/shard_map/ppermute | solution.py:330
  34.8 1.3 %collective-permute-start.4 = (bf16[256,256]{1,0:T(8,128)(2,1)}, bf16[256,256]{1,0:T(8,128)(2,1)S(1)}, u32[]{:S(2)}, u32[]{:S(2)}) collective-permute-start(bf16[256,256]{1,0:T(8,128)(2,1)} %get-tuple-element.17), channel_id=1, source_target_pairs={{0,4},{2,6},{4,8},{6,10},{8,12},{10,14},{12,0},{14,2},{1,5},{3,7},... | collective-permute-start | bytes 393224 | tf_op jit(solution)/shard_map/ppermute | solution.py:330
  36.1 0.1 broadcast_add_fusion
  36.2 0.1 add.139
  36.2 0.0 collective-permute-start.5
  36.3 2.2 %collective-permute-start.6 = (bf16[256,256]{1,0:T(8,128)(2,1)S(1)}, bf16[256,256]{1,0:T(8,128)(2,1)S(1)}, u32[]{:S(2)}, u32[]{:S(2)}) collective-permute-start(bf16[256,256]{1,0:T(8,128)(2,1)S(1)} %get-tuple-element.19), channel_id=1, source_target_pairs={{0,8},{2,10},{4,12},{6,14},{8,0},{10,2},{12,4},{14,6},{1,9},{3,11}... | collective-permute-start | bytes 393224 | tf_op jit(solution)/shard_map/ppermute | solution.py:330
  38.5 1.0 %collective-permute-start.7 = (bf16[256,256]{1,0:T(8,128)(2,1)S(1)}, bf16[256,256]{1,0:T(8,128)(2,1)S(1)}, u32[]{:S(2)}, u32[]{:S(2)}) collective-permute-start(bf16[256,256]{1,0:T(8,128)(2,1)S(1)} %get-tuple-element.20), channel_id=1, source_target_pairs={{0,10},{2,8},{4,14},{6,12},{8,2},{10,0},{12,6},{14,4},{1,11},{3,9}... | collective-permute-start | bytes 393224 | tf_op jit(solution)/shard_map/ppermute | solution.py:330
  39.5 0.0 collective-permute-done.3.refs_1_
  39.5 1.5 %collective-permute-start.8 = (bf16[256,256]{1,0:T(8,128)(2,1)S(1)}, bf16[256,256]{1,0:T(8,128)(2,1)S(1)}, u32[]{:S(2)}, u32[]{:S(2)}) collective-permute-start(bf16[256,256]{1,0:T(8,128)(2,1)S(1)} %get-tuple-element.21), channel_id=1, source_target_pairs={{0,12},{2,14},{4,0},{6,2},{8,4},{10,6},{12,8},{14,10},{1,13},{3,15... | collective-permute-start | bytes 393224 | tf_op jit(solution)/shard_map/ppermute | solution.py:330
  41.0 0.0 collective-permute-done.4.refs_2_
  41.0 1.9 %collective-permute-start.9 = (bf16[256,256]{1,0:T(8,128)(2,1)S(1)}, bf16[256,256]{1,0:T(8,128)(2,1)S(1)}, u32[]{:S(2)}, u32[]{:S(2)}) collective-permute-start(bf16[256,256]{1,0:T(8,128)(2,1)S(1)} %get-tuple-element.22), channel_id=1, source_target_pairs={{0,14},{2,12},{4,2},{6,0},{8,6},{10,4},{12,10},{14,8},{1,15},{3,13... | collective-permute-start | bytes 393224 | tf_op jit(solution)/shard_map/ppermute | solution.py:330
  42.9 0.4 compare_convert_fusion.refs_8_
  43.3 0.0 collective-permute-done.5.refs_3_
  43.4 1.8 %collective-permute-done.6.refs_4_ = bf16[256,256]{1,0:T(8,128)(2,1)S(1)} collective-permute-done((bf16[256,256]{1,0:T(8,128)(2,1)S(1)}, bf16[256,256]{1,0:T(8,128)(2,1)S(1)}, u32[]{:S(2)}, u32[]{:S(2)}) %collective-permute-start.6) | collective-permute-done | bytes 131104 | tf_op jit(solution)/shard_map/ppermute | solution.py:330
  45.1 11.6 %collective-permute-done.7.refs_5_ = bf16[256,256]{1,0:T(8,128)(2,1)S(1)} collective-permute-done((bf16[256,256]{1,0:T(8,128)(2,1)S(1)}, bf16[256,256]{1,0:T(8,128)(2,1)S(1)}, u32[]{:S(2)}, u32[]{:S(2)}) %collective-permute-start.7) | collective-permute-done | bytes 131104 | tf_op jit(solution)/shard_map/ppermute | solution.py:330
  56.7 0.0 collective-permute-done.8.refs_6_
  56.7 3.5 %collective-permute-done.9.refs_7_ = bf16[256,256]{1,0:T(8,128)(2,1)S(1)} collective-permute-done((bf16[256,256]{1,0:T(8,128)(2,1)S(1)}, bf16[256,256]{1,0:T(8,128)(2,1)S(1)}, u32[]{:S(2)}, u32[]{:S(2)}) %collective-permute-start.9) | collective-permute-done | bytes 131104 | tf_op jit(solution)/shard_map/ppermute | solution.py:330
  60.2 1.3 %order.1 = (bf16[512,1024]{1,0:T(8,128)(2,1)S(1)}, bf16[512,1024]{1,0:T(8,128)(2,1)S(1)}) custom-call(bf16[256,256]{1,0:T(8,128)(2,1)S(1)} %get-tuple-element.15.refs_0_, bf16[256,256]{1,0:T(8,128)(2,1)S(1)} %collective-permute-done.3.refs_1_, bf16[256,256]{1,0:T(8,128)(2,1)S(1)} %collective-permute-done.4.refs_2_, ...), custom_call_target="tpu_custom_call" | custom-call | tf_op jit(solution)/shard_map/order/pallas_call | solution.py:211
  61.5 0.6 collective-permute-start.10
  62.0 2.3 %collective-permute-done.10.other = bf16[512,1024]{1,0:T(8,128)(2,1)S(1)} collective-permute-done((bf16[512,1024]{1,0:T(8,128)(2,1)S(1)}, bf16[512,1024]{1,0:T(8,128)(2,1)S(1)}, u32[]{:S(2)}, u32[]{:S(2)}) %collective-permute-start.10) | collective-permute-done | bytes 1048608 | tf_op jit(solution)/shard_map/ppermute | solution.py:336
  64.3 11.4 %gram.1 = f32[2,32,1024,128]{3,2,1,0:T(8,128)} custom-call(s32[1]{0:T(128)} %bitcast.pol_ref, bf16[512,1024]{1,0:T(8,128)(2,1)S(1)} %get-tuple-element.23.own, bf16[512,1024]{1,0:T(8,128)(2,1)S(1)} %get-tuple-element.24.turned, bf16[512,1024]{1,0:T(8,128)(2,1)S(1)} %collective-permute-done.10.other), custom_call_target="tpu_custom_call" | custom-call | tf_op jit(solution)/shard_map/gram/pallas_call | solution.py:274
  (7 shorter events, 0.1 us)
Async XLA Ops:
  0.0 27.0 %copy-start.4 = (f32[16,256]{1,0:T(8,128)S(1)}, f32[16,256]{1,0:T(8,128)}, u32[]{:S(2)}) copy-start(f32[16,256]{1,0:T(8,128)} %constant.109.clone.refs_6_) | copy-start | bytes 49156
  0.0 27.1 %copy-start.2 = (bf16[512,256]{1,0:T(8,128)(2,1)S(1)}, bf16[512,256]{1,0:T(8,128)(2,1)}, u32[]{:S(2)}) copy-start(bf16[512,256]{1,0:T(8,128)(2,1)} %constant.108.clone.refs_8_) | copy-start | bytes 786436
  0.0 27.1 %copy-start.3 = (bf16[512,256]{1,0:T(8,128)(2,1)S(1)}, bf16[512,256]{1,0:T(8,128)(2,1)}, u32[]{:S(2)}) copy-start(bf16[512,256]{1,0:T(8,128)(2,1)} %constant.107.clone.refs_7_) | copy-start | bytes 786436
  0.0 27.1 %copy-start = (bf16[1,128,4096]{2,1,0:T(8,128)(2,1)S(1)}, bf16[1,128,4096]{2,1,0:T(8,128)(2,1)}, u32[]{:S(2)}) copy-start(bf16[1,128,4096]{2,1,0:T(8,128)(2,1)} %refs_0_.1) | copy-start | bytes 3145732
  0.0 6.9 %copy-start.6 = (s32[256]{0:T(256)S(1)}, s32[256]{0:T(256)}, u32[]{:S(2)}) copy-start(s32[256]{0:T(256)} %param.11) | copy-start | bytes 3076
  0.0 27.0 %copy-start.5 = (s32[1,128]{1,0:T(1,128)S(1)}, s32[1,128]{1,0:T(1,128)}, u32[]{:S(2)}) copy-start(s32[1,128]{1,0:T(1,128)} %refs_5_.1) | copy-start | bytes 1540
  0.0 27.0 %copy-start.1 = (f32[16,4096]{1,0:T(8,128)S(1)}, f32[16,4096]{1,0:T(8,128)}, u32[]{:S(2)}) copy-start(f32[16,4096]{1,0:T(8,128)} %refs_4_.1) | copy-start | bytes 786436
  2.1 10.4 %collective-permute-start.2 = (bf16[32,4096]{1,0:T(8,128)(2,1)}, bf16[32,4096]{1,0:T(8,128)(2,1)S(1)}, u32[]{:S(2)}, u32[]{:S(2)}) collective-permute-start(bf16[32,4096]{1,0:T(8,128)(2,1)} %get-tuple-element.25), channel_id=1, source_target_pairs={{0,4},{4,0},{8,12},{12,8},{1,5},{5,1},{9,13},{13,9},{2,6},{6,2},{1... | collective-permute-start | bytes 786440 | tf_op jit(solution)/shard_map/ppermute | solution.py:311
  2.1 14.1 %collective-permute-start.1 = (bf16[32,4096]{1,0:T(8,128)(2,1)S(1)}, bf16[32,4096]{1,0:T(8,128)(2,1)S(1)}, u32[]{:S(2)}, u32[]{:S(2)}) collective-permute-start(bf16[32,4096]{1,0:T(8,128)(2,1)S(1)} %get-tuple-element.26), channel_id=1, source_target_pairs={{0,8},{4,12},{8,0},{12,4},{1,9},{5,13},{9,1},{13,5},{2,10},{6,14},... | collective-permute-start | bytes 786440 | tf_op jit(solution)/shard_map/ppermute | solution.py:311
  4.5 22.5 %collective-permute-start = (bf16[32,4096]{1,0:T(8,128)(2,1)S(1)}, bf16[32,4096]{1,0:T(8,128)(2,1)S(1)}, u32[]{:S(2)}, u32[]{:S(2)}) collective-permute-start(bf16[32,4096]{1,0:T(8,128)(2,1)S(1)} %get-tuple-element.27), channel_id=1, source_target_pairs={{0,12},{4,8},{8,4},{12,0},{1,13},{5,9},{9,5},{13,1},{2,14},{6,10},... | collective-permute-start | bytes 786440 | tf_op jit(solution)/shard_map/ppermute | solution.py:311
  33.5 6.0 %collective-permute-start.3 = (bf16[256,256]{1,0:T(8,128)(2,1)}, bf16[256,256]{1,0:T(8,128)(2,1)S(1)}, u32[]{:S(2)}, u32[]{:S(2)}) collective-permute-start(bf16[256,256]{1,0:T(8,128)(2,1)} %get-tuple-element.16), channel_id=1, source_target_pairs={{0,2},{2,0},{4,6},{6,4},{8,10},{10,8},{12,14},{14,12},{1,3},{3,1},... | collective-permute-start | bytes 393224 | tf_op jit(solution)/shard_map/ppermute | solution.py:330
  34.8 6.2 %collective-permute-start.4 = (bf16[256,256]{1,0:T(8,128)(2,1)}, bf16[256,256]{1,0:T(8,128)(2,1)S(1)}, u32[]{:S(2)}, u32[]{:S(2)}) collective-permute-start(bf16[256,256]{1,0:T(8,128)(2,1)} %get-tuple-element.17), channel_id=1, source_target_pairs={{0,4},{2,6},{4,8},{6,10},{8,12},{10,14},{12,0},{14,2},{1,5},{3,7},... | collective-permute-start | bytes 393224 | tf_op jit(solution)/shard_map/ppermute | solution.py:330
  36.2 7.1 %collective-permute-start.5 = (bf16[256,256]{1,0:T(8,128)(2,1)S(1)}, bf16[256,256]{1,0:T(8,128)(2,1)S(1)}, u32[]{:S(2)}, u32[]{:S(2)}) collective-permute-start(bf16[256,256]{1,0:T(8,128)(2,1)S(1)} %get-tuple-element.18), channel_id=1, source_target_pairs={{0,6},{2,4},{4,10},{6,8},{8,14},{10,12},{12,2},{14,0},{1,7},{3,5},... | collective-permute-start | bytes 393224 | tf_op jit(solution)/shard_map/ppermute | solution.py:330
  36.3 8.9 %collective-permute-start.6 = (bf16[256,256]{1,0:T(8,128)(2,1)S(1)}, bf16[256,256]{1,0:T(8,128)(2,1)S(1)}, u32[]{:S(2)}, u32[]{:S(2)}) collective-permute-start(bf16[256,256]{1,0:T(8,128)(2,1)S(1)} %get-tuple-element.19), channel_id=1, source_target_pairs={{0,8},{2,10},{4,12},{6,14},{8,0},{10,2},{12,4},{14,6},{1,9},{3,11}... | collective-permute-start | bytes 393224 | tf_op jit(solution)/shard_map/ppermute | solution.py:330
  38.5 18.3 %collective-permute-start.7 = (bf16[256,256]{1,0:T(8,128)(2,1)S(1)}, bf16[256,256]{1,0:T(8,128)(2,1)S(1)}, u32[]{:S(2)}, u32[]{:S(2)}) collective-permute-start(bf16[256,256]{1,0:T(8,128)(2,1)S(1)} %get-tuple-element.20), channel_id=1, source_target_pairs={{0,10},{2,8},{4,14},{6,12},{8,2},{10,0},{12,6},{14,4},{1,11},{3,9}... | collective-permute-start | bytes 393224 | tf_op jit(solution)/shard_map/ppermute | solution.py:330
  39.5 17.2 %collective-permute-start.8 = (bf16[256,256]{1,0:T(8,128)(2,1)S(1)}, bf16[256,256]{1,0:T(8,128)(2,1)S(1)}, u32[]{:S(2)}, u32[]{:S(2)}) collective-permute-start(bf16[256,256]{1,0:T(8,128)(2,1)S(1)} %get-tuple-element.21), channel_id=1, source_target_pairs={{0,12},{2,14},{4,0},{6,2},{8,4},{10,6},{12,8},{14,10},{1,13},{3,15... | collective-permute-start | bytes 393224 | tf_op jit(solution)/shard_map/ppermute | solution.py:330
  41.0 19.2 %collective-permute-start.9 = (bf16[256,256]{1,0:T(8,128)(2,1)S(1)}, bf16[256,256]{1,0:T(8,128)(2,1)S(1)}, u32[]{:S(2)}, u32[]{:S(2)}) collective-permute-start(bf16[256,256]{1,0:T(8,128)(2,1)S(1)} %get-tuple-element.22), channel_id=1, source_target_pairs={{0,14},{2,12},{4,2},{6,0},{8,6},{10,4},{12,10},{14,8},{1,15},{3,13... | collective-permute-start | bytes 393224 | tf_op jit(solution)/shard_map/ppermute | solution.py:330
  61.5 2.8 %collective-permute-start.10 = (bf16[512,1024]{1,0:T(8,128)(2,1)S(1)}, bf16[512,1024]{1,0:T(8,128)(2,1)S(1)}, u32[]{:S(2)}, u32[]{:S(2)}) collective-permute-start(bf16[512,1024]{1,0:T(8,128)(2,1)S(1)} %get-tuple-element.23.own), channel_id=1, source_target_pairs={{0,1},{1,0},{2,3},{3,2},{4,5},{5,4},{6,7},{7,6},{8,9},{9,8},{10,11... | collective-permute-start | bytes 3145736 | tf_op jit(solution)/shard_map/ppermute | solution.py:336

commit v5 on v4

--- a/solution.py
+++ b/solution.py
@@ -78,19 +78,28 @@
     return high, (value - high.astype(f32)).astype(bf16)
 
 
-def filterbank_kernel(frames, rows, offset, share, chan_ref, *refs):
+def filterbank_kernel(frames, share, group, pieces, before, chan_ref, *refs):
+    offset, rows = group
     volts, *blocks = refs[:frames]
     blocks = blocks[::-1]
-    fir, flag, twiddle, dft_hi, dft_lo, select = refs[frames : frames + 6]
-    outs = refs[frames + 6 : -5]
-    x, u_hi, u_lo, spec, sem = refs[-5:]
+    fir, flag, twiddle, dft_hi, dft_lo, *rest = refs[frames:-4]
+    x, u_hi, u_lo, sem = refs[-4:]
+    if pieces:
+        spec = rest.pop()
+    prior = [rest.pop(0) for _ in range(before)]
+    select, *outs = rest
+    if not pieces:
+        [spec] = outs
     total = frames * rows
+    whole = frames * share
     chan = chan_ref[0]
     begin = pl.multiple_of(chan * share + offset, rows)
     load = pltpu.make_async_copy(volts.at[0, pl.ds(begin, rows)], x.at[chan], sem)
     load.start()
     for d in range(1, frames):
         x[jnp.bitwise_xor(chan, d)] = blocks[d - 1][...]
+    for earlier in prior:
+        spec[...] = earlier[...]
     load.wait()
     step = 16
     halves = PT // LANES
@@ -140,53 +149,57 @@
     for f in range(1, frames):
         keep = jnp.where(lane >= f * rows, pltpu.roll(mine, f * rows, 1), keep)
     keep = keep[:, :total]
+    lanes_of = [slice(part * whole + frames * offset, part * whole + frames * offset + total) for part in range(2)]
 
     def put(c, re, im):
-        spec[c, :, :total] = (re * keep).astype(bf16)
-        spec[c, :, total:] = (im * keep).astype(bf16)
-
-    def pair(c, carry):
-        got = three(2 * c - 1, 2, 2 * PT)
-        re, im = got[:, :total], got[:, total:]
-        put(c, re[:HALF] - im[HALF:PT], re[HALF:PT] + im[:HALF])
-        o = PT + HALF
-        put(RAD - c, re[PT:o] - im[o:], -(re[o:] + im[PT:o]))
-        return carry
+        spec[c, :, lanes_of[0]] = (re * keep).astype(bf16)
+        spec[c, :, lanes_of[1]] = (im * keep).astype(bf16)
 
     got = three(0, 1, PT)
     put(0, got[:HALF], got[HALF:])
-    got = three(RAD - 1, 2, PT)
-    re, im = got[:, :total], got[:, total:]
-    put(RAD // 2, re[:HALF] - im[HALF:], re[HALF:] + im[:HALF])
-    lax.fori_loop(1, RAD // 2, pair, 0, unroll=True)
-    right = spec[...].reshape(CH, 2 * total)
-    size = CH // len(outs)
-    for first in range(0, len(outs), BATCH):
+    per = max(1, LANES // total)
+    o = PT + HALF
+    for first in range(1, RAD // 2 + 1, per):
+        got = three(2 * first - 1, 2 * per, PT if first == RAD // 2 else 2 * PT)
+        for k in range(per):
+            c = first + k
+            re, im = got[:, 2 * k * total : (2 * k + 1) * total], got[:, (2 * k + 1) * total : (2 * k + 2) * total]
+            put(c, re[:HALF] - im[HALF:PT], re[HALF:PT] + im[:HALF])
+            if c < RAD // 2:
+                put(RAD - c, re[PT:o] - im[o:], -(re[o:] + im[PT:o]))
+    if not pieces:
+        return
+    right = spec[...].reshape(CH, 2 * whole)
+    size = CH // pieces
+    for first in range(0, pieces, BATCH):
         got = jnp.dot(select[first * size : (first + BATCH) * size], right, preferred_element_type=f32).astype(bf16)
         for d in range(BATCH):
             outs[first + d][...] = got[d * size : (d + 1) * size]
 
 
-def filterbank(chan, volts, blocks, fir, flag, select, owners, offset, share):
-    frames, rows = len(blocks) + 1, blocks[0].shape[0]
-    total = frames * rows
+def filterbank(chan, volts, blocks, fir, flag, share, group, prior, select, pieces):
+    frames, rows = len(blocks) + 1, group[1]
+    total, whole = frames * rows, frames * share
     vmem = pl.BlockSpec(memory_space=pltpu.VMEM)
     high, low, twiddle = (jnp.asarray(t) for t in tables())
+    spec = (RAD, HALF, 2 * whole)
+    args = [*blocks[::-1], fir, flag, twiddle, high, low] + prior + [select]
+    outs = [jax.ShapeDtypeStruct((CH // pieces, 2 * whole), bf16)] * pieces if pieces else jax.ShapeDtypeStruct(spec, bf16)
     return pl.pallas_call(
-        functools.partial(filterbank_kernel, frames, rows, offset, share),
-        out_shape=[jax.ShapeDtypeStruct((CH // owners, 2 * total), bf16)] * owners,
-        in_specs=[pl.BlockSpec(memory_space=pltpu.SMEM), pl.BlockSpec(memory_space=pl.ANY)] + [vmem] * (frames + 5),
-        out_specs=[vmem] * owners,
-        scratch_shapes=[
+        functools.partial(filterbank_kernel, frames, share, group, pieces, len(prior)),
+        out_shape=outs,
+        in_specs=[pl.BlockSpec(memory_space=pltpu.SMEM), pl.BlockSpec(memory_space=pl.ANY)] + [vmem] * len(args),
+        out_specs=[vmem] * pieces if pieces else vmem,
+        scratch_shapes=([pltpu.VMEM(spec, bf16)] if pieces else [])
+        + [
             pltpu.VMEM((frames, rows, FL), bf16),
             pltpu.VMEM((RAD + 1, total, PT), bf16),
             pltpu.VMEM((RAD + 1, total, PT), bf16),
-            pltpu.VMEM((RAD, HALF, 2 * total), bf16),
             pltpu.SemaphoreType.DMA,
         ],
         compiler_params=pltpu.CompilerParams(vmem_limit_bytes=24 << 20),
-        name="filterbank",
-    )(chan, volts, *blocks[::-1], fir, flag, twiddle, high, low, select)
+        name="filterbank" if pieces else "transform",
+    )(chan, volts, *args)
 
 
 def order_kernel(pieces, *refs):
@@ -288,7 +301,8 @@
 
 
 def groups_of(rows):
-    return [(0, rows)]
+    half = rows // 2
+    return [(0, half), (half, half)] if half % 16 == 0 else [(0, rows)]
 
 
 def fast_body(voltages, fir_coeffs, flags, station_slot, chan_map):
@@ -312,26 +326,25 @@
     lane_of = (chan_map % RAD) * HALF + chan_map // RAD
     lane_of = rolled(rolled(lane_of.reshape(chans, stns, slots), 0, chan, chans), 1, stn, stns)
     select = onehot(lane_of.reshape(CH), jnp.arange(CH, dtype=jnp.int32))
-    got = []
-    place = []
     dist = jnp.arange(owners, dtype=jnp.int32)
     row0 = (stn - dist % stns) % stns * here + (chan - dist // stns) % chans * rows
     col = station_slot[None, :] + stations * jnp.arange(frames, dtype=jnp.int32)[:, None]
-    for (offset, size), block in zip(groups, blocks, strict=True):
+    prior, place = [], []
+    for n, (group, block) in enumerate(zip(groups, blocks, strict=True)):
+        count = owners if n == len(groups) - 1 else 0
         pieces = filterbank(
-            chan.reshape(1), voltages, block, fir_coeffs, flags, select, owners, offset, rows
+            chan.reshape(1), voltages, block, fir_coeffs, flags, rows, group, prior, select, count
         )
-        got.append(pieces[0])
-        for d in range(1, owners):
-            dc, ds = divmod(d, stns)
-            route = [
-                (i * stns + j, (i + dc) % chans * stns + (j + ds) % stns) for i in range(chans) for j in range(stns)
-            ]
-            got.append(lax.ppermute(pieces[d], ("chan", "stn"), route))
-        row = row0[:, None, None] + offset + jnp.arange(size, dtype=jnp.int32)[None, None, :]
+        prior = [pieces]
+        row = row0[:, None, None] + group[0] + jnp.arange(group[1], dtype=jnp.int32)[None, None, :]
         row = row + stations * jnp.arange(frames, dtype=jnp.int32)[None, :, None]
-        place.append(row.reshape(-1))
-    place = onehot(jnp.concatenate(place), col.reshape(-1))
+        place.append(row.reshape(owners, -1))
+    place = onehot(jnp.concatenate(place, axis=1).reshape(-1), col.reshape(-1))
+    got = [pieces[0]]
+    for d in range(1, owners):
+        dc, ds = divmod(d, stns)
+        route = [(i * stns + j, (i + dc) % chans * stns + (j + ds) % stns) for i in range(chans) for j in range(stns)]
+        got.append(lax.ppermute(pieces[d], ("chan", "stn"), route))
     own, turned = order(got, place)
     other = lax.ppermute(own, "pol", [(0, 1), (1, 0)])
     out = gram(pol.reshape(1), own, turned, other, frames, coarse, 0, None)

time: 76 us -> 75.2 us (0.989)
  waiting for transfers between devices: 39.1 us -> 26.3 us
  local copies, waits for them, and re-layouts: 2.12 us -> 6.58 us
  starting transfers between devices: 12.5 us -> 16.3 us
  other arithmetic: 2.81 us -> 6.22 us
    ppermute x3 -> x6, waiting for transfers between devices: 19.9 us -> 6.06 us  [fast_body(): lax.ppermute(share, 'chan', [(i, i ^ d) for i in range(chans)])]
    ppermute x3 -> x6, starting transfers between devices: 2.65 us -> 6.15 us  [fast_body(): lax.ppermute(share, 'chan', [(i, i ^ d) for i in range(chans)])]
    convert_element_type x2, other arithmetic: 1.82 us -> 5.22 us  [onehot(): return (rows[:, None] == cols[None, :]).astype(bf16)]
    unnamed x16 -> x20, local copies, waits for them, and re-layouts: 0.04 us -> 3.42 us
    slice x0 -> x1, local copies, waits for them, and re-layouts: none -> 1.41 us  [fast_body(): shares[:, offset:offset + size]]
    ppermute x7, waiting for transfers between devices: 16.9 us -> 18 us  [fast_body(): got.append(lax.ppermute(pieces[d], ('chan', 'stn'), route))]
    squeeze x1 -> x2, local copies, waits for them, and re-layouts: 1.99 us -> 1.42 us  [fast_body(): lax.dynamic_index_in_dim(shares[:, offset:offset + size], chan ^ d, 0, ke...]
    pallas_call x1 -> x2, Pallas kernels: 6.43 us -> 6.66 us  [filterbank(): pl.pallas_call(functools.partial(filterbank_kernel, frames, share, group,...]
  transfers between devices with their start and end apart: 11 -> 14, of which waited for: 7 -> 8; matrix products, arithmetic and copies ran while one was open for 4% -> 10% of each run, Pallas kernels for 0% -> 3%
where the time goes in v5:
time: 75.2 us; the launch traced here: 75 us
  waiting for transfers between devices  26.3 us (35%)
  Pallas kernels  19.3 us (26%)
  starting transfers between devices  16.3 us (22%)
  local copies, waits for them, and re-layouts  6.58 us (9%)
  other arithmetic  6.22 us (8%)
    ppermute x7, waiting for transfers between devices, fast_body(): got.append(lax.ppermute(pieces[d], ('chan', 'stn'), route))  18 us
    pallas_call x1, Pallas kernels, gram(): pl.pallas_call(functools.partial(gram_kernel, frames, start, 1.0 / (frame...  11.4 us
    ppermute x7, starting transfers between devices, fast_body(): got.append(lax.ppermute(pieces[d], ('chan', 'stn'), route))  9.24 us
    pallas_call x2, Pallas kernels, filterbank(): pl.pallas_call(functools.partial(filterbank_kernel, frames, share, group,...  6.66 us
    ppermute x6, starting transfers between devices, fast_body(): lax.ppermute(share, 'chan', [(i, i ^ d) for i in range(chans)])  6.15 us
    ppermute x6, waiting for transfers between devices, fast_body(): lax.ppermute(share, 'chan', [(i, i ^ d) for i in range(chans)])  6.06 us
    convert_element_type x2, other arithmetic, onehot(): return (rows[:, None] == cols[None, :]).astype(bf16)  5.22 us
    unnamed x20, local copies, waits for them, and re-layouts  3.42 us
  transfers between devices with their start and end apart: 14, of which 8 were waited for; matrix products, arithmetic and copies ran while one was open for 10% of the time, Pallas kernels for 3%

profile of v5, /device:TPU:9, one launch (start us, length us, event | category | flops | bytes accessed | tf_op | source)
XLA Modules:
  0.0 75.0 jit_solution(7134711779687923346)
XLA Ops:
  0.0 0.0 copy-start.6
  0.0 0.0 copy-start.4
  0.0 0.0 copy-start.5
  0.0 0.0 copy-start.2
  0.0 0.0 copy-start.7
  0.0 0.0 copy-start.3
  0.1 1.4 %fusion.18 = (bf16[4,16,4096]{2,1,0:T(8,128)(2,1)S(1)}, bf16[4,16,4096]{2,1,0:T(8,128)(2,1)S(1)}) fusion(bf16[4,32,4096]{2,1,0:T(8,128)(2,1)} %bitcast.28), kind=kLoop, calls=%fused_computation.53 | loop fusion | bytes 2097152 | tf_op jit(solution)/shard_map/slice | solution.py:324
  1.5 0.7 dynamic-slice_bitcast_fusion
  2.2 0.0 collective-permute-start.5
  2.2 2.5 %collective-permute-start.4 = (bf16[16,4096]{1,0:T(8,128)(2,1)S(1)}, bf16[16,4096]{1,0:T(8,128)(2,1)S(1)}, u32[]{:S(2)}, u32[]{:S(2)}) collective-permute-start(bf16[16,4096]{1,0:T(8,128)(2,1)S(1)} %get-tuple-element.30), channel_id=1, source_target_pairs={{0,8},{4,12},{8,0},{12,4},{1,9},{5,13},{9,1},{13,5},{2,10},{6,14},... | collective-permute-start | bytes 393224 | tf_op jit(solution)/shard_map/ppermute | solution.py:325
  4.7 0.2 collective-permute-start.3
  4.8 0.7 dynamic-slice_bitcast_fusion.3
  5.6 1.1 %collective-permute-start.2 = (bf16[16,4096]{1,0:T(8,128)(2,1)}, bf16[16,4096]{1,0:T(8,128)(2,1)S(1)}, u32[]{:S(2)}, u32[]{:S(2)}) collective-permute-start(bf16[16,4096]{1,0:T(8,128)(2,1)} %get-tuple-element.32), channel_id=1, source_target_pairs={{0,4},{4,0},{8,12},{12,8},{1,5},{5,1},{9,13},{13,9},{2,6},{6,2},{1... | collective-permute-start | bytes 393224 | tf_op jit(solution)/shard_map/ppermute | solution.py:325
  6.7 2.1 %collective-permute-start.1 = (bf16[16,4096]{1,0:T(8,128)(2,1)}, bf16[16,4096]{1,0:T(8,128)(2,1)S(1)}, u32[]{:S(2)}, u32[]{:S(2)}) collective-permute-start(bf16[16,4096]{1,0:T(8,128)(2,1)} %get-tuple-element.33), channel_id=1, source_target_pairs={{0,8},{4,12},{8,0},{12,4},{1,9},{5,13},{9,1},{13,5},{2,10},{6,14},... | collective-permute-start | bytes 393224 | tf_op jit(solution)/shard_map/ppermute | solution.py:325
  8.8 0.1 add.202
  8.9 0.1 add.203
  8.9 0.7 fusion.2
  9.8 4.8 %fusion.refs_9_.refs_10_ = bf16[2048,2048]{1,0:T(8,128)(2,1)} fusion(s32[2048]{0:T(1024)S(1)} %bitcast.29), kind=kLoop, calls=%fused_computation.1 | loop fusion | flops 8388608 | bytes 8396800 | tf_op jit(solution)/shard_map/convert_element_type | solution.py:27
  14.6 0.1 iota_add_fusion
  14.6 0.1 add.211
  14.7 0.1 add.201
  14.8 0.0 collective-permute-done.5.refs_3_
  14.8 0.3 collective-permute-start
  15.1 0.0 collective-permute-done.4.refs_2_
  15.1 0.8 %collective-permute-done.3.refs_1_ = bf16[16,4096]{1,0:T(8,128)(2,1)S(1)} collective-permute-done((bf16[16,4096]{1,0:T(8,128)(2,1)S(1)}, bf16[16,4096]{1,0:T(8,128)(2,1)S(1)}, u32[]{:S(2)}, u32[]{:S(2)}) %collective-permute-start.3) | collective-permute-done | bytes 131104 | tf_op jit(solution)/shard_map/ppermute | solution.py:325
  15.9 0.0 copy-done.6
  15.9 0.0 copy-done.4
  15.9 0.0 copy-done.5
  15.9 0.0 copy-done.2
  15.9 0.0 copy-done.7
  16.0 0.0 copy-done.3
  16.0 0.0 copy-start
  16.0 3.4 %copy-done = bf16[2048,2048]{1,0:T(8,128)(2,1)S(1)} copy-done((bf16[2048,2048]{1,0:T(8,128)(2,1)S(1)}, bf16[2048,2048]{1,0:T(8,128)(2,1)}, u32[]{:S(2)}) %copy-start) | copy-done | bytes 8388632
  19.3 0.0 copy-start.1
  19.4 2.2 %transform.1.refs_9_ = bf16[16,128,256]{2,1,0:T(8,128)(2,1)S(1)} custom-call(s32[1]{0:T(128)} %bitcast.1.chan_ref, bf16[1,128,4096]{2,1,0:T(8,128)(2,1)S(1)} %copy-done.2, bf16[16,4096]{1,0:T(8,128)(2,1)S(1)} %collective-permute-done.3.refs_1_, bf16[16,4096]{1,0:T(8,128)(2,1)S(1)} %collective-permute-done.4.refs_2_, ...), custom_call_target="tpu_custom_call" | custom-call | tf_op jit(solution)/shard_map/transform/pallas_call | solution.py:188
  21.6 0.0 copy-start.8
  21.6 0.0 collective-permute-done.2.refs_3_
  21.6 2.2 %collective-permute-done.1.refs_2_ = bf16[16,4096]{1,0:T(8,128)(2,1)S(1)} collective-permute-done((bf16[16,4096]{1,0:T(8,128)(2,1)}, bf16[16,4096]{1,0:T(8,128)(2,1)S(1)}, u32[]{:S(2)}, u32[]{:S(2)}) %collective-permute-start.1) | collective-permute-done | bytes 131104 | tf_op jit(solution)/shard_map/ppermute | solution.py:325
  23.8 3.1 %collective-permute-done.refs_1_ = bf16[16,4096]{1,0:T(8,128)(2,1)S(1)} collective-permute-done((bf16[16,4096]{1,0:T(8,128)(2,1)S(1)}, bf16[16,4096]{1,0:T(8,128)(2,1)S(1)}, u32[]{:S(2)}, u32[]{:S(2)}) %collective-permute-start) | collective-permute-done | bytes 131104 | tf_op jit(solution)/shard_map/ppermute | solution.py:325
  26.9 0.0 copy-done.1
  26.9 4.4 %filterbank.1 = (bf16[256,256]{1,0:T(8,128)(2,1)S(1)}, bf16[256,256]{1,0:T(8,128)(2,1)S(1)}, bf16[256,256]{1,0:T(8,128)(2,1)S(1)}, bf16[256,256]{1,0:T(8,128)(2,...) custom-call(s32[1]{0:T(128)} %bitcast.1.chan_ref, ...), custom_call_target="tpu_custom_call" | custom-call | tf_op jit(solution)/shard_map/filterbank/pallas_call | solution.py:188
  31.3 1.3 %collective-permute-start.6 = (bf16[256,256]{1,0:T(8,128)(2,1)S(1)}, bf16[256,256]{1,0:T(8,128)(2,1)S(1)}, u32[]{:S(2)}, u32[]{:S(2)}) collective-permute-start(bf16[256,256]{1,0:T(8,128)(2,1)S(1)} %get-tuple-element.16), channel_id=1, source_target_pairs={{0,2},{2,0},{4,6},{6,4},{8,10},{10,8},{12,14},{14,12},{1,3},{3,1},... | collective-permute-start | bytes 393224 | tf_op jit(solution)/shard_map/ppermute | solution.py:347
  32.6 1.8 %collective-permute-start.7 = (bf16[256,256]{1,0:T(8,128)(2,1)S(1)}, bf16[256,256]{1,0:T(8,128)(2,1)S(1)}, u32[]{:S(2)}, u32[]{:S(2)}) collective-permute-start(bf16[256,256]{1,0:T(8,128)(2,1)S(1)} %get-tuple-element.17), channel_id=1, source_target_pairs={{0,4},{2,6},{4,8},{6,10},{8,12},{10,14},{12,0},{14,2},{1,5},{3,7},... | collective-permute-start | bytes 393224 | tf_op jit(solution)/shard_map/ppermute | solution.py:347
  34.4 0.0 copy-done.8
  34.4 0.1 add_bitcast_fusion.1
  34.5 0.1 add_bitcast_fusion
  34.6 0.0 collective-permute-start.8
  34.6 1.7 %collective-permute-start.9 = (bf16[256,256]{1,0:T(8,128)(2,1)S(1)}, bf16[256,256]{1,0:T(8,128)(2,1)S(1)}, u32[]{:S(2)}, u32[]{:S(2)}) collective-permute-start(bf16[256,256]{1,0:T(8,128)(2,1)S(1)} %get-tuple-element.19), channel_id=1, source_target_pairs={{0,8},{2,10},{4,12},{6,14},{8,0},{10,2},{12,4},{14,6},{1,9},{3,11}... | collective-permute-start | bytes 393224 | tf_op jit(solution)/shard_map/ppermute | solution.py:347
  36.2 1.6 %collective-permute-start.10 = (bf16[256,256]{1,0:T(8,128)(2,1)S(1)}, bf16[256,256]{1,0:T(8,128)(2,1)S(1)}, u32[]{:S(2)}, u32[]{:S(2)}) collective-permute-start(bf16[256,256]{1,0:T(8,128)(2,1)S(1)} %get-tuple-element.20), channel_id=1, source_target_pairs={{0,10},{2,8},{4,14},{6,12},{8,2},{10,0},{12,6},{14,4},{1,11},{3,9}... | collective-permute-start | bytes 393224 | tf_op jit(solution)/shard_map/ppermute | solution.py:347
  37.8 0.0 collective-permute-done.6.refs_1_
  37.8 1.5 %collective-permute-start.11 = (bf16[256,256]{1,0:T(8,128)(2,1)S(1)}, bf16[256,256]{1,0:T(8,128)(2,1)S(1)}, u32[]{:S(2)}, u32[]{:S(2)}) collective-permute-start(bf16[256,256]{1,0:T(8,128)(2,1)S(1)} %get-tuple-element.21), channel_id=1, source_target_pairs={{0,12},{2,14},{4,0},{6,2},{8,4},{10,6},{12,8},{14,10},{1,13},{3,15... | collective-permute-start | bytes 393224 | tf_op jit(solution)/shard_map/ppermute | solution.py:347
  39.3 0.0 collective-permute-done.7.refs_2_
  39.3 1.4 %collective-permute-start.12 = (bf16[256,256]{1,0:T(8,128)(2,1)S(1)}, bf16[256,256]{1,0:T(8,128)(2,1)S(1)}, u32[]{:S(2)}, u32[]{:S(2)}) collective-permute-start(bf16[256,256]{1,0:T(8,128)(2,1)S(1)} %get-tuple-element.22), channel_id=1, source_target_pairs={{0,14},{2,12},{4,2},{6,0},{8,6},{10,4},{12,10},{14,8},{1,15},{3,13... | collective-permute-start | bytes 393224 | tf_op jit(solution)/shard_map/ppermute | solution.py:347
  40.7 0.4 compare_convert_fusion.refs_8_
  41.1 0.0 collective-permute-done.8.refs_3_
  41.1 2.0 %collective-permute-done.9.refs_4_ = bf16[256,256]{1,0:T(8,128)(2,1)S(1)} collective-permute-done((bf16[256,256]{1,0:T(8,128)(2,1)S(1)}, bf16[256,256]{1,0:T(8,128)(2,1)S(1)}, u32[]{:S(2)}, u32[]{:S(2)}) %collective-permute-start.9) | collective-permute-done | bytes 131104 | tf_op jit(solution)/shard_map/ppermute | solution.py:347
  43.1 11.0 %collective-permute-done.10.refs_5_ = bf16[256,256]{1,0:T(8,128)(2,1)S(1)} collective-permute-done((bf16[256,256]{1,0:T(8,128)(2,1)S(1)}, bf16[256,256]{1,0:T(8,128)(2,1)S(1)}, u32[]{:S(2)}, u32[]{:S(2)}) %collective-permute-start.10) | collective-permute-done | bytes 131104 | tf_op jit(solution)/shard_map/ppermute | solution.py:347
  54.1 1.2 %collective-permute-done.11.refs_6_ = bf16[256,256]{1,0:T(8,128)(2,1)S(1)} collective-permute-done((bf16[256,256]{1,0:T(8,128)(2,1)S(1)}, bf16[256,256]{1,0:T(8,128)(2,1)S(1)}, u32[]{:S(2)}, u32[]{:S(2)}) %collective-permute-start.11) | collective-permute-done | bytes 131104 | tf_op jit(solution)/shard_map/ppermute | solution.py:347
  55.4 3.7 %collective-permute-done.12.refs_7_ = bf16[256,256]{1,0:T(8,128)(2,1)S(1)} collective-permute-done((bf16[256,256]{1,0:T(8,128)(2,1)S(1)}, bf16[256,256]{1,0:T(8,128)(2,1)S(1)}, u32[]{:S(2)}, u32[]{:S(2)}) %collective-permute-start.12) | collective-permute-done | bytes 131104 | tf_op jit(solution)/shard_map/ppermute | solution.py:347
  59.1 1.3 %order.1 = (bf16[512,1024]{1,0:T(8,128)(2,1)S(1)}, bf16[512,1024]{1,0:T(8,128)(2,1)S(1)}) custom-call(bf16[256,256]{1,0:T(8,128)(2,1)S(1)} %get-tuple-element.15.refs_0_, bf16[256,256]{1,0:T(8,128)(2,1)S(1)} %collective-permute-done.6.refs_1_, bf16[256,256]{1,0:T(8,128)(2,1)S(1)} %collective-permute-done.7.refs_2_, ...), custom_call_target="tpu_custom_call" | custom-call | tf_op jit(solution)/shard_map/order/pallas_call | solution.py:224
  60.4 0.9 %collective-permute-start.13 = (bf16[512,1024]{1,0:T(8,128)(2,1)S(1)}, bf16[512,1024]{1,0:T(8,128)(2,1)S(1)}, u32[]{:S(2)}, u32[]{:S(2)}) collective-permute-start(bf16[512,1024]{1,0:T(8,128)(2,1)S(1)} %get-tuple-element.23.own), channel_id=1, source_target_pairs={{0,1},{1,0},{2,3},{3,2},{4,5},{5,4},{6,7},{7,6},{8,9},{9,8},{10,11... | collective-permute-start | bytes 3145736 | tf_op jit(solution)/shard_map/ppermute | solution.py:349
  61.3 2.3 %collective-permute-done.13.other = bf16[512,1024]{1,0:T(8,128)(2,1)S(1)} collective-permute-done((bf16[512,1024]{1,0:T(8,128)(2,1)S(1)}, bf16[512,1024]{1,0:T(8,128)(2,1)S(1)}, u32[]{:S(2)}, u32[]{:S(2)}) %collective-permute-start.13) | collective-permute-done | bytes 1048608 | tf_op jit(solution)/shard_map/ppermute | solution.py:349
  63.6 11.4 %gram.1 = f32[2,32,1024,128]{3,2,1,0:T(8,128)} custom-call(s32[1]{0:T(128)} %bitcast.pol_ref, bf16[512,1024]{1,0:T(8,128)(2,1)S(1)} %get-tuple-element.23.own, bf16[512,1024]{1,0:T(8,128)(2,1)S(1)} %get-tuple-element.24.turned, bf16[512,1024]{1,0:T(8,128)(2,1)S(1)} %collective-permute-done.13.other), custom_call_target="tpu_custom_call" | custom-call | tf_op jit(solution)/shard_map/gram/pallas_call | solution.py:287
  (10 shorter events, 0.1 us)
Async XLA Ops:
  0.0 15.9 %copy-start.6 = (f32[16,256]{1,0:T(8,128)S(1)}, f32[16,256]{1,0:T(8,128)}, u32[]{:S(2)}) copy-start(f32[16,256]{1,0:T(8,128)} %constant.118.clone.refs_6_) | copy-start | bytes 49156
  0.0 15.9 %copy-start.4 = (bf16[512,256]{1,0:T(8,128)(2,1)S(1)}, bf16[512,256]{1,0:T(8,128)(2,1)}, u32[]{:S(2)}) copy-start(bf16[512,256]{1,0:T(8,128)(2,1)} %constant.117.clone.refs_8_) | copy-start | bytes 786436
  0.0 15.9 %copy-start.5 = (bf16[512,256]{1,0:T(8,128)(2,1)S(1)}, bf16[512,256]{1,0:T(8,128)(2,1)}, u32[]{:S(2)}) copy-start(bf16[512,256]{1,0:T(8,128)(2,1)} %constant.116.clone.refs_7_) | copy-start | bytes 786436
  0.0 15.9 %copy-start.2 = (bf16[1,128,4096]{2,1,0:T(8,128)(2,1)S(1)}, bf16[1,128,4096]{2,1,0:T(8,128)(2,1)}, u32[]{:S(2)}) copy-start(bf16[1,128,4096]{2,1,0:T(8,128)(2,1)} %refs_0_.3) | copy-start | bytes 3145732
  0.0 15.9 %copy-start.7 = (s32[1,128]{1,0:T(1,128)S(1)}, s32[1,128]{1,0:T(1,128)}, u32[]{:S(2)}) copy-start(s32[1,128]{1,0:T(1,128)} %refs_5_.3) | copy-start | bytes 1540
  0.0 15.9 %copy-start.3 = (f32[16,4096]{1,0:T(8,128)S(1)}, f32[16,4096]{1,0:T(8,128)}, u32[]{:S(2)}) copy-start(f32[16,4096]{1,0:T(8,128)} %refs_4_.3) | copy-start | bytes 786436
  2.2 12.6 %collective-permute-start.5 = (bf16[16,4096]{1,0:T(8,128)(2,1)}, bf16[16,4096]{1,0:T(8,128)(2,1)S(1)}, u32[]{:S(2)}, u32[]{:S(2)}) collective-permute-start(bf16[16,4096]{1,0:T(8,128)(2,1)} %get-tuple-element.29), channel_id=1, source_target_pairs={{0,4},{4,0},{8,12},{12,8},{1,5},{5,1},{9,13},{13,9},{2,6},{6,2},{1... | collective-permute-start | bytes 393224 | tf_op jit(solution)/shard_map/ppermute | solution.py:325
  2.2 12.9 %collective-permute-start.4 = (bf16[16,4096]{1,0:T(8,128)(2,1)S(1)}, bf16[16,4096]{1,0:T(8,128)(2,1)S(1)}, u32[]{:S(2)}, u32[]{:S(2)}) collective-permute-start(bf16[16,4096]{1,0:T(8,128)(2,1)S(1)} %get-tuple-element.30), channel_id=1, source_target_pairs={{0,8},{4,12},{8,0},{12,4},{1,9},{5,13},{9,1},{13,5},{2,10},{6,14},... | collective-permute-start | bytes 393224 | tf_op jit(solution)/shard_map/ppermute | solution.py:325
  4.7 11.3 %collective-permute-start.3 = (bf16[16,4096]{1,0:T(8,128)(2,1)S(1)}, bf16[16,4096]{1,0:T(8,128)(2,1)S(1)}, u32[]{:S(2)}, u32[]{:S(2)}) collective-permute-start(bf16[16,4096]{1,0:T(8,128)(2,1)S(1)} %get-tuple-element.31), channel_id=1, source_target_pairs={{0,12},{4,8},{8,4},{12,0},{1,13},{5,9},{9,5},{13,1},{2,14},{6,10},... | collective-permute-start | bytes 393224 | tf_op jit(solution)/shard_map/ppermute | solution.py:325
  5.6 16.1 %collective-permute-start.2 = (bf16[16,4096]{1,0:T(8,128)(2,1)}, bf16[16,4096]{1,0:T(8,128)(2,1)S(1)}, u32[]{:S(2)}, u32[]{:S(2)}) collective-permute-start(bf16[16,4096]{1,0:T(8,128)(2,1)} %get-tuple-element.32), channel_id=1, source_target_pairs={{0,4},{4,0},{8,12},{12,8},{1,5},{5,1},{9,13},{13,9},{2,6},{6,2},{1... | collective-permute-start | bytes 393224 | tf_op jit(solution)/shard_map/ppermute | solution.py:325
  6.7 17.1 %collective-permute-start.1 = (bf16[16,4096]{1,0:T(8,128)(2,1)}, bf16[16,4096]{1,0:T(8,128)(2,1)S(1)}, u32[]{:S(2)}, u32[]{:S(2)}) collective-permute-start(bf16[16,4096]{1,0:T(8,128)(2,1)} %get-tuple-element.33), channel_id=1, source_target_pairs={{0,8},{4,12},{8,0},{12,4},{1,9},{5,13},{9,1},{13,5},{2,10},{6,14},... | collective-permute-start | bytes 393224 | tf_op jit(solution)/shard_map/ppermute | solution.py:325
  14.8 12.0 %collective-permute-start = (bf16[16,4096]{1,0:T(8,128)(2,1)S(1)}, bf16[16,4096]{1,0:T(8,128)(2,1)S(1)}, u32[]{:S(2)}, u32[]{:S(2)}) collective-permute-start(bf16[16,4096]{1,0:T(8,128)(2,1)S(1)} %get-tuple-element.34), channel_id=1, source_target_pairs={{0,12},{4,8},{8,4},{12,0},{1,13},{5,9},{9,5},{13,1},{2,14},{6,10},... | collective-permute-start | bytes 393224 | tf_op jit(solution)/shard_map/ppermute | solution.py:325
  16.0 3.4 %copy-start = (bf16[2048,2048]{1,0:T(8,128)(2,1)S(1)}, bf16[2048,2048]{1,0:T(8,128)(2,1)}, u32[]{:S(2)}) copy-start(bf16[2048,2048]{1,0:T(8,128)(2,1)} %fusion.refs_9_.refs_10_) | copy-start | bytes 25165828
  19.3 7.5 %copy-start.1 = (bf16[2048,2048]{1,0:T(8,128)(2,1)S(1)}, bf16[2048,2048]{1,0:T(8,128)(2,1)}, u32[]{:S(2)}) copy-start(bf16[2048,2048]{1,0:T(8,128)(2,1)} %fusion.refs_9_.refs_10_) | copy-start | bytes 25165828
  21.6 12.8 %copy-start.8 = (s32[256]{0:T(256)S(1)}, s32[256]{0:T(256)}, u32[]{:S(2)}) copy-start(s32[256]{0:T(256)} %param.11) | copy-start | bytes 3076
  31.3 6.5 %collective-permute-start.6 = (bf16[256,256]{1,0:T(8,128)(2,1)S(1)}, bf16[256,256]{1,0:T(8,128)(2,1)S(1)}, u32[]{:S(2)}, u32[]{:S(2)}) collective-permute-start(bf16[256,256]{1,0:T(8,128)(2,1)S(1)} %get-tuple-element.16), channel_id=1, source_target_pairs={{0,2},{2,0},{4,6},{6,4},{8,10},{10,8},{12,14},{14,12},{1,3},{3,1},... | collective-permute-start | bytes 393224 | tf_op jit(solution)/shard_map/ppermute | solution.py:347
  32.6 6.7 %collective-permute-start.7 = (bf16[256,256]{1,0:T(8,128)(2,1)S(1)}, bf16[256,256]{1,0:T(8,128)(2,1)S(1)}, u32[]{:S(2)}, u32[]{:S(2)}) collective-permute-start(bf16[256,256]{1,0:T(8,128)(2,1)S(1)} %get-tuple-element.17), channel_id=1, source_target_pairs={{0,4},{2,6},{4,8},{6,10},{8,12},{10,14},{12,0},{14,2},{1,5},{3,7},... | collective-permute-start | bytes 393224 | tf_op jit(solution)/shard_map/ppermute | solution.py:347
  34.6 6.6 %collective-permute-start.8 = (bf16[256,256]{1,0:T(8,128)(2,1)S(1)}, bf16[256,256]{1,0:T(8,128)(2,1)S(1)}, u32[]{:S(2)}, u32[]{:S(2)}) collective-permute-start(bf16[256,256]{1,0:T(8,128)(2,1)S(1)} %get-tuple-element.18), channel_id=1, source_target_pairs={{0,6},{2,4},{4,10},{6,8},{8,14},{10,12},{12,2},{14,0},{1,7},{3,5},... | collective-permute-start | bytes 393224 | tf_op jit(solution)/shard_map/ppermute | solution.py:347
  34.6 8.6 %collective-permute-start.9 = (bf16[256,256]{1,0:T(8,128)(2,1)S(1)}, bf16[256,256]{1,0:T(8,128)(2,1)S(1)}, u32[]{:S(2)}, u32[]{:S(2)}) collective-permute-start(bf16[256,256]{1,0:T(8,128)(2,1)S(1)} %get-tuple-element.19), channel_id=1, source_target_pairs={{0,8},{2,10},{4,12},{6,14},{8,0},{10,2},{12,4},{14,6},{1,9},{3,11}... | collective-permute-start | bytes 393224 | tf_op jit(solution)/shard_map/ppermute | solution.py:347
  36.2 17.9 %collective-permute-start.10 = (bf16[256,256]{1,0:T(8,128)(2,1)S(1)}, bf16[256,256]{1,0:T(8,128)(2,1)S(1)}, u32[]{:S(2)}, u32[]{:S(2)}) collective-permute-start(bf16[256,256]{1,0:T(8,128)(2,1)S(1)} %get-tuple-element.20), channel_id=1, source_target_pairs={{0,10},{2,8},{4,14},{6,12},{8,2},{10,0},{12,6},{14,4},{1,11},{3,9}... | collective-permute-start | bytes 393224 | tf_op jit(solution)/shard_map/ppermute | solution.py:347
  37.8 17.5 %collective-permute-start.11 = (bf16[256,256]{1,0:T(8,128)(2,1)S(1)}, bf16[256,256]{1,0:T(8,128)(2,1)S(1)}, u32[]{:S(2)}, u32[]{:S(2)}) collective-permute-start(bf16[256,256]{1,0:T(8,128)(2,1)S(1)} %get-tuple-element.21), channel_id=1, source_target_pairs={{0,12},{2,14},{4,0},{6,2},{8,4},{10,6},{12,8},{14,10},{1,13},{3,15... | collective-permute-start | bytes 393224 | tf_op jit(solution)/shard_map/ppermute | solution.py:347
  39.3 19.8 %collective-permute-start.12 = (bf16[256,256]{1,0:T(8,128)(2,1)S(1)}, bf16[256,256]{1,0:T(8,128)(2,1)S(1)}, u32[]{:S(2)}, u32[]{:S(2)}) collective-permute-start(bf16[256,256]{1,0:T(8,128)(2,1)S(1)} %get-tuple-element.22), channel_id=1, source_target_pairs={{0,14},{2,12},{4,2},{6,0},{8,6},{10,4},{12,10},{14,8},{1,15},{3,13... | collective-permute-start | bytes 393224 | tf_op jit(solution)/shard_map/ppermute | solution.py:347
  60.4 3.2 %collective-permute-start.13 = (bf16[512,1024]{1,0:T(8,128)(2,1)S(1)}, bf16[512,1024]{1,0:T(8,128)(2,1)S(1)}, u32[]{:S(2)}, u32[]{:S(2)}) collective-permute-start(bf16[512,1024]{1,0:T(8,128)(2,1)S(1)} %get-tuple-element.23.own), channel_id=1, source_target_pairs={{0,1},{1,0},{2,3},{3,2},{4,5},{5,4},{6,7},{7,6},{8,9},{9,8},{10,11... | collective-permute-start | bytes 3145736 | tf_op jit(solution)/shard_map/ppermute | solution.py:349

commit v6 on v5

--- a/solution.py
+++ b/solution.py
@@ -326,7 +326,8 @@
     lane_of = (chan_map % RAD) * HALF + chan_map // RAD
     lane_of = rolled(rolled(lane_of.reshape(chans, stns, slots), 0, chan, chans), 1, stn, stns)
     select = onehot(lane_of.reshape(CH), jnp.arange(CH, dtype=jnp.int32))
-    dist = jnp.arange(owners, dtype=jnp.int32)
+    far = [*range(stns, owners), *range(1, stns)]
+    dist = jnp.asarray(np.array([0, *far], np.int32))
     row0 = (stn - dist % stns) % stns * here + (chan - dist // stns) % chans * rows
     col = station_slot[None, :] + stations * jnp.arange(frames, dtype=jnp.int32)[:, None]
     prior, place = [], []
@@ -341,7 +342,7 @@
         place.append(row.reshape(owners, -1))
     place = onehot(jnp.concatenate(place, axis=1).reshape(-1), col.reshape(-1))
     got = [pieces[0]]
-    for d in range(1, owners):
+    for d in far:
         dc, ds = divmod(d, stns)
         route = [(i * stns + j, (i + dc) % chans * stns + (j + ds) % stns) for i in range(chans) for j in range(stns)]
         got.append(lax.ppermute(pieces[d], ("chan", "stn"), route))

time: 75.2 us -> 75.9 us (level)
  starting transfers between devices: 16.3 us -> 17.5 us
  waiting for transfers between devices: 26.3 us -> 25.2 us
    ppermute x1, starting transfers between devices: 0.93 us -> 2.07 us  [fast_body(): other = lax.ppermute(own, 'pol', [(0, 1), (1, 0)])]
    ppermute x7, waiting for transfers between devices: 18 us -> 16.9 us  [fast_body(): got.append(lax.ppermute(pieces[d], ('chan', 'stn'), route))]
    unnamed x20 -> x24, local copies, waits for them, and re-layouts: 3.42 us -> 3.44 us
  transfers between devices with their start and end apart: 14 -> 14, of which waited for: 8 -> 7; matrix products, arithmetic and copies ran while one was open for 10% -> 10% of each run, Pallas kernels for 3% -> 3%
where the time goes in v6:
time: 75.9 us; the launch traced here: 75.1 us
  waiting for transfers between devices  25.2 us (33%)
  Pallas kernels  19.4 us (26%)
  starting transfers between devices  17.5 us (23%)
  local copies, waits for them, and re-layouts  6.61 us (9%)
  other arithmetic  6.22 us (8%)
    ppermute x7, waiting for transfers between devices, fast_body(): got.append(lax.ppermute(pieces[d], ('chan', 'stn'), route))  16.9 us
    pallas_call x1, Pallas kernels, gram(): pl.pallas_call(functools.partial(gram_kernel, frames, start, 1.0 / (frame...  11.4 us
    ppermute x7, starting transfers between devices, fast_body(): got.append(lax.ppermute(pieces[d], ('chan', 'stn'), route))  9.23 us
    pallas_call x2, Pallas kernels, filterbank(): pl.pallas_call(functools.partial(filterbank_kernel, frames, share, group,...  6.66 us
    ppermute x6, starting transfers between devices, fast_body(): lax.ppermute(share, 'chan', [(i, i ^ d) for i in range(chans)])  6.15 us
    ppermute x6, waiting for transfers between devices, fast_body(): lax.ppermute(share, 'chan', [(i, i ^ d) for i in range(chans)])  6.06 us
    convert_element_type x2, other arithmetic, onehot(): return (rows[:, None] == cols[None, :]).astype(bf16)  5.22 us
    unnamed x24, local copies, waits for them, and re-layouts  3.44 us
  transfers between devices with their start and end apart: 14, of which 7 were waited for; matrix products, arithmetic and copies ran while one was open for 10% of the time, Pallas kernels for 3%

profile of v6, /device:TPU:9, one launch (start us, length us, event | category | flops | bytes accessed | tf_op | source)
XLA Modules:
  0.0 75.1 jit_solution(1427731531001390483)
XLA Ops:
  0.0 0.0 copy-start.9
  0.0 0.0 copy-start.4
  0.0 0.0 copy-start.5
  0.0 0.0 copy-start.2
  0.0 0.0 copy-start.7
  0.1 0.0 copy-start.3
  0.1 1.4 %fusion.16 = (bf16[4,16,4096]{2,1,0:T(8,128)(2,1)S(1)}, bf16[4,16,4096]{2,1,0:T(8,128)(2,1)S(1)}) fusion(bf16[4,32,4096]{2,1,0:T(8,128)(2,1)} %bitcast.28), kind=kLoop, calls=%fused_computation.47 | loop fusion | bytes 2097152 | tf_op jit(solution)/shard_map/slice | solution.py:324
  1.5 0.7 dynamic-slice_bitcast_fusion
  2.2 0.0 collective-permute-start.5
  2.2 2.5 %collective-permute-start.4 = (bf16[16,4096]{1,0:T(8,128)(2,1)S(1)}, bf16[16,4096]{1,0:T(8,128)(2,1)S(1)}, u32[]{:S(2)}, u32[]{:S(2)}) collective-permute-start(bf16[16,4096]{1,0:T(8,128)(2,1)S(1)} %get-tuple-element.30), channel_id=1, source_target_pairs={{0,8},{4,12},{8,0},{12,4},{1,9},{5,13},{9,1},{13,5},{2,10},{6,14},... | collective-permute-start | bytes 393224 | tf_op jit(solution)/shard_map/ppermute | solution.py:325
  4.7 0.2 collective-permute-start.3
  4.9 0.7 dynamic-slice_bitcast_fusion.3
  5.6 1.1 %collective-permute-start.2 = (bf16[16,4096]{1,0:T(8,128)(2,1)}, bf16[16,4096]{1,0:T(8,128)(2,1)S(1)}, u32[]{:S(2)}, u32[]{:S(2)}) collective-permute-start(bf16[16,4096]{1,0:T(8,128)(2,1)} %get-tuple-element.32), channel_id=1, source_target_pairs={{0,4},{4,0},{8,12},{12,8},{1,5},{5,1},{9,13},{13,9},{2,6},{6,2},{1... | collective-permute-start | bytes 393224 | tf_op jit(solution)/shard_map/ppermute | solution.py:325
  6.7 2.1 %collective-permute-start.1 = (bf16[16,4096]{1,0:T(8,128)(2,1)}, bf16[16,4096]{1,0:T(8,128)(2,1)S(1)}, u32[]{:S(2)}, u32[]{:S(2)}) collective-permute-start(bf16[16,4096]{1,0:T(8,128)(2,1)} %get-tuple-element.33), channel_id=1, source_target_pairs={{0,8},{4,12},{8,0},{12,4},{1,9},{5,13},{9,1},{13,5},{2,10},{6,14},... | collective-permute-start | bytes 393224 | tf_op jit(solution)/shard_map/ppermute | solution.py:325
  8.8 0.1 add.165
  8.9 0.1 add.166
  9.0 0.7 fusion.2
  9.8 4.8 %fusion.refs_9_.refs_10_ = bf16[2048,2048]{1,0:T(8,128)(2,1)} fusion(s32[2048]{0:T(1024)S(1)} %bitcast.29), kind=kLoop, calls=%fused_computation.1 | loop fusion | flops 8388608 | bytes 8396800 | tf_op jit(solution)/shard_map/convert_element_type | solution.py:27
  14.6 0.0 copy-done.9
  14.6 0.0 copy-done.10
  14.6 0.1 iota_add_fusion
  14.7 0.1 add.174
  14.8 0.1 add.164
  14.9 0.0 collective-permute-done.5.refs_3_
  14.9 0.3 collective-permute-start
  15.2 0.0 collective-permute-done.4.refs_2_
  15.2 0.8 %collective-permute-done.3.refs_1_ = bf16[16,4096]{1,0:T(8,128)(2,1)S(1)} collective-permute-done((bf16[16,4096]{1,0:T(8,128)(2,1)S(1)}, bf16[16,4096]{1,0:T(8,128)(2,1)S(1)}, u32[]{:S(2)}, u32[]{:S(2)}) %collective-permute-start.3) | collective-permute-done | bytes 131104 | tf_op jit(solution)/shard_map/ppermute | solution.py:325
  16.0 0.0 copy-done.6
  16.0 0.0 copy-done.4
  16.0 0.0 copy-done.5
  16.0 0.0 copy-done.2
  16.0 0.0 copy-done.7
  16.0 0.0 copy-done.3
  16.0 0.0 copy-start
  16.0 3.4 %copy-done = bf16[2048,2048]{1,0:T(8,128)(2,1)S(1)} copy-done((bf16[2048,2048]{1,0:T(8,128)(2,1)S(1)}, bf16[2048,2048]{1,0:T(8,128)(2,1)}, u32[]{:S(2)}) %copy-start) | copy-done | bytes 8388632
  19.4 2.2 %transform.1.refs_9_ = bf16[16,128,256]{2,1,0:T(8,128)(2,1)S(1)} custom-call(s32[1]{0:T(128)} %bitcast.1.chan_ref, bf16[1,128,4096]{2,1,0:T(8,128)(2,1)S(1)} %copy-done.2, bf16[16,4096]{1,0:T(8,128)(2,1)S(1)} %collective-permute-done.3.refs_1_, bf16[16,4096]{1,0:T(8,128)(2,1)S(1)} %collective-permute-done.4.refs_2_, ...), custom_call_target="tpu_custom_call" | custom-call | tf_op jit(solution)/shard_map/transform/pallas_call | solution.py:188
  21.6 0.0 copy-start.8
  21.6 0.0 collective-permute-done.2.refs_3_
  21.7 2.2 %collective-permute-done.1.refs_2_ = bf16[16,4096]{1,0:T(8,128)(2,1)S(1)} collective-permute-done((bf16[16,4096]{1,0:T(8,128)(2,1)}, bf16[16,4096]{1,0:T(8,128)(2,1)S(1)}, u32[]{:S(2)}, u32[]{:S(2)}) %collective-permute-start.1) | collective-permute-done | bytes 131104 | tf_op jit(solution)/shard_map/ppermute | solution.py:325
  23.8 3.1 %collective-permute-done.refs_1_ = bf16[16,4096]{1,0:T(8,128)(2,1)S(1)} collective-permute-done((bf16[16,4096]{1,0:T(8,128)(2,1)S(1)}, bf16[16,4096]{1,0:T(8,128)(2,1)S(1)}, u32[]{:S(2)}, u32[]{:S(2)}) %collective-permute-start) | collective-permute-done | bytes 131104 | tf_op jit(solution)/shard_map/ppermute | solution.py:325
  26.9 0.0 copy-done.1
  26.9 4.4 %filterbank.1 = (bf16[256,256]{1,0:T(8,128)(2,1)S(1)}, bf16[256,256]{1,0:T(8,128)(2,1)S(1)}, bf16[256,256]{1,0:T(8,128)(2,1)S(1)}, bf16[256,256]{1,0:T(8,128)(2,...) custom-call(s32[1]{0:T(128)} %bitcast.1.chan_ref, ...), custom_call_target="tpu_custom_call" | custom-call | tf_op jit(solution)/shard_map/filterbank/pallas_call | solution.py:188
  31.3 1.9 %collective-permute-start.6 = (bf16[256,256]{1,0:T(8,128)(2,1)S(1)}, bf16[256,256]{1,0:T(8,128)(2,1)S(1)}, u32[]{:S(2)}, u32[]{:S(2)}) collective-permute-start(bf16[256,256]{1,0:T(8,128)(2,1)S(1)} %get-tuple-element.16), channel_id=1, source_target_pairs={{0,4},{2,6},{4,8},{6,10},{8,12},{10,14},{12,0},{14,2},{1,5},{3,7},... | collective-permute-start | bytes 393224 | tf_op jit(solution)/shard_map/ppermute | solution.py:348
  33.2 1.0 %collective-permute-start.7 = (bf16[256,256]{1,0:T(8,128)(2,1)S(1)}, bf16[256,256]{1,0:T(8,128)(2,1)S(1)}, u32[]{:S(2)}, u32[]{:S(2)}) collective-permute-start(bf16[256,256]{1,0:T(8,128)(2,1)S(1)} %get-tuple-element.17), channel_id=1, source_target_pairs={{0,6},{2,4},{4,10},{6,8},{8,14},{10,12},{12,2},{14,0},{1,7},{3,5},... | collective-permute-start | bytes 393224 | tf_op jit(solution)/shard_map/ppermute | solution.py:348
  34.2 0.0 copy-done.8
  34.2 0.1 add_bitcast_fusion.1
  34.3 0.1 add_bitcast_fusion
  34.4 1.6 %collective-permute-start.8 = (bf16[256,256]{1,0:T(8,128)(2,1)S(1)}, bf16[256,256]{1,0:T(8,128)(2,1)S(1)}, u32[]{:S(2)}, u32[]{:S(2)}) collective-permute-start(bf16[256,256]{1,0:T(8,128)(2,1)S(1)} %get-tuple-element.18), channel_id=1, source_target_pairs={{0,8},{2,10},{4,12},{6,14},{8,0},{10,2},{12,4},{14,6},{1,9},{3,11}... | collective-permute-start | bytes 393224 | tf_op jit(solution)/shard_map/ppermute | solution.py:348
  36.0 0.7 collective-permute-start.9
  36.7 1.4 %collective-permute-start.10 = (bf16[256,256]{1,0:T(8,128)(2,1)S(1)}, bf16[256,256]{1,0:T(8,128)(2,1)S(1)}, u32[]{:S(2)}, u32[]{:S(2)}) collective-permute-start(bf16[256,256]{1,0:T(8,128)(2,1)S(1)} %get-tuple-element.20), channel_id=1, source_target_pairs={{0,12},{2,14},{4,0},{6,2},{8,4},{10,6},{12,8},{14,10},{1,13},{3,15... | collective-permute-start | bytes 393224 | tf_op jit(solution)/shard_map/ppermute | solution.py:348
  38.1 0.0 collective-permute-done.6.refs_1_
  38.1 2.4 %collective-permute-start.11 = (bf16[256,256]{1,0:T(8,128)(2,1)S(1)}, bf16[256,256]{1,0:T(8,128)(2,1)S(1)}, u32[]{:S(2)}, u32[]{:S(2)}) collective-permute-start(bf16[256,256]{1,0:T(8,128)(2,1)S(1)} %get-tuple-element.21), channel_id=1, source_target_pairs={{0,14},{2,12},{4,2},{6,0},{8,6},{10,4},{12,10},{14,8},{1,15},{3,13... | collective-permute-start | bytes 393224 | tf_op jit(solution)/shard_map/ppermute | solution.py:348
  40.5 0.0 collective-permute-done.7.refs_2_
  40.5 0.3 collective-permute-start.12
  40.7 0.4 compare_convert_fusion.refs_8_
  41.1 0.0 collective-permute-done.8.refs_3_
  41.2 11.4 %collective-permute-done.9.refs_4_ = bf16[256,256]{1,0:T(8,128)(2,1)S(1)} collective-permute-done((bf16[256,256]{1,0:T(8,128)(2,1)S(1)}, bf16[256,256]{1,0:T(8,128)(2,1)S(1)}, u32[]{:S(2)}, u32[]{:S(2)}) %collective-permute-start.9) | collective-permute-done | bytes 131104 | tf_op jit(solution)/shard_map/ppermute | solution.py:348
  52.5 2.7 %collective-permute-done.10.refs_5_ = bf16[256,256]{1,0:T(8,128)(2,1)S(1)} collective-permute-done((bf16[256,256]{1,0:T(8,128)(2,1)S(1)}, bf16[256,256]{1,0:T(8,128)(2,1)S(1)}, u32[]{:S(2)}, u32[]{:S(2)}) %collective-permute-start.10) | collective-permute-done | bytes 131104 | tf_op jit(solution)/shard_map/ppermute | solution.py:348
  55.2 2.8 %collective-permute-done.11.refs_6_ = bf16[256,256]{1,0:T(8,128)(2,1)S(1)} collective-permute-done((bf16[256,256]{1,0:T(8,128)(2,1)S(1)}, bf16[256,256]{1,0:T(8,128)(2,1)S(1)}, u32[]{:S(2)}, u32[]{:S(2)}) %collective-permute-start.11) | collective-permute-done | bytes 131104 | tf_op jit(solution)/shard_map/ppermute | solution.py:348
  58.0 0.0 collective-permute-done.12.refs_7_
  58.0 1.3 %order.1 = (bf16[512,1024]{1,0:T(8,128)(2,1)S(1)}, bf16[512,1024]{1,0:T(8,128)(2,1)S(1)}) custom-call(bf16[256,256]{1,0:T(8,128)(2,1)S(1)} %get-tuple-element.15.refs_0_, bf16[256,256]{1,0:T(8,128)(2,1)S(1)} %collective-permute-done.6.refs_1_, bf16[256,256]{1,0:T(8,128)(2,1)S(1)} %collective-permute-done.7.refs_2_, ...), custom_call_target="tpu_custom_call" | custom-call | tf_op jit(solution)/shard_map/order/pallas_call | solution.py:224
  59.3 2.1 %collective-permute-start.13 = (bf16[512,1024]{1,0:T(8,128)(2,1)S(1)}, bf16[512,1024]{1,0:T(8,128)(2,1)S(1)}, u32[]{:S(2)}, u32[]{:S(2)}) collective-permute-start(bf16[512,1024]{1,0:T(8,128)(2,1)S(1)} %get-tuple-element.23.own), channel_id=1, source_target_pairs={{0,1},{1,0},{2,3},{3,2},{4,5},{5,4},{6,7},{7,6},{8,9},{9,8},{10,11... | collective-permute-start | bytes 3145736 | tf_op jit(solution)/shard_map/ppermute | solution.py:350
  61.4 2.3 %collective-permute-done.13.other = bf16[512,1024]{1,0:T(8,128)(2,1)S(1)} collective-permute-done((bf16[512,1024]{1,0:T(8,128)(2,1)S(1)}, bf16[512,1024]{1,0:T(8,128)(2,1)S(1)}, u32[]{:S(2)}, u32[]{:S(2)}) %collective-permute-start.13) | collective-permute-done | bytes 1048608 | tf_op jit(solution)/shard_map/ppermute | solution.py:350
  63.7 11.4 %gram.1 = f32[2,32,1024,128]{3,2,1,0:T(8,128)} custom-call(s32[1]{0:T(128)} %bitcast.pol_ref, bf16[512,1024]{1,0:T(8,128)(2,1)S(1)} %get-tuple-element.23.own, bf16[512,1024]{1,0:T(8,128)(2,1)S(1)} %get-tuple-element.24.turned, bf16[512,1024]{1,0:T(8,128)(2,1)S(1)} %collective-permute-done.13.other), custom_call_target="tpu_custom_call" | custom-call | tf_op jit(solution)/shard_map/gram/pallas_call | solution.py:287
  (13 shorter events, 0.1 us)
Async XLA Ops:
  0.0 14.6 %copy-start.9 = (s32[8]{0:T(128)S(1)}, s32[8]{0:T(128)}, u32[]{:S(2)}) copy-start(s32[8]{0:T(128)} %constant.142) | copy-start | bytes 100
  0.0 14.6 %copy-start.10 = (s32[8]{0:T(128)S(1)}, s32[8]{0:T(128)}, u32[]{:S(2)}) copy-start(s32[8]{0:T(128)} %constant.141) | copy-start | bytes 100
  0.0 16.0 %copy-start.6 = (f32[16,256]{1,0:T(8,128)S(1)}, f32[16,256]{1,0:T(8,128)}, u32[]{:S(2)}) copy-start(f32[16,256]{1,0:T(8,128)} %constant.119.clone.refs_6_) | copy-start | bytes 49156
  0.0 16.0 %copy-start.4 = (bf16[512,256]{1,0:T(8,128)(2,1)S(1)}, bf16[512,256]{1,0:T(8,128)(2,1)}, u32[]{:S(2)}) copy-start(bf16[512,256]{1,0:T(8,128)(2,1)} %constant.118.clone.refs_8_) | copy-start | bytes 786436
  0.0 15.9 %copy-start.5 = (bf16[512,256]{1,0:T(8,128)(2,1)S(1)}, bf16[512,256]{1,0:T(8,128)(2,1)}, u32[]{:S(2)}) copy-start(bf16[512,256]{1,0:T(8,128)(2,1)} %constant.117.clone.refs_7_) | copy-start | bytes 786436
  0.0 15.9 %copy-start.2 = (bf16[1,128,4096]{2,1,0:T(8,128)(2,1)S(1)}, bf16[1,128,4096]{2,1,0:T(8,128)(2,1)}, u32[]{:S(2)}) copy-start(bf16[1,128,4096]{2,1,0:T(8,128)(2,1)} %refs_0_.3) | copy-start | bytes 3145732
  0.0 15.9 %copy-start.7 = (s32[1,128]{1,0:T(1,128)S(1)}, s32[1,128]{1,0:T(1,128)}, u32[]{:S(2)}) copy-start(s32[1,128]{1,0:T(1,128)} %refs_5_.3) | copy-start | bytes 1540
  0.1 15.9 %copy-start.3 = (f32[16,4096]{1,0:T(8,128)S(1)}, f32[16,4096]{1,0:T(8,128)}, u32[]{:S(2)}) copy-start(f32[16,4096]{1,0:T(8,128)} %refs_4_.3) | copy-start | bytes 786436
  2.2 12.6 %collective-permute-start.5 = (bf16[16,4096]{1,0:T(8,128)(2,1)}, bf16[16,4096]{1,0:T(8,128)(2,1)S(1)}, u32[]{:S(2)}, u32[]{:S(2)}) collective-permute-start(bf16[16,4096]{1,0:T(8,128)(2,1)} %get-tuple-element.29), channel_id=1, source_target_pairs={{0,4},{4,0},{8,12},{12,8},{1,5},{5,1},{9,13},{13,9},{2,6},{6,2},{1... | collective-permute-start | bytes 393224 | tf_op jit(solution)/shard_map/ppermute | solution.py:325
  2.2 12.9 %collective-permute-start.4 = (bf16[16,4096]{1,0:T(8,128)(2,1)S(1)}, bf16[16,4096]{1,0:T(8,128)(2,1)S(1)}, u32[]{:S(2)}, u32[]{:S(2)}) collective-permute-start(bf16[16,4096]{1,0:T(8,128)(2,1)S(1)} %get-tuple-element.30), channel_id=1, source_target_pairs={{0,8},{4,12},{8,0},{12,4},{1,9},{5,13},{9,1},{13,5},{2,10},{6,14},... | collective-permute-start | bytes 393224 | tf_op jit(solution)/shard_map/ppermute | solution.py:325
  4.7 11.3 %collective-permute-start.3 = (bf16[16,4096]{1,0:T(8,128)(2,1)S(1)}, bf16[16,4096]{1,0:T(8,128)(2,1)S(1)}, u32[]{:S(2)}, u32[]{:S(2)}) collective-permute-start(bf16[16,4096]{1,0:T(8,128)(2,1)S(1)} %get-tuple-element.31), channel_id=1, source_target_pairs={{0,12},{4,8},{8,4},{12,0},{1,13},{5,9},{9,5},{13,1},{2,14},{6,10},... | collective-permute-start | bytes 393224 | tf_op jit(solution)/shard_map/ppermute | solution.py:325
  5.6 16.1 %collective-permute-start.2 = (bf16[16,4096]{1,0:T(8,128)(2,1)}, bf16[16,4096]{1,0:T(8,128)(2,1)S(1)}, u32[]{:S(2)}, u32[]{:S(2)}) collective-permute-start(bf16[16,4096]{1,0:T(8,128)(2,1)} %get-tuple-element.32), channel_id=1, source_target_pairs={{0,4},{4,0},{8,12},{12,8},{1,5},{5,1},{9,13},{13,9},{2,6},{6,2},{1... | collective-permute-start | bytes 393224 | tf_op jit(solution)/shard_map/ppermute | solution.py:325
  6.7 17.1 %collective-permute-start.1 = (bf16[16,4096]{1,0:T(8,128)(2,1)}, bf16[16,4096]{1,0:T(8,128)(2,1)S(1)}, u32[]{:S(2)}, u32[]{:S(2)}) collective-permute-start(bf16[16,4096]{1,0:T(8,128)(2,1)} %get-tuple-element.33), channel_id=1, source_target_pairs={{0,8},{4,12},{8,0},{12,4},{1,9},{5,13},{9,1},{13,5},{2,10},{6,14},... | collective-permute-start | bytes 393224 | tf_op jit(solution)/shard_map/ppermute | solution.py:325
  14.9 12.0 %collective-permute-start = (bf16[16,4096]{1,0:T(8,128)(2,1)S(1)}, bf16[16,4096]{1,0:T(8,128)(2,1)S(1)}, u32[]{:S(2)}, u32[]{:S(2)}) collective-permute-start(bf16[16,4096]{1,0:T(8,128)(2,1)S(1)} %get-tuple-element.34), channel_id=1, source_target_pairs={{0,12},{4,8},{8,4},{12,0},{1,13},{5,9},{9,5},{13,1},{2,14},{6,10},... | collective-permute-start | bytes 393224 | tf_op jit(solution)/shard_map/ppermute | solution.py:325
  16.0 3.4 %copy-start = (bf16[2048,2048]{1,0:T(8,128)(2,1)S(1)}, bf16[2048,2048]{1,0:T(8,128)(2,1)}, u32[]{:S(2)}) copy-start(bf16[2048,2048]{1,0:T(8,128)(2,1)} %fusion.refs_9_.refs_10_) | copy-start | bytes 25165828
  19.4 7.5 %copy-start.1 = (bf16[2048,2048]{1,0:T(8,128)(2,1)S(1)}, bf16[2048,2048]{1,0:T(8,128)(2,1)}, u32[]{:S(2)}) copy-start(bf16[2048,2048]{1,0:T(8,128)(2,1)} %fusion.refs_9_.refs_10_) | copy-start | bytes 25165828
  21.6 12.6 %copy-start.8 = (s32[256]{0:T(256)S(1)}, s32[256]{0:T(256)}, u32[]{:S(2)}) copy-start(s32[256]{0:T(256)} %param.12) | copy-start | bytes 3076
  31.3 6.8 %collective-permute-start.6 = (bf16[256,256]{1,0:T(8,128)(2,1)S(1)}, bf16[256,256]{1,0:T(8,128)(2,1)S(1)}, u32[]{:S(2)}, u32[]{:S(2)}) collective-permute-start(bf16[256,256]{1,0:T(8,128)(2,1)S(1)} %get-tuple-element.16), channel_id=1, source_target_pairs={{0,4},{2,6},{4,8},{6,10},{8,12},{10,14},{12,0},{14,2},{1,5},{3,7},... | collective-permute-start | bytes 393224 | tf_op jit(solution)/shard_map/ppermute | solution.py:348
  33.2 7.3 %collective-permute-start.7 = (bf16[256,256]{1,0:T(8,128)(2,1)S(1)}, bf16[256,256]{1,0:T(8,128)(2,1)S(1)}, u32[]{:S(2)}, u32[]{:S(2)}) collective-permute-start(bf16[256,256]{1,0:T(8,128)(2,1)S(1)} %get-tuple-element.17), channel_id=1, source_target_pairs={{0,6},{2,4},{4,10},{6,8},{8,14},{10,12},{12,2},{14,0},{1,7},{3,5},... | collective-permute-start | bytes 393224 | tf_op jit(solution)/shard_map/ppermute | solution.py:348
  34.4 6.8 %collective-permute-start.8 = (bf16[256,256]{1,0:T(8,128)(2,1)S(1)}, bf16[256,256]{1,0:T(8,128)(2,1)S(1)}, u32[]{:S(2)}, u32[]{:S(2)}) collective-permute-start(bf16[256,256]{1,0:T(8,128)(2,1)S(1)} %get-tuple-element.18), channel_id=1, source_target_pairs={{0,8},{2,10},{4,12},{6,14},{8,0},{10,2},{12,4},{14,6},{1,9},{3,11}... | collective-permute-start | bytes 393224 | tf_op jit(solution)/shard_map/ppermute | solution.py:348
  36.0 16.5 %collective-permute-start.9 = (bf16[256,256]{1,0:T(8,128)(2,1)S(1)}, bf16[256,256]{1,0:T(8,128)(2,1)S(1)}, u32[]{:S(2)}, u32[]{:S(2)}) collective-permute-start(bf16[256,256]{1,0:T(8,128)(2,1)S(1)} %get-tuple-element.19), channel_id=1, source_target_pairs={{0,10},{2,8},{4,14},{6,12},{8,2},{10,0},{12,6},{14,4},{1,11},{3,9}... | collective-permute-start | bytes 393224 | tf_op jit(solution)/shard_map/ppermute | solution.py:348
  36.7 18.5 %collective-permute-start.10 = (bf16[256,256]{1,0:T(8,128)(2,1)S(1)}, bf16[256,256]{1,0:T(8,128)(2,1)S(1)}, u32[]{:S(2)}, u32[]{:S(2)}) collective-permute-start(bf16[256,256]{1,0:T(8,128)(2,1)S(1)} %get-tuple-element.20), channel_id=1, source_target_pairs={{0,12},{2,14},{4,0},{6,2},{8,4},{10,6},{12,8},{14,10},{1,13},{3,15... | collective-permute-start | bytes 393224 | tf_op jit(solution)/shard_map/ppermute | solution.py:348
  38.1 19.9 %collective-permute-start.11 = (bf16[256,256]{1,0:T(8,128)(2,1)S(1)}, bf16[256,256]{1,0:T(8,128)(2,1)S(1)}, u32[]{:S(2)}, u32[]{:S(2)}) collective-permute-start(bf16[256,256]{1,0:T(8,128)(2,1)S(1)} %get-tuple-element.21), channel_id=1, source_target_pairs={{0,14},{2,12},{4,2},{6,0},{8,6},{10,4},{12,10},{14,8},{1,15},{3,13... | collective-permute-start | bytes 393224 | tf_op jit(solution)/shard_map/ppermute | solution.py:348
  40.5 17.6 %collective-permute-start.12 = (bf16[256,256]{1,0:T(8,128)(2,1)S(1)}, bf16[256,256]{1,0:T(8,128)(2,1)S(1)}, u32[]{:S(2)}, u32[]{:S(2)}) collective-permute-start(bf16[256,256]{1,0:T(8,128)(2,1)S(1)} %get-tuple-element.22), channel_id=1, source_target_pairs={{0,2},{2,0},{4,6},{6,4},{8,10},{10,8},{12,14},{14,12},{1,3},{3,1},... | collective-permute-start | bytes 393224 | tf_op jit(solution)/shard_map/ppermute | solution.py:348
  59.3 4.4 %collective-permute-start.13 = (bf16[512,1024]{1,0:T(8,128)(2,1)S(1)}, bf16[512,1024]{1,0:T(8,128)(2,1)S(1)}, u32[]{:S(2)}, u32[]{:S(2)}) collective-permute-start(bf16[512,1024]{1,0:T(8,128)(2,1)S(1)} %get-tuple-element.23.own), channel_id=1, source_target_pairs={{0,1},{1,0},{2,3},{3,2},{4,5},{5,4},{6,7},{7,6},{8,9},{9,8},{10,11... | collective-permute-start | bytes 3145736 | tf_op jit(solution)/shard_map/ppermute | solution.py:350
